TPU v7x, 32 devices: a whole 2x2x4 slice. The times are simulated.
32 devices in a mesh: dp: 16 (over z, y, core), tensor: 2 (over x).
Axes of the slice: x: 2, y: 2, z: 4, core: 2. Of those that a mesh axis runs over, the one named last changes fastest.
Arguments:
- layer_in: bfloat16 [2, 16, 1024, 1024], P(None, 'dp'), may hold values from -6 to 6
- ln1_gain: float32 [1024], replicated, may hold values from 0.25 to 1.75
- ln1_bias: float32 [1024], replicated, may hold values from -1.2 to 1.2
- qkv_weight: bfloat16 [3, 1024, 1024], P(None, None, 'tensor'), may hold values from -0.1875 to 0.1875
- out_weight: bfloat16 [1024, 1024], P('tensor'), may hold values from -1.5 to 1.5
- ssm_coef: float32 [16, 1024], P(None, 'tensor'), may hold values from -1.5 to 1.5
- ssm_skip: float32 [1024], P('tensor'), may hold values from -2 to 2
- ln2_gain: float32 [1024], replicated, may hold values from 0.25 to 1.75
- ln2_bias: float32 [1024], replicated, may hold values from -1.2 to 1.2
- up_weight: bfloat16 [1024, 4096], P(None, 'tensor'), may hold values from -0.1875 to 0.1875
- down_weight: bfloat16 [4096, 1024], P('tensor'), may hold values from -0.09375 to 0.09375
- cotangent: bfloat16 [2, 16, 1024, 1024], P(None, 'dp'), may hold values from -6 to 6
Outputs:
- layer_out: bfloat16 [2, 16, 1024, 1024], P(None, 'dp')
- grad_in: float32 [2, 16, 1024, 1024], P(None, 'dp')
- grad_ln1_gain: float32 [1024], replicated
- grad_ln1_bias: float32 [1024], replicated
- grad_qkv: float32 [3, 1024, 1024], P(None, 'dp', 'tensor')
- grad_out: float32 [1024, 1024], P('tensor', 'dp')
- grad_coef: float32 [16, 1024], P(None, 'tensor')
- grad_skip: float32 [1024], P('tensor')
- grad_ln2_gain: float32 [1024], replicated
- grad_ln2_bias: float32 [1024], replicated
- grad_up: float32 [1024, 4096], P('dp', 'tensor')
- grad_down: float32 [4096, 1024], P('tensor', 'dp')
All inputs are finite; a program needn't handle non-finite values.
Results may differ from a plain program's by a relative error of at most 0.015.
Values may be sent and summed in bfloat16 or wider, within the bound.
No kernel may reach another device: no remote copies, remote signals or barrier semaphores. Data moves between devices by JAX's collectives and lax.ppermute only.
A program may use at most 320 MiB of HBM per device.

v0:
```python
import jax
import jax.numpy as jnp
from jax import lax
from jax.sharding import PartitionSpec as P

HD = 128
NS = 16
BLK = 512
CTX = 128
CH = 128


epsilon = 1e-05
highest = lax.Precision.HIGHEST


def layer_norm(values, gain_vec, shift_vec):
    center = values - jnp.mean(values, axis=-1, keepdims=True)
    spread = jnp.mean(center * center, axis=-1, keepdims=True)
    return center * lax.rsqrt(spread + epsilon) * gain_vec + shift_vec


def gelu_tanh(values):
    return jax.nn.gelu(values, approximate=True)


def decay_tables():
    index_n = jnp.arange(NS, dtype=jnp.float32)
    decay_rates = 4.0 / CH * jnp.exp2(-8.0 * index_n / (NS - 1))
    norm_factor = jnp.sqrt(-jnp.expm1(-2.0 * decay_rates))
    positions = jnp.arange(CH, dtype=jnp.float32)
    offsets = positions[:, None] - positions[None, :]
    powers = jnp.exp(-decay_rates[:, None, None] * jnp.maximum(offsets, 0.0)[None])
    within = jnp.where(offsets[None] >= 0.0, norm_factor[:, None, None] * powers, 0.0).astype(
        jnp.bfloat16
    )
    carry_in = jnp.exp(-decay_rates[None, :] * (positions[:, None] + 1.0))
    carry_out = within[:, CH - 1, :]
    whole_decay = jnp.exp(-decay_rates * CH)
    return (within, carry_in, carry_out, whole_decay)


def ssm_forward(channels, tables, coef_rows, skip_vec):
    within, carry_in, carry_out, whole_decay = tables
    width_here = channels.shape[1]
    pieces = channels.reshape(-1, CH, width_here)

    def block_step(carry_state, block_rows):
        inner = jnp.einsum("ntj,jc->ntc", within, block_rows, preferred_element_type=jnp.float32)
        inner = inner + carry_in.T[:, :, None] * carry_state[:, None, :]
        result_rows = jnp.sum(coef_rows[:, None, :] * inner, axis=0) + skip_vec * block_rows.astype(
            jnp.float32
        )
        next_state = whole_decay[:, None] * carry_state + jnp.einsum(
            "nj,jc->nc", carry_out, block_rows, preferred_element_type=jnp.float32
        )
        return (next_state, (result_rows, carry_state))

    starting = jnp.zeros((NS, width_here), jnp.float32)
    _, (results, starts) = lax.scan(block_step, starting, pieces)
    return (results.reshape(-1, width_here), starts)


def ssm_backward(channels, grad_rows, starts, tables, coef_rows, skip_vec):
    within, carry_in, carry_out, whole_decay = tables
    width_here = channels.shape[1]
    carry_wide = carry_out.astype(jnp.float32)

    def block_step(carry, item):
        grad_state, grad_coef_sum, grad_skip_sum = carry
        block_rows, grad_block, start_state = item
        grad_wide = grad_block.astype(jnp.float32)
        rows_wide = block_rows.astype(jnp.float32)
        backed = jnp.einsum("ntj,tc->njc", within, grad_block, preferred_element_type=jnp.float32)
        grad_input = skip_vec * grad_wide + jnp.sum(coef_rows[:, None, :] * backed, axis=0)
        grad_input = grad_input + jnp.einsum("nj,nc->jc", carry_wide, grad_state, precision=highest)
        reach = jnp.einsum("tn,tc->nc", carry_in, grad_wide, precision=highest)
        grad_coef_sum = (
            grad_coef_sum + jnp.sum(rows_wide[None] * backed, axis=1) + start_state * reach
        )
        grad_skip_sum = grad_skip_sum + jnp.sum(grad_wide * rows_wide, axis=0)
        grad_state = whole_decay[:, None] * grad_state + coef_rows * reach
        return ((grad_state, grad_coef_sum, grad_skip_sum), grad_input)

    starting = (
        jnp.zeros((NS, width_here), jnp.float32),
        jnp.zeros((NS, width_here), jnp.float32),
        jnp.zeros((width_here,), jnp.float32),
    )
    items = (channels.reshape(-1, CH, width_here), grad_rows.reshape(-1, CH, width_here), starts)
    (_, grad_coef_sum, grad_skip_sum), grad_inputs = lax.scan(
        block_step, starting, items, reverse=True
    )
    return (grad_inputs.reshape(-1, width_here), grad_coef_sum, grad_skip_sum)


def visible(first_block):
    row_ids = lax.broadcasted_iota(jnp.int32, (BLK, CTX + BLK), 0)
    col_ids = lax.broadcasted_iota(jnp.int32, (BLK, CTX + BLK), 1)
    return jnp.where(col_ids < CTX, jnp.logical_not(first_block), col_ids - CTX <= row_ids)


def block_scores(query_rows, key_rows, first_block):
    scores = jnp.einsum(
        "thd,shd->hts", query_rows, key_rows, preferred_element_type=jnp.float32
    ) * HD ** (-0.5)
    return jnp.where(visible(first_block)[None], scores, -1e30)


def attend_forward(item):
    first_block, query_rows, key_rows, value_rows = item
    scores = block_scores(query_rows, key_rows, first_block)
    row_top = jnp.max(scores, axis=-1, keepdims=True)
    exps_rows = jnp.exp(scores - row_top)
    row_total = jnp.sum(exps_rows, axis=-1, keepdims=True)
    probs_low = (exps_rows / row_total).astype(jnp.bfloat16)
    heads_out = jnp.einsum(
        "hts,shd->thd", probs_low, value_rows, preferred_element_type=jnp.float32
    )
    return (heads_out.astype(jnp.bfloat16), row_top + jnp.log(row_total))


def attend_backward(item):
    first_block, query_rows, key_rows, value_rows, grad_heads, log_total = item
    scores = block_scores(query_rows, key_rows, first_block)
    probs_wide = jnp.exp(scores - log_total)
    grad_probs = jnp.einsum(
        "thd,shd->hts", grad_heads, value_rows, preferred_element_type=jnp.float32
    )
    inner = jnp.sum(probs_wide * grad_probs, axis=-1, keepdims=True)
    grad_scores = (probs_wide * (grad_probs - inner)).astype(jnp.bfloat16)
    scale_value = HD ** (-0.5)
    grad_query = (
        jnp.einsum("hts,shd->thd", grad_scores, key_rows, preferred_element_type=jnp.float32)
        * scale_value
    ).astype(jnp.bfloat16)
    grad_keys = (
        jnp.einsum("hts,thd->shd", grad_scores, query_rows, preferred_element_type=jnp.float32)
        * scale_value
    ).astype(jnp.bfloat16)
    grad_values = jnp.einsum(
        "hts,thd->shd",
        probs_wide.astype(jnp.bfloat16),
        grad_heads,
        preferred_element_type=jnp.float32,
    ).astype(jnp.bfloat16)
    return (grad_query, grad_keys, grad_values)


def add_pairs(totals, terms):
    if totals is None:
        return terms
    return tuple((total_part + term_part for total_part, term_part in zip(totals, terms)))


def shards(
    layer_in,
    ln1_gain,
    ln1_bias,
    qkv_weight,
    out_weight,
    ssm_coef,
    ssm_skip,
    ln2_gain,
    ln2_bias,
    up_weight,
    down_weight,
    cotangent,
):
    micro_count = layer_in.shape[0]
    length = layer_in.shape[2]
    group_width = qkv_weight.shape[2]
    heads_here = group_width // HD
    blocks = length // BLK
    tensor_rank = lax.axis_index("tensor")
    channel_start = tensor_rank * group_width
    tables = decay_tables()
    firsts = jnp.arange(blocks) == 0
    small_totals = None
    large_totals = None
    outputs = []
    grad_inputs = []
    for micro_index in range(micro_count):
        inputs = layer_in[micro_index, 0].astype(jnp.float32)
        first_norm, first_pull = jax.vjp(layer_norm, inputs, ln1_gain, ln1_bias)
        rounded = first_norm.astype(jnp.bfloat16)
        projected = jnp.einsum(
            "td,sde->ste", rounded, qkv_weight, preferred_element_type=jnp.float32
        ).astype(jnp.bfloat16)
        channels = lax.dynamic_slice_in_dim(rounded, channel_start, group_width, 1)
        ssm_out, starts = ssm_forward(channels, tables, ssm_coef, ssm_skip)
        tail_rows = ssm_out.reshape(blocks, BLK, group_width)[:-1, BLK - CTX :, :].astype(
            jnp.bfloat16
        )
        context = lax.all_gather(tail_rows, "tensor", axis=2, tiled=True)
        context_kv = jnp.einsum(
            "bcd,sde->sbce", context, qkv_weight[1:], preferred_element_type=jnp.float32
        ).astype(jnp.bfloat16)
        shaped = projected.reshape(3, blocks, BLK, heads_here, HD)
        padding = jnp.zeros((2, 1, CTX, heads_here, HD), jnp.bfloat16)
        padded = jnp.concatenate(
            [padding, context_kv.reshape(2, blocks - 1, CTX, heads_here, HD)], axis=1
        )
        joined = jnp.concatenate([padded, shaped[1:]], axis=2)
        heads_out, log_total = lax.map(attend_forward, (firsts, shaped[0], joined[0], joined[1]))
        heads_flat = heads_out.reshape(length, group_width)
        attn_part = jnp.dot(heads_flat, out_weight, preferred_element_type=jnp.float32)
        attn_out = lax.psum(attn_part.astype(jnp.bfloat16), "tensor").astype(jnp.float32)
        middle = inputs + attn_out
        second_norm, second_pull = jax.vjp(layer_norm, middle, ln2_gain, ln2_bias)
        rounded_second = second_norm.astype(jnp.bfloat16)
        pre_act = jnp.dot(rounded_second, up_weight, preferred_element_type=jnp.float32)
        hidden_wide, gelu_pull = jax.vjp(gelu_tanh, pre_act)
        hidden = hidden_wide.astype(jnp.bfloat16)
        mixed_part = jnp.dot(hidden, down_weight, preferred_element_type=jnp.float32)
        mixed = lax.psum(mixed_part.astype(jnp.bfloat16), "tensor").astype(jnp.float32)
        outputs.append((middle + mixed).astype(jnp.bfloat16))
        grad_result = cotangent[micro_index, 0]
        grad_down_step = jnp.einsum(
            "tf,td->fd", hidden, grad_result, preferred_element_type=jnp.float32
        )
        grad_hidden = jnp.einsum(
            "td,fd->tf", grad_result, down_weight, preferred_element_type=jnp.float32
        )
        (grad_pre,) = gelu_pull(grad_hidden)
        grad_pre_low = grad_pre.astype(jnp.bfloat16)
        grad_up_step = jnp.einsum(
            "td,tf->df", rounded_second, grad_pre_low, preferred_element_type=jnp.float32
        )
        second_part = jnp.einsum(
            "tf,df->td", grad_pre_low, up_weight, preferred_element_type=jnp.float32
        )
        grad_second = lax.psum(second_part.astype(jnp.bfloat16), "tensor").astype(jnp.float32)
        grad_middle_norm, grad_gain_two, grad_bias_two = second_pull(grad_second)
        grad_middle = grad_result.astype(jnp.float32) + grad_middle_norm
        grad_attn = grad_middle.astype(jnp.bfloat16)
        grad_out_step = jnp.einsum(
            "te,td->ed", heads_flat, grad_attn, preferred_element_type=jnp.float32
        )
        grad_heads = jnp.einsum(
            "td,ed->te", grad_attn, out_weight, preferred_element_type=jnp.float32
        ).astype(jnp.bfloat16)
        grad_heads = grad_heads.reshape(blocks, BLK, heads_here, HD)
        grad_query, grad_keys, grad_values = lax.map(
            attend_backward, (firsts, shaped[0], joined[0], joined[1], grad_heads, log_total)
        )
        grad_self = jnp.stack(
            [
                grad_query.reshape(length, group_width),
                grad_keys[:, CTX:].reshape(length, group_width),
                grad_values[:, CTX:].reshape(length, group_width),
            ]
        )
        grad_context_kv = jnp.stack([grad_keys[1:, :CTX], grad_values[1:, :CTX]]).reshape(
            2, blocks - 1, CTX, group_width
        )
        grad_qkv_step = jnp.einsum(
            "td,ste->sde", rounded, grad_self, preferred_element_type=jnp.float32
        )
        grad_qkv_step = grad_qkv_step.at[1:].add(
            jnp.einsum(
                "bcd,sbce->sde", context, grad_context_kv, preferred_element_type=jnp.float32
            )
        )
        grad_input_part = jnp.einsum(
            "ste,sde->td", grad_self, qkv_weight, preferred_element_type=jnp.float32
        )
        context_part = jnp.einsum(
            "sbce,sde->bcd", grad_context_kv, qkv_weight[1:], preferred_element_type=jnp.float32
        )
        grad_context = lax.psum_scatter(
            context_part.astype(jnp.bfloat16), "tensor", scatter_dimension=2, tiled=True
        )
        zero_head = jnp.zeros((blocks - 1, BLK - CTX, group_width), jnp.bfloat16)
        grad_early = jnp.concatenate([zero_head, grad_context], axis=1).reshape(
            (blocks - 1) * BLK, group_width
        )
        grad_ssm = jnp.concatenate(
            [grad_early, jnp.zeros((BLK, group_width), jnp.bfloat16)], axis=0
        )
        grad_channels, grad_coef_step, grad_skip_step = ssm_backward(
            channels, grad_ssm, starts, tables, ssm_coef, ssm_skip
        )
        current = lax.dynamic_slice_in_dim(grad_input_part, channel_start, group_width, 1)
        grad_input_part = lax.dynamic_update_slice_in_dim(
            grad_input_part, current + grad_channels, channel_start, 1
        )
        grad_normed = lax.psum(grad_input_part.astype(jnp.bfloat16), "tensor").astype(jnp.float32)
        grad_inputs_norm, grad_gain_one, grad_bias_one = first_pull(grad_normed)
        grad_inputs.append(grad_middle + grad_inputs_norm)
        small_totals = add_pairs(
            small_totals,
            (
                grad_gain_one,
                grad_bias_one,
                grad_coef_step,
                grad_skip_step,
                grad_gain_two,
                grad_bias_two,
            ),
        )
        large_step = (grad_qkv_step, grad_out_step, grad_up_step, grad_down_step)
        large_totals = add_pairs(large_totals, large_step)
    large_totals = (
        lax.psum_scatter(large_totals[0], "dp", scatter_dimension=1, tiled=True),
        lax.psum_scatter(large_totals[1], "dp", scatter_dimension=1, tiled=True),
        lax.psum_scatter(large_totals[2], "dp", scatter_dimension=0, tiled=True),
        lax.psum_scatter(large_totals[3], "dp", scatter_dimension=1, tiled=True),
    )
    small_totals = lax.psum(
        (
            small_totals[0],
            small_totals[1],
            small_totals[2],
            small_totals[3],
            small_totals[4],
            small_totals[5],
        ),
        "dp",
    )
    return (
        jnp.stack(outputs)[:, None],
        jnp.stack(grad_inputs)[:, None],
        small_totals[0],
        small_totals[1],
        large_totals[0],
        large_totals[1],
        small_totals[2],
        small_totals[3],
        small_totals[4],
        small_totals[5],
        large_totals[2],
        large_totals[3],
    )


def solution(mesh):
    in_specs = (
        P(None, "dp", None, None),
        P(),
        P(),
        P(None, None, "tensor"),
        P("tensor", None),
        P(None, "tensor"),
        P("tensor"),
        P(),
        P(),
        P(None, "tensor"),
        P("tensor", None),
        P(None, "dp", None, None),
    )
    out_specs = (
        P(None, "dp", None, None),
        P(None, "dp", None, None),
        P(),
        P(),
        P(None, "dp", "tensor"),
        P("tensor", "dp"),
        P(None, "tensor"),
        P("tensor"),
        P(),
        P(),
        P("dp", "tensor"),
        P("tensor", "dp"),
    )
    return jax.shard_map(shards, mesh=mesh, in_specs=in_specs, out_specs=out_specs, check_vma=False)
```

profile of v0, /device:TPU:0, one launch (start us, length us, event | category | flops | bytes accessed | tf_op | source)
XLA Modules:
  0.0 1393.8 jit_solution(13273645024775175600)
XLA Ops:
  12.5 3.7 convert_bitcast_fusion.3
  22.6 33.0 %while.146 = (s32[]{:T(128)}, f32[16,512]{1,0:T(8,128)S(1)}, bf16[8,128,512]{1,2,0:T(8,128)(2,1)}, f32[8,16,512]{2,1,0:T(8,128)S(1)}, bf16[8,128,512]{2,1,0:T(8,...) while((s32[]{:T(128)}, f32[16,512]{1,0:T(8,128)S(1)}, ...), condition=%wide.region_4.5_spmd.clone.clone.clone, body=%wide.region_2.4_spmd.clone.clone.clone.sunk | while | flops 275933248 | bytes 2039263 | solution.py:60
  58.2 7.3 all_gather.6
  67.7 4.0 slice.150
  79.0 23.8 %while.142 = (s32[]{:T(128)}, bf16[2,512,4,128]{3,2,1,0:T(4,128)(2,1)}, f32[2,4,512,1]{2,1,3,0:T(4,128)S(1)}, bf16[2,640,4,128]{3,1,2,0:T(8,128)(2,1)}, pred[2]{...) while((s32[]{:T(128)}, ...), condition=%wide.region_8.9_spmd, body=%wide.region_5.8_spmd.sunk | while | flops 687734016 | bytes 26812288 | solution.py:205
  102.9 4.6 convolution_convert_fusion.5
  107.6 64.5 %all-reduce.16.cloned.1.call-done = bf16[1024,1024]{1,0:T(8,128)(2,1)} async-done(((bf16[1024,1024]{1,0:T(8,128)(2,1)}), bf16[1024,1024]{1,0:T(8,128)(2,1)}) %all-reduce.16.cloned.1.call-update) | async-done | bytes 2097168 | tf_op jit(solution)/shard_map/psum | solution.py:208
  172.1 3.7 fusion.257
  177.7 3.7 convert_bitcast_fusion.2
  185.1 33.1 %while.147 = (s32[]{:T(128)}, f32[16,512]{1,0:T(8,128)S(1)}, bf16[8,128,512]{1,2,0:T(8,128)(2,1)}, f32[8,16,512]{2,1,0:T(8,128)S(1)}, bf16[8,128,512]{2,1,0:T(8,...) while((s32[]{:T(128)}, f32[16,512]{1,0:T(8,128)S(1)}, ...), condition=%wide.region_17.18_spmd.clone.clone.clone, body=%wide.region_15.17_spmd.clone.clone.clone.sunk | while | flops 275933248 | bytes 2039263 | solution.py:60
  220.8 6.1 all_gather.7
  229.2 4.0 slice.157
  240.5 22.5 %while.143 = (s32[]{:T(128)}, bf16[2,512,4,128]{3,2,1,0:T(4,128)(2,1)}, f32[2,4,512,1]{2,1,3,0:T(4,128)S(1)}, bf16[2,640,4,128]{3,1,2,0:T(8,128)(2,1)}, pred[2]{...) while((s32[]{:T(128)}, ...), condition=%wide.region_21.22_spmd, body=%wide.region_18.21_spmd.sunk | while | flops 687734016 | bytes 26812288 | solution.py:205
  263.1 3.8 convolution_convert_fusion.3
  267.0 63.0 %all-reduce.18.cloned.1.call-done = bf16[1024,1024]{1,0:T(8,128)(2,1)} async-done(((bf16[1024,1024]{1,0:T(8,128)(2,1)}), bf16[1024,1024]{1,0:T(8,128)(2,1)}) %all-reduce.18.cloned.1.call-update) | async-done | bytes 2097168 | tf_op jit(solution)/shard_map/psum | solution.py:208
  330.0 5.0 multiply_reduce_fusion.7
  337.4 7.3 fusion.353
  344.7 11.1 fusion.208
  355.8 7.2 fusion.354
  363.0 11.1 fusion.215
  374.2 6.0 convolution_convert_fusion.1
  380.2 5.7 convolution_convert_fusion
  386.0 11.2 convolution_convert_fusion.4
  397.2 9.9 convolution_convert_fusion.2
  407.1 87.2 %all-reduce.24.cloned.1.call-done = (bf16[1024,1024]{1,0:T(8,128)(2,1)}, bf16[1024,1024]{1,0:T(8,128)(2,1)}) async-done(((bf16[1024,1024]{1,0:T(8,128)(2,1)}, bf16[1024,1024]{1,0:T(8,128)(2,1)}), (bf16[1024,1024]{1,0:T(8,128)(2,1)}, bf16[1024,1024]{1,0:T(8,128)(2,1)})) %all-reduce.24.cloned.1.call-update) | async-done | bytes 4194320 | tf_op jit(solution)/shard_map/psum | solution.py:233
  494.3 7.5 fusion.248
  502.7 4.1 fusion.355
  520.1 44.6 %while.145 = (s32[]{:T(128)}, bf16[2,512,4,128]{3,2,1,0:T(4,128)(2,1)}, bf16[2,640,4,128]{1,3,2,0:T(8,128)(2,1)}, bf16[2,640,4,128]{1,3,2,0:T(8,128)(2,1)}, bf16...) while((s32[]{:T(128)}, ...), condition=%wide.region_46.47_spmd, body=%wide.region_44.46_spmd.sunk | while | flops 1699544320 | bytes 97453688 | solution.py:244
  534.3 3.2 fusion.485
  537.6 5.0 fusion.486
  556.5 3.2 fusion.485
  559.7 5.0 fusion.486
  578.5 44.2 %while.144 = (s32[]{:T(128)}, bf16[2,512,4,128]{3,2,1,0:T(4,128)(2,1)}, bf16[2,640,4,128]{1,3,2,0:T(8,128)(2,1)}, bf16[2,640,4,128]{1,3,2,0:T(8,128)(2,1)}, bf16...) while((s32[]{:T(128)}, ...), condition=%wide.region_31.32_spmd, body=%wide.region_29.31_spmd.sunk | while | flops 1699544320 | bytes 90637848 | solution.py:244
  592.5 3.2 fusion.473
  595.7 5.0 fusion.474
  614.5 3.2 fusion.473
  617.7 5.0 fusion.474
  639.0 7.5 fusion.282
  646.5 5.0 convolution_bitcast_fusion.5
  663.6 5.4 fusion.279
  673.9 6.6 copy.402
  683.8 4.9 fusion.255
  688.8 5.1 fusion.253
  693.8 7.1 add.514
  700.9 9.4 copy.166
  713.5 8.3 convolution_bitcast_fusion.4
  724.6 46.7 %while.148 = (s32[]{:T(128)}, f32[16,512]{1,0:T(8,128)S(1)}, f32[16,512]{1,0:T(8,128)S(1)}, f32[512]{0:T(512)S(1)}, f32[8,128,512]{2,1,0:T(8,128)}, /*index=5*/b...) while((s32[]{:T(128)}, f32[16,512]{1,0:T(8,128)S(1)}, ...), condition=%wide.region_37.38_spmd.clone.clone.clone, body=%wide.region_33.37_spmd.clone.clone.clone.sunk | while | flops 299436608 | bytes 11965844 | solution.py:91
  774.0 46.4 %while.149 = (s32[]{:T(128)}, f32[16,512]{1,0:T(8,128)S(1)}, f32[16,512]{1,0:T(8,128)S(1)}, f32[512]{0:T(512)S(1)}, f32[8,128,512]{2,1,0:T(8,128)}, /*index=5*/b...) while((s32[]{:T(128)}, f32[16,512]{1,0:T(8,128)S(1)}, ...), condition=%wide.region_52.53_spmd.clone.clone.clone, body=%wide.region_48.52_spmd.clone.clone.clone.sunk | while | flops 299436608 | bytes 11965844 | solution.py:91
  820.5 4.3 constant_dynamic-update-slice_fusion.11
  824.8 4.0 convert_element_type.387
  839.1 8.2 fusion.352
  847.3 7.1 convolution_add_fusion.3
  854.6 9.4 fusion.273
  864.0 9.8 convolution_add_fusion.2
  875.7 23.5 %all-reduce.20.cloned.1.call-done = f32[3,1024,512]{2,0,1:T(4,128)} async-done(((f32[3,1024,512]{2,0,1:T(4,128)}), f32[3,1024,512]{2,0,1:T(4,128)}) %all-reduce.20.cloned.1.call-update) | async-done | bytes 6291472
  901.2 200.6 %all-reduce.22.cloned.1.call-done = (bf16[1024,1024]{1,0:T(8,128)(2,1)}, bf16[1024,1024]{1,0:T(8,128)(2,1)}, bf16[1024,1024]{1,0:T(8,128)(2,1)}, bf16[1024,1024]{1,0:T(8,128)(2,1)}) async-done(((bf16[1024,1024]{1,0:T(8,128)(2,1)}, bf16[1024,1024]{1,0:T(8,128)(2,1)}, bf16[1024,1024]{1,0:T(8,128)(2,1)}, bf16[1024,1024]{1,0:T(8,128)(2,1)}), (bf16[1024,1024]{1,0:T(8,128)(2,1)}, bf16[1024,1024]{1,0:T(8,128)(2,1)}, ...) | async-done | bytes 8388624 | tf_op jit(solution)/shard_map/psum | solution.py:216
  1102.0 5.1 fusion.245
  1107.9 8.9 fusion.249
  1116.7 62.0 %all-reduce.7 = (f32[1024]{0:T(1024)}, f32[1024]{0:T(1024)}, f32[16,512]{1,0:T(8,128)}, f32[512]{0:T(512)}, f32[1024]{0:T(1024)}, /*index=5*/f32[1024]{0:T(1024)}) all-reduce(f32[1024]{0:T(1024)S(1)} %add.508, f32[1024]{0:T(1024)S(1)} %add.509, f32[16,512]{1,0:T(8,128)S(1)} %add.516, ...), channel_id=1, replica_groups=mesh['dp'=16,'tensor'=2] {'dp'}, use_global_device_ids=true, to_apply=%region_58.59 | all-reduce | flops 12800 | bytes 102400 | tf_op jit(solution)/shard_map/psum | solution.py:310
  1178.7 5.5 maximum_bitcast_fusion.1
  1186.2 8.4 add_bitcast_fusion.1
  1194.7 4.3 maximum_bitcast_fusion
  1198.9 78.3 %reduce-scatter.12.cloned.1.call-done = f32[64,2048]{1,0:T(8,128)} async-done(((f32[1024,2048]{1,0:T(8,128)}), f32[64,2048]{1,0:T(8,128)}) %reduce-scatter.12.cloned.1.call-update) | async-done | bytes 524304 | tf_op jit(solution)/shard_map/reduce_scatter | solution.py:307
  1277.2 109.5 %reduce-scatter.14.cloned.1.call-done = f32[2048,64]{0,1:T(8,128)} async-done(((f32[2048,1024]{0,1:T(8,128)}), f32[2048,64]{0,1:T(8,128)}) %reduce-scatter.14.cloned.1.call-update) | async-done | bytes 524304 | tf_op jit(solution)/shard_map/reduce_scatter | solution.py:308
  (843 shorter events, 386.2 us)
Async XLA Ops:
  7.2 95.7 %copy-start = (bf16[512,1024]{1,0:T(8,128)(2,1)S(1)}, bf16[512,1024]{1,0:T(8,128)(2,1)}, u32[]{:S(2)}) copy-start(bf16[512,1024]{1,0:T(8,128)(2,1)} %param.36) | copy-start | bytes 3145732
  7.2 164.8 %all-reduce.16.cloned.1.call-start = ((), (), s32[]{:S(2)}) async-start(), calls=%async_computation.5 | async-start | bytes 4194304 | tf_op jit(solution)/shard_map/psum | solution.py:208
  7.3 13.1 copy-start.46
  7.4 13.2 copy-start.66
  16.3 6.3 copy-start.41
  16.3 6.3 copy-start.80
  56.3 15.4 %copy-start.49 = (bf16[8,128,512]{2,1,0:T(8,128)(2,1)}, bf16[8,128,512]{2,1,0:T(8,128)(2,1)S(1)}, u32[]{:S(2)}) copy-start(bf16[8,128,512]{2,1,0:T(8,128)(2,1)S(1)} %get-tuple-element.3115) | copy-start | bytes 3145732
  56.3 15.4 %copy-start.127 = (pred[128,128]{1,0:T(8,128)(4,1)}, pred[128,128]{1,0:T(8,128)(4,1)S(1)}, u32[]{:S(2)}) copy-start(pred[128,128]{1,0:T(8,128)(4,1)S(1)} %get-tuple-element.3163) | copy-start | bytes 49156
  65.4 6.2 copy-start.74
  107.5 222.5 %all-reduce.18.cloned.1.call-start = ((), (), s32[]{:S(2)}) async-start(), calls=%async_computation.6 | async-start | bytes 4194304 | tf_op jit(solution)/shard_map/psum | solution.py:208
  107.5 69.4 %copy-start.95 = (f32[1024]{0:T(1024)}, f32[1024]{0:T(1024)S(1)}, u32[]{:S(2)}) copy-start(f32[1024]{0:T(1024)S(1)} %broadcast_multiply_fusion.1) | copy-start | bytes 12292
  218.8 14.3 %copy-start.42 = (f32[16,512]{1,0:T(8,128)}, f32[16,512]{1,0:T(8,128)S(1)}, u32[]{:S(2)}) copy-start(f32[16,512]{1,0:T(8,128)S(1)} %get-tuple-element.3112) | copy-start | bytes 98308
  218.8 14.3 %copy-start.50 = (bf16[8,128,512]{2,1,0:T(8,128)(2,1)}, bf16[8,128,512]{2,1,0:T(8,128)(2,1)S(1)}, u32[]{:S(2)}) copy-start(bf16[8,128,512]{2,1,0:T(8,128)(2,1)S(1)} %get-tuple-element.3116) | copy-start | bytes 3145732
  218.9 14.3 %copy-start.81 = (f32[512]{0:T(512)}, f32[512]{0:T(512)S(1)}, u32[]{:S(2)}) copy-start(f32[512]{0:T(512)S(1)} %get-tuple-element.3143) | copy-start | bytes 6148
  218.9 14.3 %copy-start.86 = (f32[16]{0:T(128)}, f32[16]{0:T(128)S(1)}, u32[]{:S(2)}) copy-start(f32[16]{0:T(128)S(1)} %get-tuple-element.3147) | copy-start | bytes 196
  218.9 14.3 %copy-start.89 = (f32[128]{0:T(128)}, f32[128]{0:T(128)S(1)}, u32[]{:S(2)}) copy-start(f32[128]{0:T(128)S(1)} %get-tuple-element.3154) | copy-start | bytes 1540
  218.9 14.3 %copy-start.109 = (f32[16]{0:T(128)}, f32[16]{0:T(128)S(1)}, u32[]{:S(2)}) copy-start(f32[16]{0:T(128)S(1)} %get-tuple-element.3160) | copy-start | bytes 196
  226.9 6.3 copy-start.76
  266.9 227.4 %all-reduce.24.cloned.1.call-start = ((), (), s32[]{:S(2)}) async-start(), calls=%async_computation.14 | async-start | bytes 8388608 | tf_op jit(solution)/shard_map/psum | solution.py:233
  266.9 234.9 %copy-start.101 = (f32[1024]{0:T(1024)}, f32[1024]{0:T(1024)S(1)}, u32[]{:S(2)}) copy-start(f32[1024]{0:T(1024)S(1)} %broadcast_multiply_fusion.2) | copy-start | bytes 12292
  330.0 6.5 copy-start.132
  335.0 166.9 %copy-start.115 = (f32[1024]{0:T(1024)}, f32[1024]{0:T(1024)S(1)}, u32[]{:S(2)}) copy-start(f32[1024]{0:T(1024)S(1)} %fusion.344) | copy-start | bytes 12292
  335.3 166.6 %copy-start.103 = (f32[1024]{0:T(1024)}, f32[1024]{0:T(1024)S(1)}, u32[]{:S(2)}) copy-start(f32[1024]{0:T(1024)S(1)} %broadcast_multiply_fusion) | copy-start | bytes 12292
  337.4 164.6 %copy-start.117 = (f32[1024]{0:T(1024)}, f32[1024]{0:T(1024)S(1)}, u32[]{:S(2)}) copy-start(f32[1024]{0:T(1024)S(1)} %fusion.346) | copy-start | bytes 12292
  337.4 7.3 copy-start.34
  337.4 7.3 copy-start.133
  355.8 18.4 %copy-start.144 = (bf16[1024,2048]{1,0:T(8,128)(2,1)}, bf16[1024,2048]{1,0:T(8,128)(2,1)S(1)}, u32[]{:S(2)}) copy-start(bf16[1024,2048]{1,0:T(8,128)(2,1)S(1)} %fusion.208) | copy-start | bytes 12582916
  374.1 6.1 copy-start.145
  385.9 336.0 %reduce-scatter.6.cloned.1.call-start = ((), (), s32[]{:S(2)}) async-start(), calls=%async_computation.7 | async-start | bytes 393216 | tf_op jit(solution)/shard_map/reduce_scatter | solution.py:271
  386.0 11.2 copy-start.134
  494.3 7.6 copy-start.9
  494.3 7.6 copy-start.20
  494.3 7.6 copy-start.23
  494.3 7.7 copy-start.51
  494.3 8.3 copy-start.52
  564.7 7.7 copy-start.70
  632.8 6.2 copy-start.55
  639.0 7.5 copy-start.88
  639.0 7.5 copy-start.137
  651.5 5.8 copy-start.58
  657.3 6.3 copy-start.57
  673.8 9.9 copy-start.75
  688.7 82.7 %reduce-scatter.8.cloned.1.call-start = ((), (), s32[]{:S(2)}) async-start(), calls=%async_computation.8 | async-start | bytes 393216 | tf_op jit(solution)/shard_map/reduce_scatter | solution.py:271
  713.4 185.8 %all-reduce.20.cloned.1.call-start = ((), (), s32[]{:S(2)}) async-start(), calls=%async_computation.12 | async-start | bytes 16777216
  721.9 380.0 %all-reduce.22.cloned.1.call-start = ((), (), s32[]{:S(2)}) async-start(), calls=%async_computation.13 | async-start | bytes 16777216 | tf_op jit(solution)/shard_map/psum | solution.py:216
  832.0 367.0 %reduce-scatter.10.cloned.1.call-start = ((), (), s32[]{:S(2)}) async-start(), calls=%async_computation.9 | async-start | bytes 2228224 | tf_op jit(solution)/shard_map/reduce_scatter | solution.py:306
  839.0 8.3 copy-start.104
  839.0 8.3 copy-start.118
  839.0 438.3 %reduce-scatter.12.cloned.1.call-start = ((), (), s32[]{:S(2)}) async-start(), calls=%async_computation.10 | async-start | bytes 8912896 | tf_op jit(solution)/shard_map/reduce_scatter | solution.py:307
  839.1 8.2 copy-start.10
  839.1 8.2 copy-start.24
  839.1 8.2 copy-start.146
  854.5 532.2 %reduce-scatter.14.cloned.1.call-start = ((), (), s32[]{:S(2)}) async-start(), calls=%async_computation.11 | async-start | bytes 8912896 | tf_op jit(solution)/shard_map/reduce_scatter | solution.py:308
  854.6 9.4 copy-start.36
  873.8 228.1 %copy-start.94 = (f32[1024]{0:T(1024)S(1)}, f32[1024]{0:T(1024)}, u32[]{:S(2)}) copy-start(f32[1024]{0:T(1024)} %copy-done.93) | copy-start | bytes 12292
  873.8 228.1 %copy-start.96 = (f32[1024]{0:T(1024)S(1)}, f32[1024]{0:T(1024)}, u32[]{:S(2)}) copy-start(f32[1024]{0:T(1024)} %copy-done.95) | copy-start | bytes 12292
  873.8 228.1 %copy-start.98 = (f32[1024]{0:T(1024)S(1)}, f32[1024]{0:T(1024)}, u32[]{:S(2)}) copy-start(f32[1024]{0:T(1024)} %param.33) | copy-start | bytes 12292
  1101.9 5.9 copy-start.32
  1101.9 5.9 copy-start.106
  1102.0 5.9 copy-start.108
  1178.7 7.5 copy-start.29
  1178.7 7.5 copy-start.120
  1178.7 7.5 copy-start.122
  1194.6 192.1 %copy-start.1 = (bf16[512,1024]{1,0:T(8,128)(2,1)S(1)}, bf16[512,1024]{1,0:T(8,128)(2,1)}, u32[]{:S(2)}) copy-start(bf16[512,1024]{1,0:T(8,128)(2,1)} %param.36) | copy-start | bytes 3145732
  (110 other events, 354.7 us)
Sparse Core Ops, SparseCore 0:
  107.6 64.4 all-reduce.15
  267.0 62.9 all-reduce.17
  386.0 108.2 all-reduce.23
  688.8 11.6 reduce-scatter.5
  713.5 11.6 reduce-scatter.7
  729.3 169.8 all-reduce.19
  902.4 199.4 all-reduce.21
  1106.2 62.0 reduce-scatter.9
  1173.5 103.6 reduce-scatter.11
  1282.3 104.4 reduce-scatter.13
where the time goes:
time: 1400 us; the launch traced here: 1390 us
  waiting for transfers between devices  627 us (45%)
  matrix products  339 us (24%)
  local copies, waits for them, and re-layouts  172 us (12%)
  other arithmetic  155 us (11%)
  blocking collectives  75.4 us (5%)
  between operations  16.9 us (1%)
    psum x1, waiting for transfers between devices, shards(): lax.psum(mixed_part.astype(jnp.bfloat16), 'tensor').astype(jnp.float32)  201 us
    psum x2, waiting for transfers between devices, shards(): lax.psum(attn_part.astype(jnp.bfloat16), 'tensor').astype(jnp.float32)  128 us
    reduce_scatter x1, waiting for transfers between devices, shards(): lax.psum_scatter(large_totals[3], 'dp', scatter_dimension=1, tiled=True)  110 us
    psum x1, waiting for transfers between devices, shards(): lax.psum(second_part.astype(jnp.bfloat16), 'tensor').astype(jnp.float32)  87.2 us
    reduce_scatter x1, waiting for transfers between devices, shards(): lax.psum_scatter(large_totals[2], 'dp', scatter_dimension=0, tiled=True)  78.3 us
    psum x1, blocking collectives, shards(): lax.psum((small_totals[0], small_totals[1], small_totals[2], small_totals...  62 us
    dot_general x16, matrix products, block_step(): jnp.einsum('ntj,jc->ntc', within, block_rows, preferred_element_type=jnp....  46.9 us
    unnamed x273, local copies, waits for them, and re-layouts  38.4 us
  transfers between devices with their start and end apart: 10, of which 7 were waited for; matrix products, arithmetic and copies ran while one was open for 17% of the time, Pallas kernels for 0%

commit v1 on v0

v1 whole, which is shorter than its diff:
```python
import functools
import math

import jax
import jax.numpy as jnp
from jax import lax
from jax.experimental import pallas as pl
from jax.experimental.pallas import tpu as pltpu
from jax.sharding import PartitionSpec as P

HD = 128
NS = 16
BLK = 512
CTX = 128
CH = 128
TILE = 256
EPS = 1e-05
F32 = jnp.float32
BF16 = jnp.bfloat16
HIGHEST = lax.Precision.HIGHEST
SCALE = HD**-0.5
LOG2 = SCALE * math.log2(math.e)


def swap(value, axis, mask, count):
    return lax.ppermute(value, axis, [(i, i ^ mask) for i in range(count)])


def mm(left, right):
    return lax.dot_general(left, right, (((1,), (0,)), ((), ())), preferred_element_type=F32)


def mm_nt(left, right):
    return lax.dot_general(left, right, (((1,), (1,)), ((), ())), preferred_element_type=F32)


def mm_tn(left, right):
    return lax.dot_general(left, right, (((0,), (0,)), ((), ())), preferred_element_type=F32)


def decay_tables():
    index_n = jnp.arange(NS, dtype=F32)
    rates = 4.0 / CH * jnp.exp2(-8.0 * index_n / (NS - 1))
    norm = jnp.sqrt(-jnp.expm1(-2.0 * rates))
    positions = jnp.arange(CH, dtype=F32)
    offsets = positions[:, None] - positions[None, :]
    powers = jnp.exp(-rates[:, None, None] * jnp.maximum(offsets, 0.0)[None])
    within = jnp.where(offsets[None] >= 0.0, norm[:, None, None] * powers, 0.0).astype(BF16)
    carry_in = jnp.exp(-rates[None, :] * (positions[:, None] + 1.0))
    carry_out = within[:, CH - 1, :]
    whole = jnp.exp(-rates * CH)
    return within, carry_in, carry_out, whole[:, None]


def ssm_forward_kernel(v_ref, within_ref, carry_in_ref, carry_out_ref, whole_ref, coef_ref, skip_ref, out_ref, state_ref):
    whole = whole_ref[...]
    before = BLK // CH - 1
    state = jnp.zeros(state_ref.shape, F32)
    for k in range(before):
        state = whole * state + mm(carry_out_ref[...], v_ref[k * CH : (k + 1) * CH, :])
    state_ref[...] = state
    rows = v_ref[before * CH :, :]
    total = skip_ref[...] * rows.astype(F32)
    total += jnp.dot(carry_in_ref[...], coef_ref[...] * state, precision=HIGHEST, preferred_element_type=F32)
    for n in range(NS):
        total += coef_ref[n : n + 1, :] * mm(within_ref[n], rows)
    out_ref[...] = total.astype(BF16)


def ssm_forward(rows, tables, coef, skip):
    within, carry_in, carry_out, whole = tables
    width = rows.shape[1]
    step = 256
    column = lambda c: (0, c)
    fixed2 = lambda c: (0, 0)
    return pl.pallas_call(
        ssm_forward_kernel,
        grid=(width // step,),
        in_specs=[
            pl.BlockSpec((BLK, step), column),
            pl.BlockSpec((NS, CH, CH), lambda c: (0, 0, 0)),
            pl.BlockSpec((CH, NS), fixed2),
            pl.BlockSpec((NS, CH), fixed2),
            pl.BlockSpec((NS, 1), fixed2),
            pl.BlockSpec((NS, step), column),
            pl.BlockSpec((1, step), column),
        ],
        out_specs=[pl.BlockSpec((CH, step), column), pl.BlockSpec((NS, step), column)],
        out_shape=[jax.ShapeDtypeStruct((CH, width), BF16), jax.ShapeDtypeStruct((NS, width), F32)],
        cost_estimate=pl.CostEstimate(flops=2 * NS * CH * CH * width, bytes_accessed=3 << 20, transcendentals=0),
        name="ssm_forward",
    )(rows, within, carry_in, carry_out, whole, coef, skip)


def ssm_backward_kernel(v_ref, grad_ref, within_ref, carry_in_ref, carry_out_ref, whole_ref, coef_ref, skip_ref, state_ref, du_ref, small_ref):
    before = BLK // CH - 1
    rows = v_ref[...].astype(F32)
    grad = grad_ref[...]
    wide = grad.astype(F32)
    du = skip_ref[...] * wide
    reach = jnp.dot(carry_in_ref[...], wide, precision=HIGHEST, preferred_element_type=F32)
    for n in range(NS):
        back = mm(within_ref[n], grad)
        du += coef_ref[n : n + 1, :] * back
        small_ref[n : n + 1, :] = (
            jnp.sum(rows * back, axis=0, keepdims=True) + state_ref[n : n + 1, :] * reach[n : n + 1, :]
        )
    small_ref[NS : NS + 1, :] = jnp.sum(rows * wide, axis=0, keepdims=True)
    du_ref[before * CH :, :] = du
    state = coef_ref[...] * reach
    for k in reversed(range(before)):
        du_ref[k * CH : (k + 1) * CH, :] = jnp.dot(
            carry_out_ref[...], state, precision=HIGHEST, preferred_element_type=F32
        )
        state = whole_ref[...] * state


def ssm_backward(rows, grad, tables, coef, skip, state):
    within, carry_in, carry_out, whole = tables
    width = rows.shape[1]
    step = 256
    column = lambda c: (0, c)
    fixed2 = lambda c: (0, 0)
    return pl.pallas_call(
        ssm_backward_kernel,
        grid=(width // step,),
        in_specs=[
            pl.BlockSpec((CH, step), lambda c: (BLK // CH - 1, c)),
            pl.BlockSpec((CH, step), column),
            pl.BlockSpec((NS, CH, CH), lambda c: (0, 0, 0)),
            pl.BlockSpec((NS, CH), fixed2),
            pl.BlockSpec((CH, NS), fixed2),
            pl.BlockSpec((NS, 1), fixed2),
            pl.BlockSpec((NS, step), column),
            pl.BlockSpec((1, step), column),
            pl.BlockSpec((NS, step), column),
        ],
        out_specs=[pl.BlockSpec((BLK, step), column), pl.BlockSpec((NS + 1, step), column)],
        out_shape=[jax.ShapeDtypeStruct((BLK, width), F32), jax.ShapeDtypeStruct((NS + 1, width), F32)],
        cost_estimate=pl.CostEstimate(flops=2 * NS * CH * CH * width, bytes_accessed=4 << 20, transcendentals=0),
        name="ssm_backward",
    )(rows, grad, within.swapaxes(1, 2), carry_in.T, carry_out.astype(F32).T, whole, coef, skip, state)


def key_parts(block, tile, k_ref, v_ref, ck_ref, cv_ref):
    parts = []
    if block > 0:
        parts.append((None, ck_ref[0], cv_ref[0], False))
    for piece in range(tile + 1):
        where = slice(block * BLK + piece * TILE, block * BLK + (piece + 1) * TILE)
        parts.append((piece, k_ref[0, where, :], v_ref[0, where, :], piece == tile))
    return parts


def tile_scores(keys, query, masked):
    scores = mm_nt(keys, query)
    if masked:
        key_ids = lax.broadcasted_iota(jnp.int32, scores.shape, 0)
        query_ids = lax.broadcasted_iota(jnp.int32, scores.shape, 1)
        scores = jnp.where(key_ids <= query_ids, scores, -1e30)
    return scores


def attend_forward_kernel(q_ref, k_ref, v_ref, ck_ref, cv_ref, out_ref, lse_ref):
    for block in range(2):
        for tile in range(BLK // TILE):
            base = block * BLK + tile * TILE
            query = q_ref[0, base : base + TILE, :]
            parts = key_parts(block, tile, k_ref, v_ref, ck_ref, cv_ref)
            scores = [tile_scores(keys, query, masked) for _, keys, _, masked in parts]
            top = functools.reduce(jnp.maximum, [jnp.max(s, axis=0, keepdims=True) for s in scores]) * LOG2
            exps = [jnp.exp2(s * LOG2 - top) for s in scores]
            total = functools.reduce(jnp.add, [jnp.sum(e, axis=0, keepdims=True) for e in exps])
            inverse = 1.0 / total
            out = functools.reduce(
                jnp.add,
                [mm_tn(values, (e * inverse).astype(BF16)) for (_, _, values, _), e in zip(parts, exps)],
            )
            out_ref[base : base + TILE, :] = out.T.astype(BF16)
            lse_ref[0, :, base : base + TILE] = top + jnp.log2(total)


def attend_forward(qkv, ckv):
    length, width = qkv.shape[1], qkv.shape[2]
    heads = width // HD
    pick = lambda s: pl.BlockSpec((1, length, HD), lambda h: (s, 0, h))
    pick_context = lambda s: pl.BlockSpec((1, CTX, HD), lambda h: (s, 0, h))
    return pl.pallas_call(
        attend_forward_kernel,
        grid=(heads,),
        in_specs=[pick(0), pick(1), pick(2), pick_context(0), pick_context(1)],
        out_specs=[
            pl.BlockSpec((length, HD), lambda h: (0, h)),
            pl.BlockSpec((1, 1, length), lambda h: (h, 0, 0)),
        ],
        out_shape=[
            jax.ShapeDtypeStruct((length, width), BF16),
            jax.ShapeDtypeStruct((heads, 1, length), F32),
        ],
        cost_estimate=pl.CostEstimate(
            flops=4 * heads * length * BLK * HD, bytes_accessed=5 << 20, transcendentals=heads * length * BLK
        ),
        name="attend_forward",
    )(qkv, qkv, qkv, ckv, ckv)


def attend_backward_kernel(q_ref, k_ref, v_ref, ck_ref, cv_ref, dout_ref, lse_ref, grad_ref, cgrad_ref):
    for block in range(2):
        grads = {}
        for tile in range(BLK // TILE):
            base = block * BLK + tile * TILE
            query = q_ref[0, base : base + TILE, :]
            dout = dout_ref[base : base + TILE, :]
            lse = lse_ref[0, :, base : base + TILE]
            parts = key_parts(block, tile, k_ref, v_ref, ck_ref, cv_ref)
            probs = [jnp.exp2(tile_scores(keys, query, masked) * LOG2 - lse) for _, keys, _, masked in parts]
            dprobs = [mm_nt(values, dout) for _, _, values, _ in parts]
            inner = functools.reduce(
                jnp.add, [jnp.sum(p * d, axis=0, keepdims=True) for p, d in zip(probs, dprobs)]
            )
            dquery = None
            for (name, keys, _, _), p, d in zip(parts, probs, dprobs):
                dscore = (p * (d - inner)).astype(BF16)
                term = mm_tn(keys, dscore)
                dquery = term if dquery is None else dquery + term
                dkey, dvalue = mm(dscore, query), mm(p.astype(BF16), dout)
                if name in grads:
                    grads[name] = (grads[name][0] + dkey, grads[name][1] + dvalue)
                else:
                    grads[name] = (dkey, dvalue)
            grad_ref[0, base : base + TILE, :] = (dquery.T * SCALE).astype(BF16)
        for name, (dkey, dvalue) in grads.items():
            dkey, dvalue = (dkey * SCALE).astype(BF16), dvalue.astype(BF16)
            if name is None:
                cgrad_ref[0] = dkey
                cgrad_ref[1] = dvalue
            else:
                where = slice(block * BLK + name * TILE, block * BLK + (name + 1) * TILE)
                grad_ref[1, where, :] = dkey
                grad_ref[2, where, :] = dvalue


def attend_backward(qkv, ckv, dheads, lse):
    length, width = qkv.shape[1], qkv.shape[2]
    heads = width // HD
    pick = lambda s: pl.BlockSpec((1, length, HD), lambda h: (s, 0, h))
    pick_context = lambda s: pl.BlockSpec((1, CTX, HD), lambda h: (s, 0, h))
    return pl.pallas_call(
        attend_backward_kernel,
        grid=(heads,),
        in_specs=[
            pick(0),
            pick(1),
            pick(2),
            pick_context(0),
            pick_context(1),
            pl.BlockSpec((length, HD), lambda h: (0, h)),
            pl.BlockSpec((1, 1, length), lambda h: (h, 0, 0)),
        ],
        out_specs=[
            pl.BlockSpec((3, length, HD), lambda h: (0, 0, h)),
            pl.BlockSpec((2, CTX, HD), lambda h: (0, 0, h)),
        ],
        out_shape=[
            jax.ShapeDtypeStruct((3, length, width), BF16),
            jax.ShapeDtypeStruct((2, CTX, width), BF16),
        ],
        cost_estimate=pl.CostEstimate(
            flops=10 * heads * length * BLK * HD, bytes_accessed=9 << 20, transcendentals=heads * length * BLK
        ),
        name="attend_backward",
    )(qkv, qkv, qkv, ckv, ckv, dheads, lse)


def normalize(values):
    center = values - jnp.mean(values, axis=-1, keepdims=True)
    rstd = lax.rsqrt(jnp.mean(center * center, axis=-1, keepdims=True) + EPS)
    return center * rstd, rstd


def normalize_backward(grad, hat, rstd, gain):
    dn = grad * gain
    dx = rstd * (dn - jnp.mean(dn, axis=-1, keepdims=True) - hat * jnp.mean(dn * hat, axis=-1, keepdims=True))
    return dx, jnp.sum(grad * hat, axis=0, keepdims=True), jnp.sum(grad, axis=0, keepdims=True)


def gelu_pair(pre):
    root = math.sqrt(2.0 / math.pi)
    squared = pre * pre
    bend = jnp.tanh(root * pre * (1.0 + 0.044715 * squared))
    half = 0.5 * (1.0 + bend)
    slope = half + 0.5 * pre * (1.0 - bend * bend) * (root * (1.0 + 3 * 0.044715 * squared))
    return (pre * half).astype(BF16), slope.astype(BF16)


def shards(dp_count, layer_in, ln1_gain, ln1_bias, qkv_weight, out_weight, ssm_coef, ssm_skip, ln2_gain, ln2_bias, up_weight, down_weight, cotangent):
    width = layer_in.shape[3]
    group = qkv_weight.shape[2]
    hidden_group = up_weight.shape[1]
    mine = lax.axis_index("tensor")
    place = lax.axis_index("dp")
    bits = dp_count.bit_length() - 1
    rows_each = width // dp_count

    over_x = lambda v: swap(v, "tensor", 1, 2)
    over = lambda v, bit: swap(v, "dp", 1 << bit, dp_count)

    quarter = place & 3

    def fetch(weight):
        flat = weight.reshape(-1, weight.shape[-1])
        size = flat.shape[0] // 4
        first = over_x(lax.dynamic_slice_in_dim(flat, quarter * size, size, 0))
        beside = over(first, 1)
        pieces = [(first, 0), (over(first, 0), 1), (beside, 2), (over(beside, 0), 3)]
        whole = jnp.zeros_like(flat)
        for piece, mask in pieces:
            whole = lax.dynamic_update_slice_in_dim(whole, piece, (quarter ^ mask) * size, 0)
        return whole.reshape(weight.shape)

    small = over_x(jnp.concatenate([ssm_coef, ssm_skip[None]], axis=0))
    qkv_other = fetch(qkv_weight)
    out_other = fetch(out_weight)
    up_other = fetch(up_weight)
    down_other = fetch(down_weight)

    def in_order(own, other, axis):
        return jnp.where(
            mine == 0, jnp.concatenate([own, other], axis=axis), jnp.concatenate([other, own], axis=axis)
        )

    coef = in_order(ssm_coef, small[:NS], 1)
    skip = in_order(ssm_skip[None], small[NS:], 1)
    tables = decay_tables()

    column = jnp.arange(width)
    spot = column // rows_each
    code = jnp.zeros_like(spot)
    for bit in range(bits):
        code = code | (((spot >> (bits - 1 - bit)) & 1) << bit)
    source = (code ^ place) * rows_each + column % rows_each
    permutation = (column[:, None] == source[None, :]).astype(BF16)

    def rows_first(values):
        return lax.dot_general(
            permutation, values, (((0,), (1,)), ((), ())), preferred_element_type=F32
        ).astype(BF16)

    def scatter(left, right_own, right_other, x_first):
        half = width // 2
        quart = width // 4
        got_other = over(mm(left[half:], right_other).astype(BF16), 0)
        got_own = over(mm(left[half:], right_own).astype(BF16), 0)
        if x_first:
            got = over_x((mm(left[:half], right_other) + got_other).astype(BF16))
            total = mm(left[:half], right_own) + got_own + got
            got = over(total[quart:].astype(BF16), 1)
            total = total[:quart] + got
        else:
            sum_other = mm(left[:half], right_other) + got_other
            sum_own = mm(left[:half], right_own) + got_own
            beside_other = over(sum_other[quart:].astype(BF16), 1)
            beside_own = over(sum_own[quart:].astype(BF16), 1)
            got = over_x((sum_other[:quart] + beside_other).astype(BF16))
            total = sum_own[:quart] + beside_own + got
        rows = quart
        for bit in range(2, bits):
            rows //= 2
            total = total[:rows] + over(total[rows:].astype(BF16), bit)
        return total

    inputs = lax.dynamic_index_in_dim(layer_in[:, 0], mine, 0, keepdims=False).astype(F32)
    grads = lax.dynamic_index_in_dim(cotangent[:, 0], mine, 0, keepdims=False)
    hat1, rstd1 = normalize(inputs)
    u1 = (hat1 * ln1_gain + ln1_bias).astype(BF16)
    context, state = ssm_forward(u1, tables, coef, skip)

    def project(rows, weight):
        return jnp.einsum("td,sde->ste", rows, weight, preferred_element_type=F32).astype(BF16)

    sides = []
    for weight in (qkv_weight, qkv_other):
        qkv = project(u1, weight)
        ckv = project(context, weight[1:])
        heads, lse = attend_forward(qkv, ckv)
        sides.append((qkv, ckv, heads, lse))
    attn_out = mm(sides[0][2], out_weight) + mm(sides[1][2], out_other)
    middle = inputs + attn_out
    hat2, rstd2 = normalize(middle)
    u2 = (hat2 * ln2_gain + ln2_bias).astype(BF16)
    hid_own, slope_own = gelu_pair(mm(u2, up_weight))
    hid_other, slope_other = gelu_pair(mm(u2, up_other))
    mixed = mm(hid_own, down_weight) + mm(hid_other, down_other)
    layer_out = (middle + mixed).astype(BF16)
    layer_out_other = over_x(layer_out)

    grad_down = scatter(rows_first(grads), hid_own, hid_other, False)
    dpre_own = (mm_nt(grads, down_weight) * slope_own.astype(F32)).astype(BF16)
    dpre_other = (mm_nt(grads, down_other) * slope_other.astype(F32)).astype(BF16)
    grad_up = scatter(rows_first(u2), dpre_own, dpre_other, True)
    du2 = mm_nt(dpre_own, up_weight) + mm_nt(dpre_other, up_other)
    dx2, grad_gain2, grad_bias2 = normalize_backward(du2, hat2, rstd2, ln2_gain)
    dx1 = grads.astype(F32) + dx2
    dattn = dx1.astype(BF16)
    grad_out = scatter(rows_first(dattn), sides[0][2], sides[1][2], False)
    dsides = []
    for (qkv, ckv, heads, lse), weight in zip(sides, (out_weight, out_other)):
        dheads = mm_nt(dattn, weight).astype(BF16)
        dsides.append(attend_backward(qkv, ckv, dheads, lse))
    both = ((dsides[0], qkv_weight), (dsides[1], qkv_other))
    dcontext = sum(
        jnp.einsum("sce,sde->cd", dckv, weight[1:], preferred_element_type=F32) for (_, dckv), weight in both
    )
    du_ssm, small_ssm = ssm_backward(u1, dcontext.astype(BF16), tables, coef, skip, state)
    du1 = sum(jnp.einsum("ste,sde->td", dqkv, weight, preferred_element_type=F32) for (dqkv, _), weight in both)
    du1 = du1 + jnp.concatenate([du_ssm, jnp.zeros_like(du_ssm)], axis=0)
    dx0, grad_gain1, grad_bias1 = normalize_backward(du1, hat1, rstd1, ln1_gain)
    grad_in = (dx1 + dx0).astype(BF16)
    grad_in_other = over_x(grad_in)

    tall = jnp.concatenate([u1, context], axis=0)
    sides_tall = []
    for dqkv, dckv in dsides:
        extra = jnp.concatenate([jnp.zeros_like(dckv[:1]), dckv], axis=0)
        stacked = jnp.concatenate([dqkv, extra], axis=1)
        sides_tall.append(stacked.swapaxes(0, 1).reshape(stacked.shape[1], -1))
    grad_qkv = scatter(rows_first(tall), sides_tall[0], sides_tall[1], True)

    small_all = jnp.concatenate([small_ssm, grad_gain2, grad_bias2, grad_gain1, grad_bias1], axis=0)
    small_all = small_all + over_x(small_all)
    for bit in range(bits):
        small_all = small_all + over(small_all, bit)
    here = lax.dynamic_slice_in_dim(small_all[: NS + 1], mine * group, group, 1)

    def both_parts(own, other):
        stacked = jnp.where(mine == 0, jnp.stack([own, other]), jnp.stack([other, own]))
        return stacked[:, None]

    return (
        both_parts(layer_out, layer_out_other),
        both_parts(grad_in, grad_in_other).astype(F32),
        small_all[NS + 3],
        small_all[NS + 4],
        grad_qkv.reshape(rows_each, 3, group).swapaxes(0, 1),
        grad_out.T,
        here[:NS],
        here[NS],
        small_all[NS + 1],
        small_all[NS + 2],
        grad_up,
        grad_down.T,
    )


def solution(mesh):
    in_specs = (
        P(None, "dp", None, None),
        P(),
        P(),
        P(None, None, "tensor"),
        P("tensor", None),
        P(None, "tensor"),
        P("tensor"),
        P(),
        P(),
        P(None, "tensor"),
        P("tensor", None),
        P(None, "dp", None, None),
    )
    out_specs = (
        P(None, "dp", None, None),
        P(None, "dp", None, None),
        P(),
        P(),
        P(None, "dp", "tensor"),
        P("tensor", "dp"),
        P(None, "tensor"),
        P("tensor"),
        P(),
        P(),
        P("dp", "tensor"),
        P("tensor", "dp"),
    )
    body = functools.partial(shards, mesh.shape["dp"])
    return jax.shard_map(body, mesh=mesh, in_specs=in_specs, out_specs=out_specs, check_vma=False)
```

time: 1400 us -> 671 us (0.48)
  waiting for transfers between devices: 627 us -> 250 us
  matrix products: 339 us -> 209 us
  other arithmetic: 155 us -> 45.3 us
  local copies, waits for them, and re-layouts: 172 us -> 67.4 us
  blocking collectives: 75.4 us -> 0 us
  Pallas kernels: 0 us -> 48.7 us
  starting transfers between devices: 0.41 us -> 38 us
  between operations: 16.9 us -> 2.23 us
    psum x4 -> x0, waiting for transfers between devices: 415 us -> none  [the longest x1 201 us: shards(): lax.psum(mixed_part.astype(jnp.bfloat16), 'tensor').astype(jnp.float32)]
    ppermute x0 -> x50, waiting for transfers between devices: none -> 250 us  [swap(): return lax.ppermute(value, axis, [(i, i ^ mask) for i in range(count)])]
    reduce_scatter x5 -> x0, waiting for transfers between devices: 188 us -> none  [the longest x1 110 us: shards(): lax.psum_scatter(large_totals[3], 'dp', scatter_dimension=1, tiled=True)]
    dot_general x122 -> x40, matrix products: 328 us -> 209 us  [the longest x22 109 us: mm(): lax.dot_general(left, right, (((1,), (0,)), ((), ())), preferred_element_...]
    reduce_sum x45 -> x3, other arithmetic: 69.3 us -> 4.92 us  [the longest x2 2.84 us: normalize(): rstd = lax.rsqrt(jnp.mean(center * center, axis=-1, keepdims=True) + EPS)]
    psum x1 -> x0, blocking collectives: 62 us -> none  [shards(): lax.psum((small_totals[0], small_totals[1], small_totals[2], small_totals...]
    pallas_call x0 -> x6, Pallas kernels: none -> 48.7 us  [the longest x2 22.2 us: attend_backward(): pl.pallas_call(attend_backward_kernel, grid=(heads,), in_specs=[pick(0),...]
    ppermute x0 -> x50, starting transfers between devices: none -> 38 us  [swap(): return lax.ppermute(value, axis, [(i, i ^ mask) for i in range(count)])]
  transfers between devices with their start and end apart: 10 -> 50, of which waited for: 7 -> 17; matrix products, arithmetic and copies ran while one was open for 17% -> 46% of each run, Pallas kernels for 0% -> 7%
where the time goes in v1:
time: 671 us; the launch traced here: 661 us
  waiting for transfers between devices  250 us (37%)
  matrix products  209 us (31%)
  local copies, waits for them, and re-layouts  67.4 us (10%)
  Pallas kernels  48.7 us (7%)
  other arithmetic  45.3 us (7%)
  starting transfers between devices  38 us (6%)
    ppermute x50, waiting for transfers between devices, swap(): return lax.ppermute(value, axis, [(i, i ^ mask) for i in range(count)])  250 us
    dot_general x22, matrix products, mm(): lax.dot_general(left, right, (((1,), (0,)), ((), ())), preferred_element_...  109 us
    dot_general x6, matrix products, mm_nt(): lax.dot_general(left, right, (((1,), (1,)), ((), ())), preferred_element_...  48.9 us
    ppermute x50, starting transfers between devices, swap(): return lax.ppermute(value, axis, [(i, i ^ mask) for i in range(count)])  38 us
    pallas_call x2, Pallas kernels, attend_backward(): pl.pallas_call(attend_backward_kernel, grid=(heads,), in_specs=[pick(0),...  22.2 us
    dot_general x2, matrix products, shards(): jnp.einsum('ste,sde->td', dqkv, weight, preferred_element_type=F32)  19.9 us
    pallas_call x2, Pallas kernels, attend_forward(): pl.pallas_call(attend_forward_kernel, grid=(heads,), in_specs=[pick(0), p...  15.8 us
    dynamic_update_slice x16, local copies, waits for them, and re-layouts, fetch(): lax.dynamic_update_slice_in_dim(whole, piece, (quarter ^ mask) * size, 0)  15.2 us
  transfers between devices with their start and end apart: 50, of which 17 were waited for; matrix products, arithmetic and copies ran while one was open for 46% of the time, Pallas kernels for 7%

profile of v1, /device:TPU:0, one launch (start us, length us, event | category | flops | bytes accessed | tf_op | source)
XLA Modules:
  0.0 660.8 jit_solution(7812308363687392985)
XLA Ops:
  2.8 2.9 collective-permute-start.1
  9.3 2.4 constant_dynamic-slice_fusion.2
  22.1 5.6 select_convert_fusion
  31.3 4.8 convert_bitcast_fusion.2.q_ref.k_ref.v_ref
  36.1 3.7 fusion.66
  39.8 6.3 multiply_select_fusion
  46.7 4.6 copy.47.within_ref
  52.0 4.6 copy.55.within_ref
  57.9 5.0 ssm_forward.1
  62.9 5.3 fusion.34
  70.9 8.0 %attend_forward.2 = (bf16[1024,512]{1,0:T(8,128)(2,1)}, f32[4,1,1024]{2,1,0:T(1,128)}) custom-call(bf16[3,1024,512]{2,1,0:T(8,128)(2,1)} %convert_bitcast_fusion.2.q_ref.k_ref.v_ref, bf16[3,1024,512]{2,1,0:T(8,128)(2,1)} %convert_bitcast_fusion.2.q_ref.k_ref.v_ref, bf16[3,1024,512]{2,1,0:T(8,128)(2,1)} %convert_bitcast_fusion.2.q_ref.k_ref.v_ref, ...), custom_call_target="tpu_custom_call" | custom-call | flops 1073741824 | bytes 5242880 | tf_op jit(solution)/shard_map/attend_forward/pallas_call | solution.py:188
  79.6 4.5 fusion.172
  92.4 2.6 broadcast_in_dim.41
  97.3 8.5 %collective-permute-done.3 = bf16[768,512]{1,0:T(8,128)(2,1)S(1)} collective-permute-done((bf16[768,512]{1,0:T(8,128)(2,1)}, bf16[768,512]{1,0:T(8,128)(2,1)S(1)}, u32[]{:S(2)}, u32[]{:S(2)}) %collective-permute-start.3) | collective-permute-done | bytes 786464 | tf_op jit(solution)/shard_map/ppermute | solution.py:26
  106.0 44.4 %collective-permute-done.11 = bf16[256,2048]{1,0:T(8,128)(2,1)} collective-permute-done((bf16[256,2048]{1,0:T(8,128)(2,1)}, bf16[256,2048]{1,0:T(8,128)(2,1)}, u32[]{:S(2)}, u32[]{:S(2)}) %collective-permute-start.11) | collective-permute-done | bytes 1048608 | tf_op jit(solution)/shard_map/ppermute | solution.py:26
  160.1 5.1 convert_bitcast_fusion.1.q_ref.k_ref.v_ref
  165.2 7.8 %attend_forward.3 = (bf16[1024,512]{1,0:T(8,128)(2,1)}, f32[4,1,1024]{2,1,0:T(1,128)}) custom-call(bf16[3,1024,512]{2,1,0:T(8,128)(2,1)} %convert_bitcast_fusion.1.q_ref.k_ref.v_ref, bf16[3,1024,512]{2,1,0:T(8,128)(2,1)} %convert_bitcast_fusion.1.q_ref.k_ref.v_ref, bf16[3,1024,512]{2,1,0:T(8,128)(2,1)} %convert_bitcast_fusion.1.q_ref.k_ref.v_ref, ...), custom_call_target="tpu_custom_call" | custom-call | flops 1073741824 | bytes 5242880 | tf_op jit(solution)/shard_map/attend_forward/pallas_call | solution.py:188
  173.0 4.5 fusion.171
  181.2 9.2 %multiply_convert_fusion.3 = (bf16[1024,2048]{1,0:T(8,128)(2,1)}, f32[1024,2048]{1,0:T(8,128)}) fusion(bf16[1024,1024]{1,0:T(8,128)(2,1)S(1)} %add_convert_fusion.4, bf16[1024,2048]{1,0:T(8,128)(2,1)S(1)} %copy-done.31), kind=kOutput, calls=%fused_computation.8 | convolution fusion | flops 4313841664 | bytes 18874368 | tf_op jit(solution)/shard_map/dot_general | solution.py:30
  190.5 2.4 fusion.63
  194.0 11.9 %multiply_convert_fusion.1 = bf16[1024,2048]{1,0:T(8,128)(2,1)} fusion(bf16[2048,1024]{1,0:T(8,128)(2,1)S(1)} %copy-done.32, f32[1024,2048]{1,0:T(8,128)} %get-tuple-element.77, bf16[2,1,1024,1024]{3,2,1,0:T(8,128)(2,1)S(1)} %copy-done.28, s32[]{:T(128)S(6)} %select_n.134), kind=kOutput, calls=%fused_computation.3 | convolution fusion | flops 4336910336 | bytes 18874372 | tf_op jit(solution)/shard_map/dot_general | solution.py:34
  205.9 6.0 convolution_convert_fusion.3
  211.9 4.5 fusion.112
  216.4 8.7 %fusion.174 = f32[1024,1024]{1,0:T(8,128)} fusion(bf16[1024,2048]{1,0:T(8,128)(2,1)} %multiply_convert_fusion.1, bf16[1024,2048]{1,0:T(8,128)(2,1)S(1)} %copy-done.31), kind=kOutput, calls=%fused_computation.268 | convolution fusion | flops 4294967296 | bytes 12582912 | tf_op jit(solution)/shard_map/dot_general | solution.py:34
  225.1 3.7 convolution_convert_fusion.1
  228.8 6.0 fusion.173
  237.2 10.5 %multiply_convert_fusion.2 = (bf16[1024,2048]{1,0:T(8,128)(2,1)S(1)}, f32[1024,2048]{1,0:T(8,128)}) fusion(bf16[1024,1024]{1,0:T(8,128)(2,1)S(1)} %add_convert_fusion.4, bf16[1024,2048]{1,0:T(8,128)(2,1)} %constant_dynamic-update-slice_fusion.4), kind=kOutput, calls=%fused_computation.5 | convolution fusion | flops 4313841664 | bytes 18874368 | tf_op jit(solution)/shard_map/dot_general | solution.py:30
  249.9 13.4 %multiply_convert_fusion = bf16[1024,2048]{1,0:T(8,128)(2,1)} fusion(bf16[2048,1024]{1,0:T(8,128)(2,1)S(1)} %constant_dynamic-update-slice_fusion, f32[1024,2048]{1,0:T(8,128)} %get-tuple-element.79, bf16[2,1,1024,1024]{3,2,1,0:T(8,128)(2,1)S(1)} %copy-done.28, s32[]{:T(128)S(6)} %select_n.134), kind=kOutput, calls=%fused_computation.1 | convolution fusion | flops 4336910336 | bytes 18874372 | tf_op jit(solution)/shard_map/dot_general | solution.py:34
  263.3 5.9 convolution_convert_fusion.2
  269.2 10.3 %multiply_reduce_fusion = (f32[1024]{0:T(1024)S(1)}, f32[1024]{0:T(1024)S(1)}, f32[1024]{0:T(1024)S(1)}, f32[1024]{0:T(1024)S(1)}, f32[1024,1024]{1,0:T(8,128)S(1)}) fusion(f32[1024,1024]{1,0:T(8,128)S(1)} %get-tuple-element.75, f32[1024]{0:T(1024)S(1)} %add_rsqrt_fusion, f32[1024]{0:T(1024)S(1)} %broadcast_multiply_fusion.4, f32[1024]{0:T(1024)S(1)} %copy-done.40, ...), kind=kOutput, calls=%fused_computation.49 | convolution fusion | flops 4305448960 | bytes 21000192 | tf_op jit(solution)/shard_map/dot_general | solution.py:34
  281.6 2.4 fusion.60
  291.5 3.7 convolution_convert_fusion
  296.3 11.0 %attend_backward.2 = (bf16[3,1024,512]{2,1,0:T(8,128)(2,1)}, bf16[2,128,512]{2,1,0:T(8,128)(2,1)}) custom-call(bf16[3,1024,512]{2,1,0:T(8,128)(2,1)} %convert_bitcast_fusion.2.q_ref.k_ref.v_ref, bf16[3,1024,512]{2,1,0:T(8,128)(2,1)} %convert_bitcast_fusion.2.q_ref.k_ref.v_ref, bf16[3,1024,512]{2,1,0:T(8,128)(2,1)} %convert_bitcast_fusion.2.q_ref.k_ref.v_ref, ...), custom_call_target="tpu_custom_call" | custom-call | flops 2684354560 | bytes 9437184 | tf_op jit(solution)/shard_map/attend_backward/pallas_call | solution.py:248
  307.2 3.3 fusion.78
  310.5 8.3 %fusion.175 = f32[1024,1024,1]{1,0,2:T(8,128)} fusion(bf16[3,1024,512]{2,1,0:T(8,128)(2,1)} %get-tuple-element.28, bf16[3,1024,512]{2,1,0:T(8,128)(2,1)} %param.15), kind=kOutput, calls=%fused_computation.269 | convolution fusion | flops 3221225472 | bytes 10485760 | tf_op jit(solution)/shard_map/ste,sde->td/dot_general | solution.py:415
  318.9 11.2 %attend_backward.3 = (bf16[3,1024,512]{2,1,0:T(8,128)(2,1)}, bf16[2,128,512]{2,1,0:T(8,128)(2,1)}) custom-call(bf16[3,1024,512]{2,1,0:T(8,128)(2,1)} %convert_bitcast_fusion.1.q_ref.k_ref.v_ref, bf16[3,1024,512]{2,1,0:T(8,128)(2,1)} %convert_bitcast_fusion.1.q_ref.k_ref.v_ref, bf16[3,1024,512]{2,1,0:T(8,128)(2,1)} %convert_bitcast_fusion.1.q_ref.k_ref.v_ref, ...), custom_call_target="tpu_custom_call" | custom-call | flops 2684354560 | bytes 9437184 | tf_op jit(solution)/shard_map/attend_backward/pallas_call | solution.py:248
  330.1 2.6 fusion.85.grad_ref
  332.7 5.7 ssm_backward.1
  338.5 11.5 %fusion.17 = (f32[1024]{0:T(1024)S(1)}, f32[1024]{0:T(1024)S(1)}, f32[1024]{0:T(1024)S(1)}, f32[1024]{0:T(1024)S(1)}, f32[1024,1024]{1,0:T(8,128)}) fusion(f32[1024]{0:T(1024)S(1)} %add_rsqrt_fusion.1, f32[1024]{0:T(1024)S(1)} %broadcast_multiply_fusion.5, bf16[2,1,1024,1024]{3,2,1,0:T(8,128)(2,1)} %param.12, s32[]{:T(128)S(6)} %select_n.134, ...), kind=kOutput, calls=%fused_computation.33 | convolution fusion | flops 3233804288 | bytes 18903044 | tf_op jit(solution)/shard_map/ste,sde->td/dot_general | solution.py:415
  350.6 11.8 %add_convert_fusion.3 = bf16[1024,1024]{1,0:T(8,128)(2,1)} fusion(f32[1024,1024]{1,0:T(8,128)} %copy-done.1, f32[1024,1024]{1,0:T(8,128)} %fusion.173, bf16[1024,2048]{1,0:T(8,128)(2,1)} %copy-done.52, bf16[2048,1024]{1,0:T(8,128)(2,1)} %copy-done.19), kind=kOutput, calls=%fused_computation.52 | convolution fusion | flops 4298113024 | bytes 18874368 | tf_op jit(solution)/shard_map/dot_general | solution.py:30
  366.2 5.7 copy.56
  372.1 6.3 fusion.94
  378.8 3.4 convolution_convert_fusion.5
  387.3 5.9 copy.57
  393.3 2.6 collective-permute-start.23
  395.9 2.4 convert_add_fusion.4
  402.3 5.3 collective-permute-done.33
  415.4 3.9 collective-permute-done.35
  420.7 4.6 collective-permute-done.36
  427.5 4.0 convert_add_fusion.1
  432.2 4.7 add_convert_fusion.5
  438.5 5.5 convert_add_fusion
  444.1 29.7 %collective-permute-done.17 = bf16[1024,1024]{1,0:T(8,128)(2,1)S(1)} collective-permute-done((bf16[1024,1024]{1,0:T(8,128)(2,1)S(1)}, bf16[1024,1024]{1,0:T(8,128)(2,1)S(1)}, u32[]{:S(2)}, u32[]{:S(2)}) %collective-permute-start.17) | collective-permute-done | bytes 2097184 | tf_op jit(solution)/shard_map/ppermute | solution.py:26
  473.8 2.5 maximum_select_fusion
  477.5 4.9 add_convert_fusion.2
  483.2 66.2 %collective-permute-done.26 = bf16[512,1536]{1,0:T(8,128)(2,1)S(1)} collective-permute-done((bf16[512,1536]{1,0:T(8,128)(2,1)}, bf16[512,1536]{1,0:T(8,128)(2,1)S(1)}, u32[]{:S(2)}, u32[]{:S(2)}) %collective-permute-start.26) | collective-permute-done | bytes 1572896 | tf_op jit(solution)/shard_map/ppermute | solution.py:26
  552.3 4.0 fusion.23
  557.1 6.3 collective-permute-done.27
  563.9 34.4 %collective-permute-done.39 = bf16[512,2048]{1,0:T(8,128)(2,1)S(1)} collective-permute-done((bf16[512,2048]{1,0:T(8,128)(2,1)}, bf16[512,2048]{1,0:T(8,128)(2,1)S(1)}, u32[]{:S(2)}, u32[]{:S(2)}) %collective-permute-start.39) | collective-permute-done | bytes 2097184 | tf_op jit(solution)/shard_map/ppermute | solution.py:26
  600.1 15.1 %collective-permute-done.47 = bf16[256,2048]{1,0:T(8,128)(2,1)S(1)} collective-permute-done((bf16[256,2048]{1,0:T(8,128)(2,1)S(1)}, bf16[256,2048]{1,0:T(8,128)(2,1)S(1)}, u32[]{:S(2)}, u32[]{:S(2)}) %collective-permute-start.47) | collective-permute-done | bytes 1048608 | tf_op jit(solution)/shard_map/ppermute | solution.py:26
  621.2 12.1 %collective-permute-done.29 = bf16[64,1536]{1,0:T(8,128)(2,1)S(1)} collective-permute-done((bf16[64,1536]{1,0:T(8,128)(2,1)S(1)}, bf16[64,1536]{1,0:T(8,128)(2,1)S(1)}, u32[]{:S(2)}, u32[]{:S(2)}) %collective-permute-start.29) | collective-permute-done | bytes 196640 | tf_op jit(solution)/shard_map/ppermute | solution.py:26
  637.7 3.3 collective-permute-start.49
  641.1 2.7 collective-permute-done.41
  645.0 11.2 %collective-permute-done.49 = bf16[64,2048]{1,0:T(8,128)(2,1)S(1)} collective-permute-done((bf16[64,2048]{1,0:T(8,128)(2,1)S(1)}, bf16[64,2048]{1,0:T(8,128)(2,1)S(1)}, u32[]{:S(2)}, u32[]{:S(2)}) %collective-permute-start.49) | collective-permute-done | bytes 262176 | tf_op jit(solution)/shard_map/ppermute | solution.py:26
  (312 shorter events, 116.8 us)
Async XLA Ops:
  2.8 76.7 %collective-permute-start.1 = (bf16[768,512]{1,0:T(8,128)(2,1)}, bf16[768,512]{1,0:T(8,128)(2,1)}, u32[]{:S(2)}, u32[]{:S(2)}) collective-permute-start(bf16[768,512]{1,0:T(8,128)(2,1)} %constant_dynamic-slice_fusion.4), channel_id=1, source_target_pairs={{0,1},{1,0},{2,3},{3,2},{4,5},{5,4},{6,7},{7,6},{8,9},{9,8},{10,11... | collective-permute-start | bytes 2359304 | tf_op jit(solution)/shard_map/ppermute | solution.py:26
  6.5 50.1 %collective-permute-start = (f32[17,512]{1,0:T(8,128)S(1)}, f32[17,512]{1,0:T(8,128)S(1)}, u32[]{:S(2)}, u32[]{:S(2)}) collective-permute-start(f32[17,512]{1,0:T(8,128)S(1)} %pad_maximum_fusion), channel_id=1, source_target_pairs={{0,1},{1,0},{2,3},{3,2},{4,5},{5,4},{6,7},{7,6},{8,9},{9,8},{10,11... | collective-permute-start | bytes 104456 | tf_op jit(solution)/shard_map/ppermute | solution.py:26
  7.3 61.0 %collective-permute-start.5 = (bf16[128,1024]{1,0:T(8,128)(2,1)}, bf16[128,1024]{1,0:T(8,128)(2,1)}, u32[]{:S(2)}, u32[]{:S(2)}) collective-permute-start(bf16[128,1024]{1,0:T(8,128)(2,1)} %constant_dynamic-slice_fusion.3), channel_id=1, source_target_pairs={{0,1},{1,0},{2,3},{3,2},{4,5},{5,4},{6,7},{7,6},{8,9},{9,8},{10,11... | collective-permute-start | bytes 786440 | tf_op jit(solution)/shard_map/ppermute | solution.py:26
  11.7 75.8 %collective-permute-start.9 = (bf16[256,2048]{1,0:T(8,128)(2,1)}, bf16[256,2048]{1,0:T(8,128)(2,1)}, u32[]{:S(2)}, u32[]{:S(2)}) collective-permute-start(bf16[256,2048]{1,0:T(8,128)(2,1)} %constant_dynamic-slice_fusion.2), channel_id=1, source_target_pairs={{0,1},{1,0},{2,3},{3,2},{4,5},{5,4},{6,7},{7,6},{8,9},{9,8},{10,11... | collective-permute-start | bytes 3145736 | tf_op jit(solution)/shard_map/ppermute | solution.py:26
  14.1 71.7 %collective-permute-start.13 = (bf16[512,1024]{1,0:T(8,128)(2,1)}, bf16[512,1024]{1,0:T(8,128)(2,1)}, u32[]{:S(2)}, u32[]{:S(2)}) collective-permute-start(bf16[512,1024]{1,0:T(8,128)(2,1)} %constant_dynamic-slice_fusion.1), channel_id=1, source_target_pairs={{0,1},{1,0},{2,3},{3,2},{4,5},{5,4},{6,7},{7,6},{8,9},{9,8},{10,11... | collective-permute-start | bytes 3145736 | tf_op jit(solution)/shard_map/ppermute | solution.py:26
  17.7 12.7 %copy-start.43 = (f32[1024]{0:T(1024)S(1)}, f32[1024]{0:T(1024)}, u32[]{:S(2)}) copy-start(f32[1024]{0:T(1024)} %param.14) | copy-start | bytes 12292
  68.2 10.8 %collective-permute-start.7 = (bf16[128,1024]{1,0:T(8,128)(2,1)}, bf16[128,1024]{1,0:T(8,128)(2,1)S(1)}, u32[]{:S(2)}, u32[]{:S(2)}) collective-permute-start(bf16[128,1024]{1,0:T(8,128)(2,1)} %collective-permute-done.5), channel_id=1, source_target_pairs={{0,4},{2,6},{4,0},{6,2},{8,12},{10,14},{12,8},{14,10},{16,20},{18,... | collective-permute-start | bytes 786440 | tf_op jit(solution)/shard_map/ppermute | solution.py:26
  79.0 6.3 collective-permute-start.6
  79.1 6.9 %collective-permute-start.8 = (bf16[128,1024]{1,0:T(8,128)(2,1)S(1)}, bf16[128,1024]{1,0:T(8,128)(2,1)S(1)}, u32[]{:S(2)}, u32[]{:S(2)}) collective-permute-start(bf16[128,1024]{1,0:T(8,128)(2,1)S(1)} %collective-permute-done.7), channel_id=1, source_target_pairs={{0,2},{2,0},{4,6},{6,4},{8,10},{10,8},{12,14},{14,12},{16,18},{18,... | collective-permute-start | bytes 786440 | tf_op jit(solution)/shard_map/ppermute | solution.py:26
  79.5 9.5 %collective-permute-start.2 = (bf16[768,512]{1,0:T(8,128)(2,1)}, bf16[768,512]{1,0:T(8,128)(2,1)S(1)}, u32[]{:S(2)}, u32[]{:S(2)}) collective-permute-start(bf16[768,512]{1,0:T(8,128)(2,1)} %collective-permute-done.1), channel_id=1, source_target_pairs={{0,2},{2,0},{4,6},{6,4},{8,10},{10,8},{12,14},{14,12},{16,18},{18,... | collective-permute-start | bytes 2359304 | tf_op jit(solution)/shard_map/ppermute | solution.py:26
  85.2 20.6 %collective-permute-start.3 = (bf16[768,512]{1,0:T(8,128)(2,1)}, bf16[768,512]{1,0:T(8,128)(2,1)S(1)}, u32[]{:S(2)}, u32[]{:S(2)}) collective-permute-start(bf16[768,512]{1,0:T(8,128)(2,1)} %collective-permute-done.1), channel_id=1, source_target_pairs={{0,4},{2,6},{4,0},{6,2},{8,12},{10,14},{12,8},{14,10},{16,20},{18,... | collective-permute-start | bytes 2359304 | tf_op jit(solution)/shard_map/ppermute | solution.py:26
  85.8 65.1 %collective-permute-start.14 = (bf16[512,1024]{1,0:T(8,128)(2,1)}, bf16[512,1024]{1,0:T(8,128)(2,1)S(1)}, u32[]{:S(2)}, u32[]{:S(2)}) collective-permute-start(bf16[512,1024]{1,0:T(8,128)(2,1)} %collective-permute-done.13), channel_id=1, source_target_pairs={{0,2},{2,0},{4,6},{6,4},{8,10},{10,8},{12,14},{14,12},{16,18},{18,... | collective-permute-start | bytes 3145736 | tf_op jit(solution)/shard_map/ppermute | solution.py:26
  86.0 64.5 %collective-permute-start.15 = (bf16[512,1024]{1,0:T(8,128)(2,1)}, bf16[512,1024]{1,0:T(8,128)(2,1)S(1)}, u32[]{:S(2)}, u32[]{:S(2)}) collective-permute-start(bf16[512,1024]{1,0:T(8,128)(2,1)} %collective-permute-done.13), channel_id=1, source_target_pairs={{0,4},{2,6},{4,0},{6,2},{8,12},{10,14},{12,8},{14,10},{16,20},{18,... | collective-permute-start | bytes 3145736 | tf_op jit(solution)/shard_map/ppermute | solution.py:26
  87.5 62.9 %collective-permute-start.11 = (bf16[256,2048]{1,0:T(8,128)(2,1)}, bf16[256,2048]{1,0:T(8,128)(2,1)}, u32[]{:S(2)}, u32[]{:S(2)}) collective-permute-start(bf16[256,2048]{1,0:T(8,128)(2,1)} %collective-permute-done.9), channel_id=1, source_target_pairs={{0,4},{2,6},{4,0},{6,2},{8,12},{10,14},{12,8},{14,10},{16,20},{18,... | collective-permute-start | bytes 3145736 | tf_op jit(solution)/shard_map/ppermute | solution.py:26
  89.1 62.1 %collective-permute-start.10 = (bf16[256,2048]{1,0:T(8,128)(2,1)}, bf16[256,2048]{1,0:T(8,128)(2,1)S(1)}, u32[]{:S(2)}, u32[]{:S(2)}) collective-permute-start(bf16[256,2048]{1,0:T(8,128)(2,1)} %collective-permute-done.9), channel_id=1, source_target_pairs={{0,2},{2,0},{4,6},{6,4},{8,10},{10,8},{12,14},{14,12},{16,18},{18,... | collective-permute-start | bytes 3145736 | tf_op jit(solution)/shard_map/ppermute | solution.py:26
  105.9 50.1 %collective-permute-start.4 = (bf16[768,512]{1,0:T(8,128)(2,1)S(1)}, bf16[768,512]{1,0:T(8,128)(2,1)S(1)}, u32[]{:S(2)}, u32[]{:S(2)}) collective-permute-start(bf16[768,512]{1,0:T(8,128)(2,1)S(1)} %collective-permute-done.3), channel_id=1, source_target_pairs={{0,2},{2,0},{4,6},{6,4},{8,10},{10,8},{12,14},{14,12},{16,18},{18,... | collective-permute-start | bytes 2359304 | tf_op jit(solution)/shard_map/ppermute | solution.py:26
  150.4 84.4 %collective-permute-start.12 = (bf16[256,2048]{1,0:T(8,128)(2,1)}, bf16[256,2048]{1,0:T(8,128)(2,1)}, u32[]{:S(2)}, u32[]{:S(2)}) collective-permute-start(bf16[256,2048]{1,0:T(8,128)(2,1)} %collective-permute-done.11), channel_id=1, source_target_pairs={{0,2},{2,0},{4,6},{6,4},{8,10},{10,8},{12,14},{14,12},{16,18},{18,... | collective-permute-start | bytes 3145736 | tf_op jit(solution)/shard_map/ppermute | solution.py:26
  150.5 97.3 %collective-permute-start.16 = (bf16[512,1024]{1,0:T(8,128)(2,1)S(1)}, bf16[512,1024]{1,0:T(8,128)(2,1)}, u32[]{:S(2)}, u32[]{:S(2)}) collective-permute-start(bf16[512,1024]{1,0:T(8,128)(2,1)S(1)} %collective-permute-done.15), channel_id=1, source_target_pairs={{0,2},{2,0},{4,6},{6,4},{8,10},{10,8},{12,14},{14,12},{16,18},{18,... | collective-permute-start | bytes 3145736 | tf_op jit(solution)/shard_map/ppermute | solution.py:26
  177.5 102.0 %copy-start.1 = (f32[1024,1024]{1,0:T(8,128)}, f32[1024,1024]{1,0:T(8,128)S(1)}, u32[]{:S(2)}) copy-start(f32[1024,1024]{1,0:T(8,128)S(1)} %get-tuple-element.75) | copy-start | bytes 12582916
  192.9 19.0 %copy-start.59 = (bf16[1024,1024]{1,0:T(8,128)(2,1)}, bf16[1024,1024]{1,0:T(8,128)(2,1)S(1)}, u32[]{:S(2)}) copy-start(bf16[1024,1024]{1,0:T(8,128)(2,1)S(1)} %fusion.63) | copy-start | bytes 6291460
  228.8 198.7 %collective-permute-start.43 = (bf16[512,2048]{1,0:T(8,128)(2,1)}, bf16[512,2048]{1,0:T(8,128)(2,1)}, u32[]{:S(2)}, u32[]{:S(2)}) collective-permute-start(bf16[512,2048]{1,0:T(8,128)(2,1)} %convolution_convert_fusion.1), channel_id=1, source_target_pairs={{0,2},{2,0},{4,6},{6,4},{8,10},{10,8},{12,14},{14,12},{16,18},{18,... | collective-permute-start | bytes 6291464 | tf_op jit(solution)/shard_map/ppermute | solution.py:26
  247.7 43.8 %copy-start.52 = (bf16[1024,2048]{1,0:T(8,128)(2,1)}, bf16[1024,2048]{1,0:T(8,128)(2,1)S(1)}, u32[]{:S(2)}) copy-start(bf16[1024,2048]{1,0:T(8,128)(2,1)S(1)} %get-tuple-element.78) | copy-start | bytes 12582916
  249.9 13.5 %copy-start.19 = (bf16[2048,1024]{1,0:T(8,128)(2,1)}, bf16[2048,1024]{1,0:T(8,128)(2,1)S(1)}, u32[]{:S(2)}) copy-start(bf16[2048,1024]{1,0:T(8,128)(2,1)S(1)} %constant_dynamic-update-slice_fusion) | copy-start | bytes 12582916
  249.9 13.5 %copy-start.60 = (bf16[1024,1024]{1,0:T(8,128)(2,1)S(1)}, bf16[1024,1024]{1,0:T(8,128)(2,1)}, u32[]{:S(2)}) copy-start(bf16[1024,1024]{1,0:T(8,128)(2,1)} %copy-done.59) | copy-start | bytes 6291460
  295.2 141.6 %collective-permute-start.45 = (bf16[512,2048]{1,0:T(8,128)(2,1)}, bf16[512,2048]{1,0:T(8,128)(2,1)}, u32[]{:S(2)}, u32[]{:S(2)}) collective-permute-start(bf16[512,2048]{1,0:T(8,128)(2,1)} %convolution_convert_fusion), channel_id=1, source_target_pairs={{0,2},{2,0},{4,6},{6,4},{8,10},{10,8},{12,14},{14,12},{16,18},{18,... | collective-permute-start | bytes 6291464 | tf_op jit(solution)/shard_map/ppermute | solution.py:26
  295.8 100.2 %collective-permute-start.32 = (bf16[512,512]{1,0:T(8,128)(2,1)}, bf16[512,512]{1,0:T(8,128)(2,1)}, u32[]{:S(2)}, u32[]{:S(2)}) collective-permute-start(bf16[512,512]{1,0:T(8,128)(2,1)} %convolution_convert_fusion.8), channel_id=1, source_target_pairs={{0,2},{2,0},{4,6},{6,4},{8,10},{10,8},{12,14},{14,12},{16,18},{18,... | collective-permute-start | bytes 1572872 | tf_op jit(solution)/shard_map/ppermute | solution.py:26
  295.8 103.1 %collective-permute-start.30 = (bf16[512,512]{1,0:T(8,128)(2,1)}, bf16[512,512]{1,0:T(8,128)(2,1)}, u32[]{:S(2)}, u32[]{:S(2)}) collective-permute-start(bf16[512,512]{1,0:T(8,128)(2,1)} %convolution_convert_fusion.9), channel_id=1, source_target_pairs={{0,2},{2,0},{4,6},{6,4},{8,10},{10,8},{12,14},{14,12},{16,18},{18,... | collective-permute-start | bytes 1572872 | tf_op jit(solution)/shard_map/ppermute | solution.py:26
  350.0 21.9 %collective-permute-start.19 = (f32[21,1024]{1,0:T(8,128)S(1)}, f32[21,1024]{1,0:T(8,128)S(1)}, u32[]{:S(2)}, u32[]{:S(2)}) collective-permute-start(f32[21,1024]{1,0:T(8,128)S(1)} %concatenate.86), channel_id=1, source_target_pairs={{0,1},{1,0},{2,3},{3,2},{4,5},{5,4},{6,7},{7,6},{8,9},{9,8},{10,11... | collective-permute-start | bytes 258056 | tf_op jit(solution)/shard_map/ppermute | solution.py:26
  372.0 6.5 collective-permute-start.20
  378.5 5.2 collective-permute-start.21
  383.7 9.5 %collective-permute-start.22 = (f32[21,1024]{1,0:T(8,128)S(1)}, f32[21,1024]{1,0:T(8,128)S(1)}, u32[]{:S(2)}, u32[]{:S(2)}) collective-permute-start(f32[21,1024]{1,0:T(8,128)S(1)} %add.332), channel_id=1, source_target_pairs={{0,8},{2,10},{4,12},{6,14},{8,0},{10,2},{12,4},{14,6},{16,24},{18,... | collective-permute-start | bytes 258056 | tf_op jit(solution)/shard_map/ppermute | solution.py:26
  393.3 16.1 %copy-start.20 = (bf16[1152,3,512]{0,2,1:T(8,128)(2,1)S(1)}, bf16[1152,3,512]{0,2,1:T(8,128)(2,1)}, u32[]{:S(2)}) copy-start(bf16[1152,3,512]{0,2,1:T(8,128)(2,1)} %copy.57) | copy-start | bytes 10616836
  393.3 16.0 %copy-start.56 = (bf16[1024,1152]{1,0:T(8,128)(2,1)S(1)}, bf16[1024,1152]{1,0:T(8,128)(2,1)}, u32[]{:S(2)}) copy-start(bf16[1024,1152]{1,0:T(8,128)(2,1)} %fusion.34) | copy-start | bytes 7077892
  393.3 18.3 %collective-permute-start.23 = (f32[21,1024]{1,0:T(8,128)S(1)}, f32[21,1024]{1,0:T(8,128)S(1)}, u32[]{:S(2)}, u32[]{:S(2)}) collective-permute-start(f32[21,1024]{1,0:T(8,128)S(1)} %add.333), channel_id=1, source_target_pairs={{0,16},{2,18},{4,20},{6,22},{8,24},{10,26},{12,28},{14,30},{16,0},... | collective-permute-start | bytes 258056 | tf_op jit(solution)/shard_map/ppermute | solution.py:26
  398.4 9.3 %collective-permute-start.33 = (bf16[256,512]{1,0:T(8,128)(2,1)S(1)}, bf16[256,512]{1,0:T(8,128)(2,1)S(1)}, u32[]{:S(2)}, u32[]{:S(2)}) collective-permute-start(bf16[256,512]{1,0:T(8,128)(2,1)S(1)} %slice.373), channel_id=1, source_target_pairs={{0,4},{2,6},{4,0},{6,2},{8,12},{10,14},{12,8},{14,10},{16,20},{18,... | collective-permute-start | bytes 786440 | tf_op jit(solution)/shard_map/ppermute | solution.py:26
  400.7 11.6 %collective-permute-start.31 = (bf16[256,512]{1,0:T(8,128)(2,1)S(1)}, bf16[256,512]{1,0:T(8,128)(2,1)S(1)}, u32[]{:S(2)}, u32[]{:S(2)}) collective-permute-start(bf16[256,512]{1,0:T(8,128)(2,1)S(1)} %slice.374), channel_id=1, source_target_pairs={{0,4},{2,6},{4,0},{6,2},{8,12},{10,14},{12,8},{14,10},{16,20},{18,... | collective-permute-start | bytes 786440 | tf_op jit(solution)/shard_map/ppermute | solution.py:26
  407.7 6.4 collective-permute-start.34
  409.3 15.9 %copy-start.25 = (bf16[1024,1024]{1,0:T(8,128)(2,1)S(1)}, bf16[1024,1024]{1,0:T(8,128)(2,1)}, u32[]{:S(2)}) copy-start(bf16[1024,1024]{1,0:T(8,128)(2,1)} %add_convert_fusion.3) | copy-start | bytes 6291460
  409.3 18.2 %copy-start.51 = (bf16[1024,2048]{1,0:T(8,128)(2,1)S(1)}, bf16[1024,2048]{1,0:T(8,128)(2,1)}, u32[]{:S(2)}) copy-start(bf16[1024,2048]{1,0:T(8,128)(2,1)} %get-tuple-element.76) | copy-start | bytes 12582916
  409.3 18.2 %copy-start.54 = (bf16[1024,1024]{1,0:T(8,128)(2,1)S(1)}, bf16[1024,1024]{1,0:T(8,128)(2,1)}, u32[]{:S(2)}) copy-start(bf16[1024,1024]{1,0:T(8,128)(2,1)} %fusion.66) | copy-start | bytes 6291460
  411.6 64.7 %collective-permute-start.38 = (bf16[512,2048]{1,0:T(8,128)(2,1)S(1)}, bf16[512,2048]{1,0:T(8,128)(2,1)S(1)}, u32[]{:S(2)}, u32[]{:S(2)}) collective-permute-start(bf16[512,2048]{1,0:T(8,128)(2,1)S(1)} %copy-done.45), channel_id=1, source_target_pairs={{0,2},{2,0},{4,6},{6,4},{8,10},{10,8},{12,14},{14,12},{16,18},{18,... | collective-permute-start | bytes 6291464 | tf_op jit(solution)/shard_map/ppermute | solution.py:26
  412.3 19.4 %collective-permute-start.25 = (bf16[512,1536]{1,0:T(8,128)(2,1)S(1)}, bf16[512,1536]{1,0:T(8,128)(2,1)S(1)}, u32[]{:S(2)}, u32[]{:S(2)}) collective-permute-start(bf16[512,1536]{1,0:T(8,128)(2,1)S(1)} %convolution_convert_fusion.4), channel_id=1, source_target_pairs={{0,2},{2,0},{4,6},{6,4},{8,10},{10,8},{12,14},{14,12},{16,18},{18,... | collective-permute-start | bytes 4718600 | tf_op jit(solution)/shard_map/ppermute | solution.py:26
  414.3 5.0 collective-permute-start.35
  419.4 5.8 collective-permute-start.36
  425.2 48.6 %collective-permute-start.17 = (bf16[1024,1024]{1,0:T(8,128)(2,1)S(1)}, bf16[1024,1024]{1,0:T(8,128)(2,1)S(1)}, u32[]{:S(2)}, u32[]{:S(2)}) collective-permute-start(bf16[1024,1024]{1,0:T(8,128)(2,1)S(1)} %copy-done.25), channel_id=1, source_target_pairs={{0,1},{1,0},{2,3},{3,2},{4,5},{5,4},{6,7},{7,6},{8,9},{9,8},{10,11... | collective-permute-start | bytes 6291464 | tf_op jit(solution)/shard_map/ppermute | solution.py:26
  427.5 54.9 %collective-permute-start.24 = (bf16[512,1536]{1,0:T(8,128)(2,1)}, bf16[512,1536]{1,0:T(8,128)(2,1)S(1)}, u32[]{:S(2)}, u32[]{:S(2)}) collective-permute-start(bf16[512,1536]{1,0:T(8,128)(2,1)} %convolution_convert_fusion.5), channel_id=1, source_target_pairs={{0,2},{2,0},{4,6},{6,4},{8,10},{10,8},{12,14},{14,12},{16,18},{18,... | collective-permute-start | bytes 4718600 | tf_op jit(solution)/shard_map/ppermute | solution.py:26
  431.7 119.7 %collective-permute-start.18 = (bf16[1024,1024]{1,0:T(8,128)(2,1)S(1)}, bf16[1024,1024]{1,0:T(8,128)(2,1)S(1)}, u32[]{:S(2)}, u32[]{:S(2)}) collective-permute-start(bf16[1024,1024]{1,0:T(8,128)(2,1)S(1)} %fusion.16), channel_id=1, source_target_pairs={{0,1},{1,0},{2,3},{3,2},{4,5},{5,4},{6,7},{7,6},{8,9},{9,8},{10,11... | collective-permute-start | bytes 6291464 | tf_op jit(solution)/shard_map/ppermute | solution.py:26
  436.8 36.9 %copy-start.44 = (bf16[512,2048]{1,0:T(8,128)(2,1)S(1)}, bf16[512,2048]{1,0:T(8,128)(2,1)}, u32[]{:S(2)}) copy-start(bf16[512,2048]{1,0:T(8,128)(2,1)} %convolution_convert_fusion.3) | copy-start | bytes 6291460
  436.8 112.6 %collective-permute-start.26 = (bf16[512,1536]{1,0:T(8,128)(2,1)}, bf16[512,1536]{1,0:T(8,128)(2,1)S(1)}, u32[]{:S(2)}, u32[]{:S(2)}) collective-permute-start(bf16[512,1536]{1,0:T(8,128)(2,1)} %add_convert_fusion.5), channel_id=1, source_target_pairs={{0,1},{1,0},{2,3},{3,2},{4,5},{5,4},{6,7},{7,6},{8,9},{9,8},{10,11... | collective-permute-start | bytes 4718600 | tf_op jit(solution)/shard_map/ppermute | solution.py:26
  473.8 90.1 %collective-permute-start.37 = (bf16[512,2048]{1,0:T(8,128)(2,1)S(1)}, bf16[512,2048]{1,0:T(8,128)(2,1)S(1)}, u32[]{:S(2)}, u32[]{:S(2)}) collective-permute-start(bf16[512,2048]{1,0:T(8,128)(2,1)S(1)} %copy-done.44), channel_id=1, source_target_pairs={{0,2},{2,0},{4,6},{6,4},{8,10},{10,8},{12,14},{14,12},{16,18},{18,... | collective-permute-start | bytes 6291464 | tf_op jit(solution)/shard_map/ppermute | solution.py:26
  476.3 74.4 %copy-start.24 = (f32[512,1536]{1,0:T(8,128)S(1)}, f32[512,1536]{1,0:T(8,128)}, u32[]{:S(2)}) copy-start(f32[512,1536]{1,0:T(8,128)} %fusion.94) | copy-start | bytes 9437188
  476.3 123.8 %collective-permute-start.44 = (bf16[256,2048]{1,0:T(8,128)(2,1)S(1)}, bf16[256,2048]{1,0:T(8,128)(2,1)S(1)}, u32[]{:S(2)}, u32[]{:S(2)}) collective-permute-start(bf16[256,2048]{1,0:T(8,128)(2,1)S(1)} %slice.365), channel_id=1, source_target_pairs={{0,4},{2,6},{4,0},{6,2},{8,12},{10,14},{12,8},{14,10},{16,20},{18,... | collective-permute-start | bytes 3145736 | tf_op jit(solution)/shard_map/ppermute | solution.py:26
  482.4 73.9 %collective-permute-start.46 = (bf16[256,2048]{1,0:T(8,128)(2,1)S(1)}, bf16[256,2048]{1,0:T(8,128)(2,1)S(1)}, u32[]{:S(2)}, u32[]{:S(2)}) collective-permute-start(bf16[256,2048]{1,0:T(8,128)(2,1)S(1)} %slice.364), channel_id=1, source_target_pairs={{0,4},{2,6},{4,0},{6,2},{8,12},{10,14},{12,8},{14,10},{16,20},{18,... | collective-permute-start | bytes 3145736 | tf_op jit(solution)/shard_map/ppermute | solution.py:26
  549.5 48.8 %collective-permute-start.39 = (bf16[512,2048]{1,0:T(8,128)(2,1)}, bf16[512,2048]{1,0:T(8,128)(2,1)S(1)}, u32[]{:S(2)}, u32[]{:S(2)}) collective-permute-start(bf16[512,2048]{1,0:T(8,128)(2,1)} %add_convert_fusion.2), channel_id=1, source_target_pairs={{0,1},{1,0},{2,3},{3,2},{4,5},{5,4},{6,7},{7,6},{8,9},{9,8},{10,11... | collective-permute-start | bytes 6291464 | tf_op jit(solution)/shard_map/ppermute | solution.py:26
  551.4 12.1 %collective-permute-start.27 = (bf16[256,1536]{1,0:T(8,128)(2,1)S(1)}, bf16[256,1536]{1,0:T(8,128)(2,1)S(1)}, u32[]{:S(2)}, u32[]{:S(2)}) collective-permute-start(bf16[256,1536]{1,0:T(8,128)(2,1)S(1)} %slice.367), channel_id=1, source_target_pairs={{0,4},{2,6},{4,0},{6,2},{8,12},{10,14},{12,8},{14,10},{16,20},{18,... | collective-permute-start | bytes 2359304 | tf_op jit(solution)/shard_map/ppermute | solution.py:26
  556.3 41.9 %copy-start.15 = (f32[512,2048]{1,0:T(8,128)S(1)}, f32[512,2048]{1,0:T(8,128)}, u32[]{:S(2)}) copy-start(f32[512,2048]{1,0:T(8,128)} %fusion.112) | copy-start | bytes 12582916
  556.6 58.5 %collective-permute-start.47 = (bf16[256,2048]{1,0:T(8,128)(2,1)S(1)}, bf16[256,2048]{1,0:T(8,128)(2,1)S(1)}, u32[]{:S(2)}, u32[]{:S(2)}) collective-permute-start(bf16[256,2048]{1,0:T(8,128)(2,1)S(1)} %fusion.46), channel_id=1, source_target_pairs={{0,1},{1,0},{2,3},{3,2},{4,5},{5,4},{6,7},{7,6},{8,9},{9,8},{10,11... | collective-permute-start | bytes 3145736 | tf_op jit(solution)/shard_map/ppermute | solution.py:26
  563.7 52.8 %collective-permute-start.28 = (bf16[128,1536]{1,0:T(8,128)(2,1)S(1)}, bf16[128,1536]{1,0:T(8,128)(2,1)S(1)}, u32[]{:S(2)}, u32[]{:S(2)}) collective-permute-start(bf16[128,1536]{1,0:T(8,128)(2,1)S(1)} %slice.370), channel_id=1, source_target_pairs={{0,8},{2,10},{4,12},{6,14},{8,0},{10,2},{12,4},{14,6},{16,24},{18,... | collective-permute-start | bytes 1179656 | tf_op jit(solution)/shard_map/ppermute | solution.py:26
  599.6 17.5 %collective-permute-start.40 = (bf16[256,2048]{1,0:T(8,128)(2,1)S(1)}, bf16[256,2048]{1,0:T(8,128)(2,1)S(1)}, u32[]{:S(2)}, u32[]{:S(2)}) collective-permute-start(bf16[256,2048]{1,0:T(8,128)(2,1)S(1)} %slice.366), channel_id=1, source_target_pairs={{0,4},{2,6},{4,0},{6,2},{8,12},{10,14},{12,8},{14,10},{16,20},{18,... | collective-permute-start | bytes 3145736 | tf_op jit(solution)/shard_map/ppermute | solution.py:26
  616.4 20.1 %collective-permute-start.48 = (bf16[128,2048]{1,0:T(8,128)(2,1)}, bf16[128,2048]{1,0:T(8,128)(2,1)}, u32[]{:S(2)}, u32[]{:S(2)}) collective-permute-start(bf16[128,2048]{1,0:T(8,128)(2,1)} %slice.368), channel_id=1, source_target_pairs={{0,8},{2,10},{4,12},{6,14},{8,0},{10,2},{12,4},{14,6},{16,24},{18,... | collective-permute-start | bytes 1572872 | tf_op jit(solution)/shard_map/ppermute | solution.py:26
  616.6 16.7 %collective-permute-start.29 = (bf16[64,1536]{1,0:T(8,128)(2,1)S(1)}, bf16[64,1536]{1,0:T(8,128)(2,1)S(1)}, u32[]{:S(2)}, u32[]{:S(2)}) collective-permute-start(bf16[64,1536]{1,0:T(8,128)(2,1)S(1)} %slice.375), channel_id=1, source_target_pairs={{0,16},{2,18},{4,20},{6,22},{8,24},{10,26},{12,28},{14,30},{16,0},... | collective-permute-start | bytes 589832 | tf_op jit(solution)/shard_map/ppermute | solution.py:26
  619.6 24.2 %collective-permute-start.41 = (bf16[128,2048]{1,0:T(8,128)(2,1)}, bf16[128,2048]{1,0:T(8,128)(2,1)}, u32[]{:S(2)}, u32[]{:S(2)}) collective-permute-start(bf16[128,2048]{1,0:T(8,128)(2,1)} %slice.369), channel_id=1, source_target_pairs={{0,8},{2,10},{4,12},{6,14},{8,0},{10,2},{12,4},{14,6},{16,24},{18,... | collective-permute-start | bytes 1572872 | tf_op jit(solution)/shard_map/ppermute | solution.py:26
  637.7 18.5 %collective-permute-start.49 = (bf16[64,2048]{1,0:T(8,128)(2,1)S(1)}, bf16[64,2048]{1,0:T(8,128)(2,1)S(1)}, u32[]{:S(2)}, u32[]{:S(2)}) collective-permute-start(bf16[64,2048]{1,0:T(8,128)(2,1)S(1)} %slice.371), channel_id=1, source_target_pairs={{0,16},{2,18},{4,20},{6,22},{8,24},{10,26},{12,28},{14,30},{16,0},... | collective-permute-start | bytes 786440 | tf_op jit(solution)/shard_map/ppermute | solution.py:26
  645.0 14.5 %collective-permute-start.42 = (bf16[64,2048]{1,0:T(8,128)(2,1)S(1)}, bf16[64,2048]{1,0:T(8,128)(2,1)S(1)}, u32[]{:S(2)}, u32[]{:S(2)}) collective-permute-start(bf16[64,2048]{1,0:T(8,128)(2,1)S(1)} %slice.372), channel_id=1, source_target_pairs={{0,16},{2,18},{4,20},{6,22},{8,24},{10,26},{12,28},{14,30},{16,0},... | collective-permute-start | bytes 786440 | tf_op jit(solution)/shard_map/ppermute | solution.py:26
  (47 other events, 294.7 us)

commit v2 on v1

v2 whole, which is shorter than its diff:
```python
import functools
import math

import jax
import jax.numpy as jnp
from jax import lax
from jax.experimental import pallas as pl
from jax.experimental.pallas import tpu as pltpu
from jax.sharding import PartitionSpec as P
import numpy as np

HD = 128
NS = 16
BLK = 512
CTX = 128
CH = 128
TILE = 256
EPS = 1e-05
F32 = jnp.float32
BF16 = jnp.bfloat16
HIGHEST = lax.Precision.HIGHEST
SCALE = HD**-0.5
LOG2 = SCALE * math.log2(math.e)


def swap(value, axis, mask, count):
    return lax.ppermute(value, axis, [(i, i ^ mask) for i in range(count)])


def tie(value, *deps):
    return lax.optimization_barrier((value, *deps))[0] if deps else value


def mm(left, right):
    return lax.dot_general(left, right, (((1,), (0,)), ((), ())), preferred_element_type=F32)


def mm_nt(left, right):
    return lax.dot_general(left, right, (((1,), (1,)), ((), ())), preferred_element_type=F32)


def mm_tn(left, right):
    return lax.dot_general(left, right, (((0,), (0,)), ((), ())), preferred_element_type=F32)


def decay_constants():
    rates = 4.0 / CH * np.exp2(-8.0 * np.arange(NS, dtype=np.float64) / (NS - 1))
    return rates, np.sqrt(-np.expm1(-2.0 * rates))


RATES, NORMS = decay_constants()


def decay_within(n, transposed):
    rows = lax.broadcasted_iota(jnp.int32, (CH, CH), 0)
    columns = lax.broadcasted_iota(jnp.int32, (CH, CH), 1)
    offset = columns - rows if transposed else rows - columns
    powers = jnp.exp(offset.astype(F32) * -float(RATES[n]))
    return jnp.where(offset >= 0, float(NORMS[n]) * powers, 0.0).astype(BF16)


def decay_vectors(rates, norms):
    steps = lax.broadcasted_iota(jnp.int32, (NS, CH), 1).astype(F32)
    carry_in = jnp.exp(-rates * (steps + 1.0))
    carry_out = (norms * jnp.exp(-rates * (CH - 1.0 - steps))).astype(BF16)
    return carry_in, carry_out, jnp.exp(-rates * CH)


def ssm_forward_kernel(v_ref, rates_ref, norms_ref, coef_ref, skip_ref, out_ref, state_ref, within_ref):
    @pl.when(pl.program_id(0) == 0)
    def _():
        for n in range(NS):
            within_ref[n] = decay_within(n, False)

    carry_in, carry_out, whole = decay_vectors(rates_ref[...], norms_ref[...])
    before = BLK // CH - 1
    state = jnp.zeros(state_ref.shape, F32)
    for k in range(before):
        state = whole * state + mm(carry_out, v_ref[k * CH : (k + 1) * CH, :])
    state_ref[...] = state
    rows = v_ref[before * CH :, :]
    total = skip_ref[...] * rows.astype(F32)
    total += lax.dot_general(
        carry_in, coef_ref[...] * state, (((0,), (0,)), ((), ())), precision=HIGHEST, preferred_element_type=F32
    )
    for n in range(NS):
        total += coef_ref[n : n + 1, :] * mm(within_ref[n], rows)
    out_ref[...] = total.astype(BF16)


def decay_arrays():
    return jnp.asarray(RATES[:, None], F32), jnp.asarray(NORMS[:, None], F32)


def ssm_forward(rows, coef, skip):
    width = rows.shape[1]
    step = 256
    column = lambda c: (0, c)
    fixed = pl.BlockSpec((NS, 1), lambda c: (0, 0))
    return pl.pallas_call(
        ssm_forward_kernel,
        grid=(width // step,),
        in_specs=[
            pl.BlockSpec((BLK, step), column),
            fixed,
            fixed,
            pl.BlockSpec((NS, step), column),
            pl.BlockSpec((1, step), column),
        ],
        out_specs=[pl.BlockSpec((CH, step), column), pl.BlockSpec((NS, step), column)],
        out_shape=[jax.ShapeDtypeStruct((CH, width), BF16), jax.ShapeDtypeStruct((NS, width), F32)],
        scratch_shapes=[pltpu.VMEM((NS, CH, CH), BF16)],
        cost_estimate=brief(),
        name="ssm_forward",
    )(rows, *decay_arrays(), coef, skip)


def ssm_backward_kernel(v_ref, grad_ref, rates_ref, norms_ref, coef_ref, skip_ref, state_ref, du_ref, small_ref, within_ref):
    @pl.when(pl.program_id(0) == 0)
    def _():
        for n in range(NS):
            within_ref[n] = decay_within(n, True)

    carry_in, carry_out, whole = decay_vectors(rates_ref[...], norms_ref[...])
    before = BLK // CH - 1
    rows = v_ref[...].astype(F32)
    grad = grad_ref[...].astype(BF16)
    wide = grad.astype(F32)
    du = skip_ref[...] * wide
    reach = jnp.dot(carry_in, wide, precision=HIGHEST, preferred_element_type=F32)
    for n in range(NS):
        back = mm(within_ref[n], grad)
        du += coef_ref[n : n + 1, :] * back
        small_ref[n : n + 1, :] = (
            jnp.sum(rows * back, axis=0, keepdims=True) + state_ref[n : n + 1, :] * reach[n : n + 1, :]
        )
    small_ref[NS : NS + 1, :] = jnp.sum(rows * wide, axis=0, keepdims=True)
    du_ref[before * CH :, :] = du
    state = coef_ref[...] * reach
    for k in reversed(range(before)):
        du_ref[k * CH : (k + 1) * CH, :] = lax.dot_general(
            carry_out.astype(F32), state, (((0,), (0,)), ((), ())), precision=HIGHEST, preferred_element_type=F32
        )
        state = whole * state


def ssm_backward(rows, grad, coef, skip, state):
    width = rows.shape[1]
    step = 256
    column = lambda c: (0, c)
    fixed = pl.BlockSpec((NS, 1), lambda c: (0, 0))
    return pl.pallas_call(
        ssm_backward_kernel,
        grid=(width // step,),
        in_specs=[
            pl.BlockSpec((CH, step), lambda c: (BLK // CH - 1, c)),
            pl.BlockSpec((CH, step), column),
            fixed,
            fixed,
            pl.BlockSpec((NS, step), column),
            pl.BlockSpec((1, step), column),
            pl.BlockSpec((NS, step), column),
        ],
        out_specs=[pl.BlockSpec((BLK, step), column), pl.BlockSpec((NS + 1, step), column)],
        out_shape=[jax.ShapeDtypeStruct((BLK, width), F32), jax.ShapeDtypeStruct((NS + 1, width), F32)],
        scratch_shapes=[pltpu.VMEM((NS, CH, CH), BF16)],
        cost_estimate=brief(),
        name="ssm_backward",
    )(rows, grad, *decay_arrays(), coef, skip, state)


def key_parts(block, tile, k_ref, v_ref, ck_ref, cv_ref):
    parts = []
    if block > 0:
        parts.append((None, ck_ref[0], cv_ref[0], False))
    for piece in range(tile + 1):
        where = slice(block * BLK + piece * TILE, block * BLK + (piece + 1) * TILE)
        parts.append((piece, k_ref[0, where, :], v_ref[0, where, :], piece == tile))
    return parts


def tile_scores(keys, query, masked):
    scores = mm_nt(keys, query)
    if masked:
        key_ids = lax.broadcasted_iota(jnp.int32, scores.shape, 0)
        query_ids = lax.broadcasted_iota(jnp.int32, scores.shape, 1)
        scores = jnp.where(key_ids <= query_ids, scores, -1e30)
    return scores


def attend_forward_kernel(q_ref, k_ref, v_ref, ck_ref, cv_ref, out_ref, lse_ref):
    for block in range(2):
        for tile in range(BLK // TILE):
            base = block * BLK + tile * TILE
            query = q_ref[0, base : base + TILE, :]
            parts = key_parts(block, tile, k_ref, v_ref, ck_ref, cv_ref)
            scores = [tile_scores(keys, query, masked) for _, keys, _, masked in parts]
            top = functools.reduce(jnp.maximum, [jnp.max(s, axis=0, keepdims=True) for s in scores]) * LOG2
            exps = [jnp.exp2(s * LOG2 - top) for s in scores]
            total = functools.reduce(jnp.add, [jnp.sum(e, axis=0, keepdims=True) for e in exps])
            inverse = 1.0 / total
            out = functools.reduce(
                jnp.add,
                [mm_tn(values, (e * inverse).astype(BF16)) for (_, _, values, _), e in zip(parts, exps)],
            )
            out_ref[base : base + TILE, :] = out.T.astype(BF16)
            lse_ref[0, :, base : base + TILE] = top + jnp.log2(total)


def attend_forward(qkv, ckv):
    length, width = qkv.shape[1], qkv.shape[2]
    heads = width // HD
    pick = lambda s: pl.BlockSpec((1, length, HD), lambda h: (s, 0, h))
    pick_context = lambda s: pl.BlockSpec((1, CTX, HD), lambda h: (s, 0, h))
    return pl.pallas_call(
        attend_forward_kernel,
        grid=(heads,),
        in_specs=[pick(0), pick(1), pick(2), pick_context(0), pick_context(1)],
        out_specs=[
            pl.BlockSpec((length, HD), lambda h: (0, h)),
            pl.BlockSpec((1, 1, length), lambda h: (h, 0, 0)),
        ],
        out_shape=[
            jax.ShapeDtypeStruct((length, width), BF16),
            jax.ShapeDtypeStruct((heads, 1, length), F32),
        ],
        cost_estimate=brief(),
        name="attend_forward",
    )(qkv, qkv, qkv, ckv, ckv)


def attend_backward_kernel(q_ref, k_ref, v_ref, ck_ref, cv_ref, dout_ref, lse_ref, grad_ref, cgrad_ref):
    for block in range(2):
        grads = {}
        for tile in range(BLK // TILE):
            base = block * BLK + tile * TILE
            query = q_ref[0, base : base + TILE, :]
            dout = dout_ref[base : base + TILE, :]
            lse = lse_ref[0, :, base : base + TILE]
            parts = key_parts(block, tile, k_ref, v_ref, ck_ref, cv_ref)
            probs = [jnp.exp2(tile_scores(keys, query, masked) * LOG2 - lse) for _, keys, _, masked in parts]
            dprobs = [mm_nt(values, dout) for _, _, values, _ in parts]
            inner = functools.reduce(
                jnp.add, [jnp.sum(p * d, axis=0, keepdims=True) for p, d in zip(probs, dprobs)]
            )
            dquery = None
            for (name, keys, _, _), p, d in zip(parts, probs, dprobs):
                dscore = (p * (d - inner)).astype(BF16)
                term = mm_tn(keys, dscore)
                dquery = term if dquery is None else dquery + term
                dkey, dvalue = mm(dscore, query), mm(p.astype(BF16), dout)
                if name in grads:
                    grads[name] = (grads[name][0] + dkey, grads[name][1] + dvalue)
                else:
                    grads[name] = (dkey, dvalue)
            grad_ref[0, base : base + TILE, :] = (dquery.T * SCALE).astype(BF16)
        for name, (dkey, dvalue) in grads.items():
            dkey, dvalue = (dkey * SCALE).astype(BF16), dvalue.astype(BF16)
            if name is None:
                cgrad_ref[0] = dkey
                cgrad_ref[1] = dvalue
            else:
                where = slice(block * BLK + name * TILE, block * BLK + (name + 1) * TILE)
                grad_ref[1, where, :] = dkey
                grad_ref[2, where, :] = dvalue


def attend_backward(qkv, ckv, dheads, lse):
    length, width = qkv.shape[1], qkv.shape[2]
    heads = width // HD
    pick = lambda s: pl.BlockSpec((1, length, HD), lambda h: (s, 0, h))
    pick_context = lambda s: pl.BlockSpec((1, CTX, HD), lambda h: (s, 0, h))
    return pl.pallas_call(
        attend_backward_kernel,
        grid=(heads,),
        in_specs=[
            pick(0),
            pick(1),
            pick(2),
            pick_context(0),
            pick_context(1),
            pl.BlockSpec((length, HD), lambda h: (0, h)),
            pl.BlockSpec((1, 1, length), lambda h: (h, 0, 0)),
        ],
        out_specs=[
            pl.BlockSpec((3, length, HD), lambda h: (0, 0, h)),
            pl.BlockSpec((2, CTX, HD), lambda h: (0, 0, h)),
        ],
        out_shape=[
            jax.ShapeDtypeStruct((3, length, width), BF16),
            jax.ShapeDtypeStruct((2, CTX, width), BF16),
        ],
        cost_estimate=brief(),
        name="attend_backward",
    )(qkv, qkv, qkv, ckv, ckv, dheads, lse)


def brief():
    return pl.CostEstimate(flops=1 << 32, bytes_accessed=1 << 16, transcendentals=0)


def roomy():
    return pltpu.CompilerParams(vmem_limit_bytes=56 << 20)


def halving_order(count):
    bits = count.bit_length() - 1
    return [sum(((p >> (bits - 1 - b)) & 1) << b for b in range(bits)) for p in range(count)]


def place_rows(where_ref, tall_ref, out_ref, count):
    size = tall_ref.shape[0] // count
    for p, code in enumerate(halving_order(count)):
        start = pl.multiple_of((where_ref[1] ^ code) * size, size)
        out_ref[p * size : (p + 1) * size, :] = tall_ref[pl.ds(start, size), :]


def whole_block(shape):
    return pl.BlockSpec(shape, lambda *_: (0,) * len(shape), pipeline_mode=pl.Buffered(1))


def normalize(values):
    center = values - jnp.mean(values, axis=-1, keepdims=True)
    rstd = lax.rsqrt(jnp.mean(center * center, axis=-1, keepdims=True) + EPS)
    return center * rstd, rstd


def normalize_backward(grad, hat, rstd, gain):
    dn = grad * gain
    return rstd * (dn - jnp.mean(dn, axis=-1, keepdims=True) - hat * jnp.mean(dn * hat, axis=-1, keepdims=True))


def first_norm(where, layer_in, cotangent, gain, bias, count):
    length, width = layer_in.shape[2:]
    step = 256

    def kernel(where_ref, x_ref, dy_ref, gain_ref, bias_ref, u_ref, ut_ref, dyt_ref, tall):
        hat, _ = normalize(x_ref[0, 0].astype(F32))
        u = (hat * gain_ref[...] + bias_ref[...]).astype(BF16)
        u_ref[...] = u
        tall[...] = u.T
        place_rows(where_ref, tall, ut_ref, count)
        tall[...] = dy_ref[0, 0].T
        place_rows(where_ref, tall, dyt_ref, count)

    mine = lambda i, w: (w[0], 0, i, 0)
    return pl.pallas_call(
        kernel,
        grid_spec=pltpu.PrefetchScalarGridSpec(
            num_scalar_prefetch=1,
            grid=(length // step,),
            in_specs=[
                pl.BlockSpec((1, 1, step, width), mine),
                pl.BlockSpec((1, 1, step, width), mine),
                whole_block((1, width)),
                whole_block((1, width)),
            ],
            out_specs=[
                pl.BlockSpec((step, width), lambda i, w: (i, 0)),
                pl.BlockSpec((width, step), lambda i, w: (0, i)),
                pl.BlockSpec((width, step), lambda i, w: (0, i)),
            ],
            scratch_shapes=[pltpu.VMEM((width, step), BF16)],
        ),
        out_shape=[
            jax.ShapeDtypeStruct((length, width), BF16),
            jax.ShapeDtypeStruct((width, length), BF16),
            jax.ShapeDtypeStruct((width, length), BF16),
        ],
        cost_estimate=brief(),
        name="first_norm",
    )(where, layer_in, cotangent, gain, bias)


def context_rows(where, context, count):
    def kernel(where_ref, c_ref, out_ref, tall):
        tall[...] = c_ref[...].T
        place_rows(where_ref, tall, out_ref, count)

    rows, width = context.shape
    return pl.pallas_call(
        kernel,
        in_specs=[pl.BlockSpec(memory_space=pltpu.SMEM), pl.BlockSpec(memory_space=pltpu.VMEM)],
        out_specs=pl.BlockSpec(memory_space=pltpu.VMEM),
        out_shape=jax.ShapeDtypeStruct((width, rows), BF16),
        scratch_shapes=[pltpu.VMEM((width, rows), BF16)],
        cost_estimate=brief(),
        name="context_rows",
    )(where, context)


def attention_out(where, layer_in, heads_own, heads_other, out_own, out_other, gain, bias, count):
    length, width = layer_in.shape[2:]
    group = heads_own.shape[1]
    step = 256

    def kernel(where_ref, x_ref, ho_ref, ht_ref, wo_ref, wt_ref, gain_ref, bias_ref, x1_ref, u_ref, ut_ref, tall):
        x1 = x_ref[0, 0].astype(F32) + mm(ho_ref[...], wo_ref[...]) + mm(ht_ref[...], wt_ref[...])
        x1_ref[...] = x1
        hat, _ = normalize(x1)
        u = (hat * gain_ref[...] + bias_ref[...]).astype(BF16)
        u_ref[...] = u
        tall[...] = u.T
        place_rows(where_ref, tall, ut_ref, count)

    row = lambda i, w: (i, 0)
    return pl.pallas_call(
        kernel,
        grid_spec=pltpu.PrefetchScalarGridSpec(
            num_scalar_prefetch=1,
            grid=(length // step,),
            in_specs=[
                pl.BlockSpec((1, 1, step, width), lambda i, w: (w[0], 0, i, 0)),
                pl.BlockSpec((step, group), row),
                pl.BlockSpec((step, group), row),
                whole_block((group, width)),
                whole_block((group, width)),
                whole_block((1, width)),
                whole_block((1, width)),
            ],
            out_specs=[
                pl.BlockSpec((step, width), row),
                pl.BlockSpec((step, width), row),
                pl.BlockSpec((width, step), lambda i, w: (0, i)),
            ],
            scratch_shapes=[pltpu.VMEM((width, step), BF16)],
        ),
        out_shape=[
            jax.ShapeDtypeStruct((length, width), F32),
            jax.ShapeDtypeStruct((length, width), BF16),
            jax.ShapeDtypeStruct((width, length), BF16),
        ],
        compiler_params=roomy(),
        cost_estimate=brief(),
        name="attention_out",
    )(where, layer_in, heads_own, heads_other, out_own, out_other, gain, bias)


STEP = 1024


def weight_copies(own_ref, piece_refs, held, sems, axis):
    count = own_ref.shape[axis] // STEP
    size = piece_refs[0].shape[axis]
    per = STEP // size

    def part(ref, start, extent):
        return ref.at[pl.ds(start, extent), :] if axis == 0 else ref.at[:, pl.ds(start, extent)]

    copies = []
    for j in range(count):
        copies.append([pltpu.make_async_copy(part(own_ref, j * STEP, STEP), held.at[j], sems.at[j, 0])])
    for j in range(len(piece_refs) // per):
        copies.append(
            [
                pltpu.make_async_copy(
                    piece_refs[j * per + k], part(held.at[count + j], k * size, size), sems.at[count + j, k]
                )
                for k in range(per)
            ]
        )
    return copies


def stream_weights(copies):
    step = pl.program_id(0)

    @pl.when(step == 0)
    def _():
        for some in copies:
            for copy in some:
                copy.start()

    for j, some in enumerate(copies):

        @pl.when(step == j)
        def _(some=some):
            for copy in some:
                copy.wait()


ANYWHERE = pl.BlockSpec(memory_space=pl.ANY)


def gelu_pair(pre):
    root = math.sqrt(2.0 / math.pi)
    squared = pre * pre
    bend = jnp.tanh(pre * (root + (root * 0.044715) * squared))
    half = 0.5 + 0.5 * bend
    slope = half + pre * ((0.5 - 0.5 * bend * bend) * (root + (3 * 0.044715 * root) * squared))
    return (pre * half).astype(BF16), slope.astype(BF16)


def hidden_forward(u2, up_own, up_pieces):
    length, width = u2.shape
    steps = 2 * up_own.shape[1] // STEP
    chunk = 256

    def kernel(u_ref, own_ref, p0, p1, p2, p3, hid_ref, slope_ref, held, sems):
        stream_weights(weight_copies(own_ref, (p0, p1, p2, p3), held, sems, 1))
        j = pl.program_id(0)
        for i in range(length // chunk):
            rows = slice(i * chunk, (i + 1) * chunk)
            hid, slope = gelu_pair(mm(u_ref[rows, :], held[j]))
            hid_ref[rows, :] = hid
            slope_ref[rows, :] = slope

    tile = pl.BlockSpec((length, STEP), lambda j: (0, j))
    return pl.pallas_call(
        kernel,
        grid=(steps,),
        in_specs=[whole_block((length, width))] + [ANYWHERE] * 5,
        out_specs=[tile, tile],
        out_shape=[jax.ShapeDtypeStruct((length, steps * STEP), BF16)] * 2,
        scratch_shapes=[pltpu.VMEM((steps, width, STEP), BF16), pltpu.SemaphoreType.DMA((steps, 2))],
        compiler_params=roomy(),
        cost_estimate=brief(),
        name="hidden_forward",
    )(u2, up_own, *up_pieces)


def hidden_backward(where, cotangent, down_own, down_pieces, slope):
    length, width = cotangent.shape[2:]
    steps = 2 * down_own.shape[0] // STEP
    chunk = 256

    def kernel(where_ref, dy_ref, own_ref, p0, p1, p2, p3, slope_ref, out_ref, held, sems):
        stream_weights(weight_copies(own_ref, (p0, p1, p2, p3), held, sems, 0))
        j = pl.program_id(0)
        for i in range(length // chunk):
            rows = slice(i * chunk, (i + 1) * chunk)
            out_ref[rows, :] = (mm_nt(dy_ref[0, 0, rows, :], held[j]) * slope_ref[rows, :].astype(F32)).astype(BF16)

    tile = pl.BlockSpec((length, STEP), lambda j, w: (0, j))
    return pl.pallas_call(
        kernel,
        grid_spec=pltpu.PrefetchScalarGridSpec(
            num_scalar_prefetch=1,
            grid=(steps,),
            in_specs=[
                pl.BlockSpec((1, 1, length, width), lambda j, w: (w[0], 0, 0, 0), pipeline_mode=pl.Buffered(1))
            ]
            + [ANYWHERE] * 5
            + [tile],
            out_specs=tile,
            scratch_shapes=[pltpu.VMEM((steps, STEP, width), BF16), pltpu.SemaphoreType.DMA((steps, 2))],
        ),
        out_shape=jax.ShapeDtypeStruct((length, steps * STEP), BF16),
        compiler_params=roomy(),
        cost_estimate=brief(),
        name="hidden_backward",
    )(where, cotangent, down_own, *down_pieces, slope)


def hidden_out(hid, down_own, down_pieces, x1):
    length, width = x1.shape
    steps = 2 * down_own.shape[0] // STEP

    def kernel(hid_ref, own_ref, p0, p1, p2, p3, x1_ref, out_ref, held, total, sems):
        stream_weights(weight_copies(own_ref, (p0, p1, p2, p3), held, sems, 0))
        j = pl.program_id(0)

        @pl.when(j == 0)
        def _():
            total[...] = x1_ref[...]

        total[...] += mm(hid_ref[...], held[j])

        @pl.when(j == steps - 1)
        def _():
            out_ref[...] = total[...].astype(BF16)

    return pl.pallas_call(
        kernel,
        grid=(steps,),
        in_specs=[pl.BlockSpec((length, STEP), lambda j: (0, j))] + [ANYWHERE] * 5 + [whole_block((length, width))],
        out_specs=whole_block((length, width)),
        out_shape=jax.ShapeDtypeStruct((length, width), BF16),
        scratch_shapes=[
            pltpu.VMEM((steps, STEP, width), BF16),
            pltpu.VMEM((length, width), F32),
            pltpu.SemaphoreType.DMA((steps, 2)),
        ],
        compiler_params=roomy(),
        cost_estimate=brief(),
        name="hidden_out",
    )(hid, down_own, *down_pieces, x1)


def second_norm_backward(where, dpre, up_own, up_pieces, x1, cotangent, gain, count):
    length, width = x1.shape
    steps = 2 * up_own.shape[1] // STEP
    chunk = 128

    def kernel(where_ref, dpre_ref, own_ref, p0, p1, p2, p3, x1_ref, dy_ref, gain_ref, out_ref, outt_ref, sums_ref, held, total, tall, sems):
        stream_weights(weight_copies(own_ref, (p0, p1, p2, p3), held, sems, 1))
        j = pl.program_id(0)

        @pl.when(j == 0)
        def _():
            total[...] = mm_nt(dpre_ref[...], held[j])
            sums_ref[...] = jnp.zeros_like(sums_ref)

        @pl.when(j > 0)
        def _():
            total[...] += mm_nt(dpre_ref[...], held[j])

        @pl.when(j == steps - 1)
        def _():
            @pl.loop(0, length // chunk)
            def _(i):
                rows = pl.ds(pl.multiple_of(i * chunk, chunk), chunk)
                du = total[rows, :]
                hat, rstd = normalize(x1_ref[rows, :])
                sums_ref[0:1, :] += jnp.sum(du * hat, axis=0, keepdims=True)
                sums_ref[1:2, :] += jnp.sum(du, axis=0, keepdims=True)
                out = dy_ref[0, 0, rows, :].astype(F32) + normalize_backward(du, hat, rstd, gain_ref[...])
                out = out.astype(BF16)
                out_ref[rows, :] = out
                tall[:, rows] = out.T

            place_rows(where_ref, tall, outt_ref, count)

    mine = pl.BlockSpec((1, 1, length, width), lambda j, w: (w[0], 0, 0, 0), pipeline_mode=pl.Buffered(1))
    return pl.pallas_call(
        kernel,
        grid_spec=pltpu.PrefetchScalarGridSpec(
            num_scalar_prefetch=1,
            grid=(steps,),
            in_specs=[pl.BlockSpec((length, STEP), lambda j, w: (0, j))]
            + [ANYWHERE] * 5
            + [whole_block((length, width)), mine, whole_block((1, width))],
            out_specs=[whole_block((length, width)), whole_block((width, length)), whole_block((2, width))],
            scratch_shapes=[
                pltpu.VMEM((steps, width, STEP), BF16),
                pltpu.VMEM((length, width), F32),
                pltpu.VMEM((width, length), BF16),
                pltpu.SemaphoreType.DMA((steps, 2)),
            ],
        ),
        out_shape=[
            jax.ShapeDtypeStruct((length, width), BF16),
            jax.ShapeDtypeStruct((width, length), BF16),
            jax.ShapeDtypeStruct((2, width), F32),
        ],
        compiler_params=roomy(),
        cost_estimate=brief(),
        name="second_norm_backward",
    )(where, dpre, up_own, *up_pieces, x1, cotangent, gain)


def first_norm_backward(where, dsides, qkv_own, qkv_pieces, du_ssm, layer_in, dattn, gain):
    length, width = layer_in.shape[2:]
    group = qkv_own.shape[2]
    size = qkv_pieces[0].shape[2]
    chunk = 128
    steps = 6

    def kernel(where_ref, do_ref, dt_ref, own_ref, p0, p1, p2, p3, ssm_ref, x_ref, dx_ref, gain_ref, out_ref, sums_ref, held, grads, total, sems):
        copies = []
        for s in range(3):
            copies.append(
                [
                    pltpu.make_async_copy(do_ref.at[s], grads.at[s], sems.at[s, 0]),
                    pltpu.make_async_copy(own_ref.at[s], held.at[s], sems.at[s, 1]),
                ]
            )
        for s in range(3):
            some = [pltpu.make_async_copy(dt_ref.at[s], grads.at[3 + s], sems.at[3 + s, 0])]
            for k, piece in enumerate((p0, p1, p2, p3)):
                some.append(
                    pltpu.make_async_copy(
                        piece.at[s], held.at[3 + s, :, pl.ds(k * size, size)], sems.at[3 + s, 1 + k]
                    )
                )
            copies.append(some)
        stream_weights(copies)
        j = pl.program_id(0)

        @pl.when(j == 0)
        def _():
            total[0 : ssm_ref.shape[0], :] = ssm_ref[...]
            total[ssm_ref.shape[0] :, :] = jnp.zeros((length - ssm_ref.shape[0], width), F32)
            sums_ref[...] = jnp.zeros_like(sums_ref)

        total[...] += mm_nt(grads[j], held[j])

        @pl.when(j == steps - 1)
        def _():
            @pl.loop(0, length // chunk)
            def _(i):
                rows = pl.ds(pl.multiple_of(i * chunk, chunk), chunk)
                du = total[rows, :]
                hat, rstd = normalize(x_ref[0, 0, rows, :].astype(F32))
                sums_ref[0:1, :] += jnp.sum(du * hat, axis=0, keepdims=True)
                sums_ref[1:2, :] += jnp.sum(du, axis=0, keepdims=True)
                out = dx_ref[rows, :].astype(F32) + normalize_backward(du, hat, rstd, gain_ref[...])
                out_ref[rows, :] = out.astype(BF16)

    mine = pl.BlockSpec((1, 1, length, width), lambda j, w: (w[0], 0, 0, 0), pipeline_mode=pl.Buffered(1))
    return pl.pallas_call(
        kernel,
        grid_spec=pltpu.PrefetchScalarGridSpec(
            num_scalar_prefetch=1,
            grid=(steps,),
            in_specs=[ANYWHERE] * 7
            + [whole_block(du_ssm.shape), mine, whole_block((length, width)), whole_block((1, width))],
            out_specs=[whole_block((length, width)), whole_block((2, width))],
            scratch_shapes=[
                pltpu.VMEM((steps, width, group), BF16),
                pltpu.VMEM((steps, length, group), BF16),
                pltpu.VMEM((length, width), F32),
                pltpu.SemaphoreType.DMA((steps, 5)),
            ],
        ),
        out_shape=[jax.ShapeDtypeStruct((length, width), BF16), jax.ShapeDtypeStruct((2, width), F32)],
        compiler_params=roomy(),
        cost_estimate=brief(),
        name="first_norm_backward",
    )(where, dsides[0], dsides[1], qkv_own, *qkv_pieces, du_ssm, layer_in, dattn, gain)


def rows_sent(left, right):
    width, length = left.shape
    half = width // 2
    columns = right.shape[1]

    def kernel(left_ref, right_ref, out_ref):
        out_ref[...] = mm(left_ref[...], right_ref[...]).astype(BF16)

    return pl.pallas_call(
        kernel,
        grid=(columns // STEP,),
        in_specs=[
            pl.BlockSpec((half, length), lambda j: (1, 0), pipeline_mode=pl.Buffered(1)),
            pl.BlockSpec((length, STEP), lambda j: (0, j)),
        ],
        out_specs=pl.BlockSpec((half, STEP), lambda j: (0, j)),
        out_shape=jax.ShapeDtypeStruct((half, columns), BF16),
        compiler_params=roomy(),
        cost_estimate=brief(),
        name="rows_sent",
    )(left, right)


def rows_kept(left, right, got):
    width, length = left.shape
    half = width // 2
    quart = width // 4
    columns = right.shape[1]
    piece = columns // 8
    steps = columns // STEP

    def kernel(left_ref, right_ref, got_ref, keep_ref, send_ref):
        j = pl.program_id(0)
        for part, out_ref in enumerate((keep_ref, send_ref)):
            rows = slice(part * quart, (part + 1) * quart)
            total = mm(left_ref[rows, :], right_ref[...])

            @pl.when(j < steps // 2)
            def _(total=total, out_ref=out_ref, rows=rows):
                out_ref[...] = (total + got_ref[rows, :].astype(F32)).astype(BF16)

            @pl.when(j >= steps // 2)
            def _(total=total, out_ref=out_ref, rows=rows):
                for k in range(STEP // piece):
                    here = slice(k * piece, (k + 1) * piece)
                    there = slice((k ^ 1) * piece, ((k ^ 1) + 1) * piece)
                    out_ref[:, here] = (total[:, here] + got_ref[rows, there].astype(F32)).astype(BF16)

    tile = pl.BlockSpec((quart, STEP), lambda j: (0, j))
    return pl.pallas_call(
        kernel,
        grid=(steps,),
        in_specs=[
            pl.BlockSpec((half, length), lambda j: (0, 0), pipeline_mode=pl.Buffered(1)),
            pl.BlockSpec((length, STEP), lambda j: (0, j)),
            pl.BlockSpec((half, STEP), lambda j: (0, j)),
        ],
        out_specs=[tile, tile],
        out_shape=[jax.ShapeDtypeStruct((quart, columns), BF16)] * 2,
        compiler_params=roomy(),
        cost_estimate=brief(),
        name="rows_kept",
    )(left, right, got)


def group_rows(left, own, other, extra, got):
    width, length = left.shape
    half = width // 2
    quart = width // 4
    count, _, group = own.shape
    piece = group // 4
    keeping = got is not None

    def kernel(*refs):
        refs = list(refs)
        left_ref, sides = refs.pop(0), [refs.pop(0), refs.pop(0)]
        if extra is not None:
            cleft_ref, csides = refs.pop(0), [refs.pop(0), refs.pop(0)]
        got_ref = refs.pop(0) if keeping else None
        j = pl.program_id(0)
        for side in range(2):

            @pl.when((j >= count) if side else (j < count))
            def _(side=side):
                for part in range(2 if keeping else 1):
                    rows = slice(part * quart, (part + 1) * quart) if keeping else slice(0, half)
                    total = mm(left_ref[rows, :], sides[side][0])
                    if extra is not None:
                        term = mm(cleft_ref[rows, :], csides[side][0])
                        total += jnp.where(lax.rem(j, count) > 0, term, 0.0)
                    if not keeping:
                        refs[0][...] = total.astype(BF16)
                        continue
                    for k in range(4):
                        here = slice(k * piece, (k + 1) * piece)
                        come = k ^ side
                        there = slice(come * piece, (come + 1) * piece)
                        refs[part][:, here] = (total[:, here] + got_ref[rows, there].astype(F32)).astype(BF16)

    first = lambda j: jnp.minimum(j, count - 1)
    second = lambda j: jnp.maximum(j - count, 0)
    before = lambda s: jnp.maximum(s - 1, 0)
    pick = 0 if keeping else 1
    in_specs = [
        pl.BlockSpec((half, length), lambda j: (pick, 0), pipeline_mode=pl.Buffered(1)),
        pl.BlockSpec((1, length, group), lambda j: (first(j), 0, 0)),
        pl.BlockSpec((1, length, group), lambda j: (second(j), 0, 0)),
    ]
    operands = [left, own, other]
    if extra is not None:
        rows = extra[0].shape[1]
        in_specs += [
            pl.BlockSpec((half, rows), lambda j: (pick, 0), pipeline_mode=pl.Buffered(1)),
            pl.BlockSpec((1, rows, group), lambda j: (before(first(j)), 0, 0)),
            pl.BlockSpec((1, rows, group), lambda j: (before(second(j)), 0, 0)),
        ]
        operands += list(extra)
    columns = 2 * count * group
    if keeping:
        in_specs.append(pl.BlockSpec((half, group), lambda j: (0, j)))
        operands.append(got)
        out_specs = [pl.BlockSpec((quart, group), lambda j: (0, j))] * 2
        out_shape = [jax.ShapeDtypeStruct((quart, columns), BF16)] * 2
    else:
        out_specs = pl.BlockSpec((half, group), lambda j: (0, j))
        out_shape = jax.ShapeDtypeStruct((half, columns), BF16)
    return pl.pallas_call(
        kernel,
        grid=(2 * count,),
        in_specs=in_specs,
        out_specs=out_specs,
        out_shape=out_shape,
        compiler_params=roomy(),
        cost_estimate=brief(),
        name="group_kept" if keeping else "group_sent",
    )(*operands)


def reorder(values, count, mask):
    piece = values.shape[1] // (4 * count)
    order = [4 * c + (k ^ mask) for c in range(count) for k in range(4)]
    return jnp.concatenate([values[:, i * piece : (i + 1) * piece] for i in order], axis=1)


def shards(
    dp_count,
    layer_in,
    ln1_gain,
    ln1_bias,
    qkv_weight,
    out_weight,
    ssm_coef,
    ssm_skip,
    ln2_gain,
    ln2_bias,
    up_weight,
    down_weight,
    cotangent,
):
    width = layer_in.shape[3]
    group = qkv_weight.shape[2]
    mine = lax.axis_index("tensor")
    place = lax.axis_index("dp")
    where = jnp.stack([mine, place]).astype(jnp.int32)
    bits = dp_count.bit_length() - 1
    rows_each = width // dp_count
    gain1, bias1, gain2, bias2 = ln1_gain[None], ln1_bias[None], ln2_gain[None], ln2_bias[None]

    over_x = lambda v: swap(v, "tensor", 1, 2)
    over = lambda v, bit: swap(v, "dp", 1 << bit, dp_count)

    quarter = place & 3

    def quarter_of(weight, axis):
        size = weight.shape[axis] // 4
        return lax.dynamic_slice_in_dim(weight, quarter * size, size, axis)

    def pieces(first, beside):
        return [first, over(first, 0), beside, over(beside, 0)]

    small = over_x(jnp.concatenate([ssm_coef, ssm_skip[None]], axis=0))
    qkv_first = over_x(quarter_of(qkv_weight, 2))

    def in_order(own, other, axis):
        return jnp.where(
            mine == 0, jnp.concatenate([own, other], axis=axis), jnp.concatenate([other, own], axis=axis)
        )

    coef = in_order(ssm_coef, small[:NS], 1)
    skip = in_order(ssm_skip[None], small[NS:], 1)

    class Halvings:
        def __init__(self, keep, send, count):
            self.columns, self.count, self.bit, self.crossed = keep.shape[1] // 2, count, 2, False
            self.total, self.message = keep.astype(F32), send
            self.got = over(send, 1)

        def step(self, *deps):
            got = tie(self.got, *deps)
            if self.bit == 2:
                other = reorder(got[:, self.columns :], self.count, 2)
                got = jnp.concatenate([got[:, : self.columns], other], axis=1)
            self.total = self.total + got
            if self.bit < bits:
                rows = self.total.shape[0] // 2
                self.message = self.total[rows:].astype(BF16)
                self.total = self.total[:rows]
                self.got = over(self.message, self.bit)
                self.bit += 1
            else:
                self.message = self.total[:, self.columns :].astype(BF16)
                self.got = over_x(self.message)
                self.crossed = True
            return self.message

        def last(self):
            while not self.crossed:
                self.step()
            got = self.got
            for bit in range(2):
                got = jnp.where((place >> bit) & 1 == 1, reorder(got, self.count, 1 << bit), got)
            return self.total[:, : self.columns] + got

    u1, u1_rows, dy_rows = first_norm(where, layer_in, cotangent, gain1, bias1, dp_count)

    def project(rows, weight):
        return jnp.einsum("td,sde->ste", rows, weight, preferred_element_type=F32).astype(BF16)

    out_first = over_x(tie(quarter_of(out_weight, 0), u1))
    up_first = over_x(tie(quarter_of(up_weight, 1), u1))
    qkv_own = project(u1, qkv_weight)
    down_first = over_x(tie(quarter_of(down_weight, 0), qkv_own))
    context, state = ssm_forward(tie(u1, qkv_own), coef, skip)
    qkv_first = tie(qkv_first, context)
    qkv_beside = over(qkv_first, 1)
    context_turned = context_rows(tie(where, context, qkv_first), context, dp_count)
    ckv_own = project(tie(context, context_turned), qkv_weight[1:])
    heads_own, lse_own = attend_forward(qkv_own, ckv_own)
    out_first = tie(out_first, heads_own)
    out_beside = over(out_first, 1)
    qkv_pieces = pieces(qkv_first, tie(qkv_beside, heads_own))
    qkv_other_weight = tie(jnp.concatenate(qkv_pieces, axis=2), heads_own, out_first)
    qkv_other = project(u1, qkv_other_weight)
    up_first = tie(up_first, qkv_other)
    up_beside = over(up_first, 1)
    out_beside = tie(out_beside, qkv_other)
    out_pieces = pieces(out_first, out_beside)
    ckv_other = project(tie(context, up_first, out_beside), qkv_other_weight[1:])
    heads_other, lse_other = attend_forward(qkv_other, ckv_other)
    out_other = jnp.concatenate([tie(piece, heads_other) for piece in out_pieces], axis=0)
    x1, u2, u2_rows = attention_out(
        where, layer_in, heads_own, heads_other, out_weight, out_other, gain2, bias2, dp_count
    )
    up_pieces = pieces(up_first, tie(up_beside, u2))
    down_first = tie(down_first, u2)
    down_beside = over(down_first, 1)
    hid, slope = hidden_forward(tie(u2, down_first), up_weight, up_pieces)

    down_part = rows_sent(dy_rows, hid)
    down_got = over(down_part, 0)
    down_pieces = pieces(down_first, tie(down_beside, down_part))
    dpre = hidden_backward(tie(where, down_part), cotangent, down_weight, down_pieces, slope)
    down_keep, down_send = rows_kept(tie(dy_rows, dpre), hid, tie(down_got, dpre))
    down = Halvings(down_keep, down_send, 1)
    up_part = rows_sent(tie(u2_rows, down_keep), dpre)
    up_got = over(up_part, 0)
    dattn, dattn_rows, sums2 = second_norm_backward(
        tie(where, up_part), dpre, up_weight, up_pieces, x1, cotangent, gain2, dp_count
    )
    up_keep, up_send = rows_kept(tie(u2_rows, dattn), dpre, tie(up_got, dattn))
    up = Halvings(up_keep, up_send, 1)
    message = down.step(up_keep)
    layer_out = hidden_out(hid, down_weight, down_pieces, tie(x1, up_keep, message))
    layer_out_other = over_x(layer_out)

    out_part = group_rows(tie(dattn_rows, layer_out), heads_own[None], heads_other[None], None, None)
    out_got = over(out_part, 0)
    dattn_then = tie(dattn, out_part)
    dheads_other = mm_nt(dattn_then, out_other).astype(BF16)
    dheads_own = mm_nt(dattn_then, out_weight).astype(BF16)
    message = down.step(dheads_own, dheads_other)
    dqkv_other, dckv_other = attend_backward(
        qkv_other, ckv_other, tie(dheads_other, dheads_own, message), lse_other
    )
    out_keep, out_send = group_rows(
        tie(dattn_rows, dqkv_other), heads_own[None], heads_other[None], None, tie(out_got, dqkv_other)
    )
    out = Halvings(out_keep, out_send, 1)
    dqkv_own, dckv_own = attend_backward(qkv_own, ckv_own, tie(dheads_own, out_keep), lse_own)

    extra = (context_turned, dckv_own, dckv_other)
    message_up, message_down = up.step(dqkv_own), down.step(dqkv_own)
    qkv_part = group_rows(tie(u1_rows, message_up, message_down), dqkv_own, dqkv_other, extra, None)
    qkv_got = over(qkv_part, 0)
    message = out.step(qkv_part)
    dckv_then = tie(dckv_own, qkv_part, message)
    dcontext = jnp.einsum("sce,sde->cd", dckv_then, qkv_weight[1:], preferred_element_type=F32)
    dcontext += jnp.einsum("sce,sde->cd", dckv_other, qkv_other_weight[1:], preferred_element_type=F32)
    du_ssm, small_ssm = ssm_backward(u1, dcontext, coef, skip, state)
    message = out.step(du_ssm)
    qkv_keep, qkv_send = group_rows(
        tie(u1_rows, du_ssm, message), dqkv_own, dqkv_other, extra, tie(qkv_got, du_ssm)
    )
    qkv = Halvings(qkv_keep, qkv_send, 3)
    message_up, message_out = up.step(qkv_keep), out.step(qkv_keep)
    layer_out_other, down.got = tie(layer_out_other, qkv_keep), tie(down.got, qkv_keep)
    grad_in, sums1 = first_norm_backward(
        tie(where, qkv_keep, message_up, message_out, layer_out_other, down.got),
        (dqkv_own, dqkv_other),
        qkv_weight,
        qkv_pieces,
        du_ssm,
        layer_in,
        dattn,
        gain1,
    )
    grad_in_other = over_x(grad_in)
    up.step(grad_in)

    small_all = jnp.concatenate([small_ssm, sums2, sums1], axis=0)
    small_all = small_all + over_x(small_all)
    for bit in range(bits):
        small_all = small_all + over(small_all, bit)
    here = lax.dynamic_slice_in_dim(small_all[: NS + 1], mine * group, group, 1)
    grad_down, grad_up, grad_out, grad_qkv = down.last(), up.last(), out.last(), qkv.last()

    def both_parts(own, other):
        return jnp.where(mine == 0, jnp.stack([own, other]), jnp.stack([other, own]))[:, None]

    return (
        both_parts(layer_out, layer_out_other),
        both_parts(grad_in, grad_in_other).astype(F32),
        small_all[NS + 3],
        small_all[NS + 4],
        grad_qkv.reshape(rows_each, 3, group).swapaxes(0, 1),
        grad_out.T,
        here[:NS],
        here[NS],
        small_all[NS + 1],
        small_all[NS + 2],
        grad_up,
        grad_down.T,
    )


def solution(mesh):
    in_specs = (
        P(None, "dp", None, None),
        P(),
        P(),
        P(None, None, "tensor"),
        P("tensor", None),
        P(None, "tensor"),
        P("tensor"),
        P(),
        P(),
        P(None, "tensor"),
        P("tensor", None),
        P(None, "dp", None, None),
    )
    out_specs = (
        P(None, "dp", None, None),
        P(None, "dp", None, None),
        P(),
        P(),
        P(None, "dp", "tensor"),
        P("tensor", "dp"),
        P(None, "tensor"),
        P("tensor"),
        P(),
        P(),
        P("dp", "tensor"),
        P("tensor", "dp"),
    )
    body = functools.partial(shards, mesh.shape["dp"])
    return jax.shard_map(body, mesh=mesh, in_specs=in_specs, out_specs=out_specs, check_vma=False)
```

time: 671 us -> 542 us (0.81)
  matrix products: 209 us -> 23.3 us
  Pallas kernels: 48.7 us -> 229 us
  waiting for transfers between devices: 250 us -> 181 us
  local copies, waits for them, and re-layouts: 67.4 us -> 31.5 us
  other arithmetic: 45.3 us -> 25.2 us
    pallas_call x0 -> x16, Pallas kernels: none -> 181 us  [the longest x4 27.6 us: group_rows(): pl.pallas_call(kernel, grid=(2 * count,), in_specs=in_specs, out_specs=ou...]
    dot_general x30 -> x2, matrix products: 148 us -> 3.36 us  [the longest x1 1.76 us: shards(): jnp.einsum('sce,sde->cd', dckv_then, qkv_weight[1:], preferred_element_ty...]
    ppermute x50 -> x44, waiting for transfers between devices: 250 us -> 181 us  [swap(): return lax.ppermute(value, axis, [(i, i ^ mask) for i in range(count)])]
    dot_general x6 -> x2, matrix products: 48.9 us -> 6.39 us  [mm_nt(): lax.dot_general(left, right, (((1,), (1,)), ((), ())), preferred_element_...]
    dynamic_update_slice x16 -> x0, local copies, waits for them, and re-layouts: 15.2 us -> none  [fetch(): lax.dynamic_update_slice_in_dim(whole, piece, (quarter ^ mask) * size, 0)]
    transpose x2 -> x0, local copies, waits for them, and re-layouts: 11.6 us -> none  [shards(): sides_tall.append(stacked.swapaxes(0, 1).reshape(stacked.shape[1], -1))]
    convert_element_type x6 -> x0, other arithmetic: 9.15 us -> none  [the longest x1 5.63 us: decay_tables(): jnp.where(offsets[None] >= 0.0, norm[:, None, None] * powers, 0.0)]
    slice x15 -> x24, local copies, waits for them, and re-layouts: 2.57 us -> 9.67 us  [the longest x8 3.99 us: step(): self.message = self.total[rows:].astype(BF16)]
  transfers between devices with their start and end apart: 50 -> 44, of which waited for: 17 -> 21; matrix products, arithmetic and copies ran while one was open for 46% -> 12% of each run, Pallas kernels for 7% -> 32%
where the time goes in v2:
time: 542 us; the launch traced here: 533 us
  Pallas kernels  229 us (42%)
  waiting for transfers between devices  181 us (33%)
  starting transfers between devices  40.5 us (7%)
  local copies, waits for them, and re-layouts  31.5 us (6%)
  other arithmetic  25.2 us (5%)
  matrix products  23.3 us (4%)
    ppermute x44, waiting for transfers between devices, swap(): return lax.ppermute(value, axis, [(i, i ^ mask) for i in range(count)])  181 us
    ppermute x44, starting transfers between devices, swap(): return lax.ppermute(value, axis, [(i, i ^ mask) for i in range(count)])  40.5 us
    pallas_call x4, Pallas kernels, group_rows(): pl.pallas_call(kernel, grid=(2 * count,), in_specs=in_specs, out_specs=ou...  27.6 us
    pallas_call x1, Pallas kernels, hidden_forward(): pl.pallas_call(kernel, grid=(steps,), in_specs=[whole_block((length, widt...  22.9 us
    pallas_call x2, Pallas kernels, rows_kept(): pl.pallas_call(kernel, grid=(steps,), in_specs=[pl.BlockSpec((half, lengt...  22.2 us
    pallas_call x2, Pallas kernels, attend_backward(): pl.pallas_call(attend_backward_kernel, grid=(heads,), in_specs=[pick(0),...  22 us
    pallas_call x1, Pallas kernels, second_norm_backward(): pl.pallas_call(kernel, grid_spec=pltpu.PrefetchScalarGridSpec(num_scalar_...  21.8 us
    pallas_call x1, Pallas kernels, first_norm_backward(): pl.pallas_call(kernel, grid_spec=pltpu.PrefetchScalarGridSpec(num_scalar_...  19 us
  transfers between devices with their start and end apart: 44, of which 21 were waited for; matrix products, arithmetic and copies ran while one was open for 12% of the time, Pallas kernels for 32%

profile of v2, /device:TPU:0, one launch (start us, length us, event | category | flops | bytes accessed | tf_op | source)
XLA Modules:
  0.0 532.9 jit_solution(4180370817579697096)
XLA Ops:
  1.4 2.9 collective-permute-start
  4.4 2.1 constant_dynamic-slice_fusion.4
  7.0 7.2 %first_norm.1 = (bf16[1024,1024]{1,0:T(8,128)(2,1)}, bf16[1024,1024]{1,0:T(8,128)(2,1)}, bf16[1024,1024]{1,0:T(8,128)(2,1)}) custom-call(s32[2]{0:T(128)} %pad_add_fusion.where_ref, bf16[2,1,1024,1024]{3,2,1,0:T(8,128)(2,1)} %x_ref.5, bf16[2,1,1024,1024]{3,2,1,0:T(8,128)(2,1)} %dy_ref.5, f32[1,1024]{1,0:T(1,128)} %bitcast.67, f32[1,1024]{1,0:T(1,128)} %bitcast.74), custom_call_target="tpu_custom_call" | custom-call | flops 4294967296 | bytes 65536 | tf_op jit(solution)/shard_map/first_norm/pallas_call | solution.py:347
  14.3 6.4 %convert_bitcast_fusion.1.q_ref.k_ref.v_ref = bf16[3,1024,512]{2,1,0:T(8,128)(2,1)} fusion(bf16[3,1024,512]{2,1,0:T(8,128)(2,1)S(1)} %copy-done.6, bf16[1024,1024]{1,0:T(8,128)(2,1)} %get-tuple-element.97.v_ref), kind=kOutput, calls=%fused_computation.8 | convolution fusion | flops 3222798336 | bytes 8388608 | tf_op jit(solution)/shard_map/td,sde->ste/dot_general | solution.py:949
  21.9 5.1 ssm_forward.1
  27.1 2.1 collective-permute-start.3
  29.2 1.8 context_rows.1.refs_3_
  32.1 7.8 %attend_forward.2 = (bf16[1024,512]{1,0:T(8,128)(2,1)}, f32[4,1,1024]{2,1,0:T(1,128)}) custom-call(bf16[3,1024,512]{2,1,0:T(8,128)(2,1)} %convert_bitcast_fusion.1.q_ref.k_ref.v_ref, bf16[3,1024,512]{2,1,0:T(8,128)(2,1)} %convert_bitcast_fusion.1.q_ref.k_ref.v_ref, bf16[3,1024,512]{2,1,0:T(8,128)(2,1)} %convert_bitcast_fusion.1.q_ref.k_ref.v_ref, ...), custom_call_target="tpu_custom_call" | custom-call | flops 4294967296 | bytes 65536 | tf_op jit(solution)/shard_map/attend_forward/pallas_call | solution.py:215
  39.9 6.5 %collective-permute-done.3.p2 = bf16[3,1024,128]{2,1,0:T(8,128)(2,1)} collective-permute-done((bf16[3,1024,128]{2,1,0:T(8,128)(2,1)}, bf16[3,1024,128]{2,1,0:T(8,128)(2,1)}, u32[]{:S(2)}, u32[]{:S(2)}) %collective-permute-start.3) | collective-permute-done | bytes 786464 | tf_op jit(solution)/shard_map/ppermute | solution.py:27
  47.5 1.8 collective-permute-start.5
  50.9 2.3 constant_dynamic-slice_fusion.1
  53.2 1.7 collective-permute-start.10
  54.9 1.7 collective-permute-done.5
  56.6 1.7 collective-permute-start.7
  58.4 2.1 pad_maximum_fusion
  60.5 4.8 convert_bitcast_fusion.q_ref.k_ref.v_ref
  65.3 13.9 %collective-permute-done.6.p0 = bf16[1024,512]{1,0:T(8,128)(2,1)} collective-permute-done((bf16[1024,512]{1,0:T(8,128)(2,1)S(1)}, bf16[1024,512]{1,0:T(8,128)(2,1)}, u32[]{:S(2)}, u32[]{:S(2)}) %collective-permute-start.6) | collective-permute-done | bytes 1048608 | tf_op jit(solution)/shard_map/ppermute | solution.py:27
  79.9 1.7 collective-permute-start.12
  82.8 7.8 %attend_forward.3 = (bf16[1024,512]{1,0:T(8,128)(2,1)}, f32[4,1,1024]{2,1,0:T(1,128)}) custom-call(bf16[3,1024,512]{2,1,0:T(8,128)(2,1)} %convert_bitcast_fusion.q_ref.k_ref.v_ref, bf16[3,1024,512]{2,1,0:T(8,128)(2,1)} %convert_bitcast_fusion.q_ref.k_ref.v_ref, bf16[3,1024,512]{2,1,0:T(8,128)(2,1)} %convert_bitcast_fusion.q_ref.k_ref.v_ref, ...), custom_call_target="tpu_custom_call" | custom-call | flops 4294967296 | bytes 65536 | tf_op jit(solution)/shard_map/attend_forward/pallas_call | solution.py:215
  94.2 8.9 %attention_out.1 = (f32[1024,1024]{1,0:T(8,128)}, bf16[1024,1024]{1,0:T(8,128)(2,1)}, bf16[1024,1024]{1,0:T(8,128)(2,1)}) custom-call(s32[2]{0:T(128)} %pad_add_fusion.where_ref, bf16[2,1,1024,1024]{3,2,1,0:T(8,128)(2,1)} %x_ref.5, bf16[1024,512]{1,0:T(8,128)(2,1)} %get-tuple-element.102.ho_ref, bf16[1024,512]{1,0:T(8,128)(2,1)} %get-tuple-element.111.ht_ref, ...), custom_call_target="tpu_custom_call" | custom-call | flops 4294967296 | bytes 65536 | tf_op jit(solution)/shard_map/attention_out/pallas_call | solution.py:407
  104.7 2.8 collective-permute-done.13.p3
  108.5 22.9 %hidden_forward.1 = (bf16[1024,4096]{1,0:T(8,128)(2,1)}, bf16[1024,4096]{1,0:T(8,128)(2,1)}) custom-call(bf16[1024,1024]{1,0:T(8,128)(2,1)} %get-tuple-element.119.u_ref, bf16[1024,2048]{1,0:T(8,128)(2,1)} %own_ref.7, bf16[1024,512]{1,0:T(8,128)(2,1)} %collective-permute-done.6.p0, bf16[1024,512]{1,0:T(8,128)(2,1)} %copy-done.20, ...), custom_call_target="tpu_custom_call" | custom-call | flops 4294967296 | bytes 65536 | tf_op jit(solution)/shard_map/hidden_forward/pallas_call | solution.py:509
  131.3 8.8 %rows_sent.2 = bf16[512,4096]{1,0:T(8,128)(2,1)} custom-call(bf16[1024,1024]{1,0:T(8,128)(2,1)} %get-tuple-element.128.left_ref, bf16[1024,4096]{1,0:T(8,128)(2,1)} %get-tuple-element.121.right_ref.hid_ref), custom_call_target="tpu_custom_call" | custom-call | flops 4294967296 | bytes 65536 | tf_op jit(solution)/shard_map/rows_sent/pallas_call | solution.py:731
  140.3 1.8 collective-permute-start.15
  142.2 23.8 %collective-permute-done.15.p2 = bf16[512,1024]{1,0:T(8,128)(2,1)S(1)} collective-permute-done((bf16[512,1024]{1,0:T(8,128)(2,1)}, bf16[512,1024]{1,0:T(8,128)(2,1)S(1)}, u32[]{:S(2)}, u32[]{:S(2)}) %collective-permute-start.15) | collective-permute-done | bytes 1048608 | tf_op jit(solution)/shard_map/ppermute | solution.py:27
  166.0 2.6 collective-permute-done.16.p3
  169.6 15.7 %hidden_backward.1.right_ref.dpre_ref = bf16[1024,4096]{1,0:T(8,128)(2,1)} custom-call(s32[2]{0:T(128)} %pad_add_fusion.where_ref, bf16[2,1,1024,1024]{3,2,1,0:T(8,128)(2,1)} %dy_ref.5, bf16[2048,1024]{1,0:T(8,128)(2,1)} %own_ref.8, bf16[512,1024]{1,0:T(8,128)(2,1)} %collective-permute-done.10.p0, bf16[512,1024]{1,0:T(8,128)(2,1)} %copy-done.9, ...), custom_call_target="tpu_custom_call" | custom-call | flops 4294967296 | bytes 65536 | tf_op jit(solution)/shard_map/hidden_backward/pallas_call | solution.py:535
  185.3 11.1 %rows_kept.2 = (bf16[256,4096]{1,0:T(8,128)(2,1)}, bf16[256,4096]{1,0:T(8,128)(2,1)}) custom-call(bf16[1024,1024]{1,0:T(8,128)(2,1)} %get-tuple-element.128.left_ref, bf16[1024,4096]{1,0:T(8,128)(2,1)} %get-tuple-element.121.right_ref.hid_ref, bf16[512,4096]{1,0:T(8,128)(2,1)} %collective-permute-done.17.got_ref), custom_call_target="tpu_custom_call" | custom-call | flops 4294967296 | bytes 65536 | tf_op jit(solution)/shard_map/rows_kept/pallas_call | solution.py:772
  196.5 8.9 %rows_sent.3 = bf16[512,4096]{1,0:T(8,128)(2,1)} custom-call(bf16[1024,1024]{1,0:T(8,128)(2,1)} %get-tuple-element.134.left_ref, bf16[1024,4096]{1,0:T(8,128)(2,1)} %hidden_backward.1.right_ref.dpre_ref), custom_call_target="tpu_custom_call" | custom-call | flops 4294967296 | bytes 65536 | tf_op jit(solution)/shard_map/rows_sent/pallas_call | solution.py:731
  205.5 1.7 collective-permute-start.19
  207.3 21.8 %second_norm_backward.1 = (bf16[1024,1024]{1,0:T(8,128)(2,1)}, bf16[1024,1024]{1,0:T(8,128)(2,1)}, f32[2,1024]{1,0:T(2,128)}) custom-call(s32[2]{0:T(128)} %pad_add_fusion.where_ref, bf16[1024,4096]{1,0:T(8,128)(2,1)} %hidden_backward.1.right_ref.dpre_ref, bf16[1024,2048]{1,0:T(8,128)(2,1)} %own_ref.7, bf16[1024,512]{1,0:T(8,128)(2,1)} %collective-permute-done.6.p0, ...), custom_call_target="tpu_custom_call" | custom-call | flops 4294967296 | bytes 65536 | tf_op jit(solution)/shard_map/second_norm_backward/pallas_call | solution.py:625
  229.1 11.0 %rows_kept.3 = (bf16[256,4096]{1,0:T(8,128)(2,1)}, bf16[256,4096]{1,0:T(8,128)(2,1)}) custom-call(bf16[1024,1024]{1,0:T(8,128)(2,1)} %get-tuple-element.134.left_ref, bf16[1024,4096]{1,0:T(8,128)(2,1)} %hidden_backward.1.right_ref.dpre_ref, bf16[512,4096]{1,0:T(8,128)(2,1)} %collective-permute-done.18.got_ref), custom_call_target="tpu_custom_call" | custom-call | flops 4294967296 | bytes 65536 | tf_op jit(solution)/shard_map/rows_kept/pallas_call | solution.py:772
  240.2 13.3 %collective-permute-done.19 = bf16[256,4096]{1,0:T(8,128)(2,1)S(1)} collective-permute-done((bf16[256,4096]{1,0:T(8,128)(2,1)S(1)}, bf16[256,4096]{1,0:T(8,128)(2,1)S(1)}, u32[]{:S(2)}, u32[]{:S(2)}) %collective-permute-start.19) | collective-permute-done | bytes 2097184 | tf_op jit(solution)/shard_map/ppermute | solution.py:27
  256.8 1.8 collective-permute-start.21
  258.6 15.9 %hidden_out.1 = bf16[1024,1024]{1,0:T(8,128)(2,1)} custom-call(bf16[1024,4096]{1,0:T(8,128)(2,1)} %get-tuple-element.121.right_ref.hid_ref, bf16[2048,1024]{1,0:T(8,128)(2,1)} %own_ref.8, bf16[512,1024]{1,0:T(8,128)(2,1)} %collective-permute-done.10.p0, bf16[512,1024]{1,0:T(8,128)(2,1)} %copy-done.9, bf16[512,1024]{1,0:T(8,128)(2,1)} %copy-done.8, ...), custom_call_target="tpu_custom_call" | custom-call | flops 4294967296 | bytes 65536 | tf_op jit(solution)/shard_map/hidden_out/pallas_call | solution.py:573
  274.5 4.2 group_sent.2
  280.3 4.1 convolution_convert_fusion.1.dout_ref
  284.4 2.3 convolution_convert_fusion.dout_ref
  290.3 2.6 collective-permute-start.24
  292.9 11.1 %attend_backward.2 = (bf16[3,1024,512]{2,1,0:T(8,128)(2,1)}, bf16[2,128,512]{2,1,0:T(8,128)(2,1)}) custom-call(bf16[3,1024,512]{2,1,0:T(8,128)(2,1)} %convert_bitcast_fusion.q_ref.k_ref.v_ref, bf16[3,1024,512]{2,1,0:T(8,128)(2,1)} %convert_bitcast_fusion.q_ref.k_ref.v_ref, bf16[3,1024,512]{2,1,0:T(8,128)(2,1)} %convert_bitcast_fusion.q_ref.k_ref.v_ref, ...), custom_call_target="tpu_custom_call" | custom-call | flops 4294967296 | bytes 65536 | tf_op jit(solution)/shard_map/attend_backward/pallas_call | solution.py:273
  304.0 4.3 group_kept.2
  308.3 10.9 %attend_backward.3 = (bf16[3,1024,512]{2,1,0:T(8,128)(2,1)}, bf16[2,128,512]{2,1,0:T(8,128)(2,1)}) custom-call(bf16[3,1024,512]{2,1,0:T(8,128)(2,1)} %convert_bitcast_fusion.1.q_ref.k_ref.v_ref, bf16[3,1024,512]{2,1,0:T(8,128)(2,1)} %convert_bitcast_fusion.1.q_ref.k_ref.v_ref, bf16[3,1024,512]{2,1,0:T(8,128)(2,1)} %convert_bitcast_fusion.1.q_ref.k_ref.v_ref, ...), custom_call_target="tpu_custom_call" | custom-call | flops 4294967296 | bytes 65536 | tf_op jit(solution)/shard_map/attend_backward/pallas_call | solution.py:273
  321.5 5.6 %collective-permute-done.23 = bf16[256,4096]{1,0:T(8,128)(2,1)} collective-permute-done((bf16[256,4096]{1,0:T(8,128)(2,1)}, bf16[256,4096]{1,0:T(8,128)(2,1)}, u32[]{:S(2)}, u32[]{:S(2)}) %collective-permute-start.23) | collective-permute-done | bytes 2097184 | tf_op jit(solution)/shard_map/ppermute | solution.py:27
  330.4 2.0 copy-done
  333.5 9.2 %group_sent.3 = bf16[512,3072]{1,0:T(8,128)(2,1)} custom-call(bf16[1024,1024]{1,0:T(8,128)(2,1)} %get-tuple-element.166.refs_0_, bf16[3,1024,512]{2,1,0:T(8,128)(2,1)} %get-tuple-element.155.refs_1_.do_ref, bf16[3,1024,512]{2,1,0:T(8,128)(2,1)} %get-tuple-element.147.refs_2_.dt_ref, bf16[1024,128]{1,0:T(8,128)(2,1)} %context_rows.1.refs_3_, ...), custom_call_target="tpu_custom_call" | custom-call | flops 4294967296 | bytes 65536 | tf_op jit(solution)/shard_map/group_sent/pallas_call | solution.py:849
  346.3 11.0 %collective-permute-done.25 = bf16[256,1024]{1,0:T(8,128)(2,1)} collective-permute-done((bf16[256,1024]{1,0:T(8,128)(2,1)}, bf16[256,1024]{1,0:T(8,128)(2,1)}, u32[]{:S(2)}, u32[]{:S(2)}) %collective-permute-start.25) | collective-permute-done | bytes 524320 | tf_op jit(solution)/shard_map/ppermute | solution.py:27
  362.5 1.8 collective-permute-start.28
  364.3 1.8 fusion.11
  367.6 5.8 %ssm_backward.1 = (f32[512,1024]{1,0:T(8,128)}, f32[17,1024]{1,0:T(8,128)}) custom-call(bf16[1024,1024]{1,0:T(8,128)(2,1)} %get-tuple-element.97.v_ref, f32[128,1024]{1,0:T(8,128)} %fusion.17.grad_ref, f32[16,1]{1,0:T(8,128)} %constant.26.clone.rates_ref, f32[16,1]{1,0:T(8,128)} %constant.27.clone.norms_ref, f32[16,1024]{1,0:T(8,128)} %maximum_select_fusion.6.coef_ref, ...), custom_call_target="tpu_custom_call" | custom-call | flops 4294967296 | bytes 65536 | tf_op jit(solution)/shard_map/ssm_backward/pallas_call | solution.py:152
  374.5 2.7 collective-permute-start.29
  377.2 9.9 %group_kept.3 = (bf16[256,3072]{1,0:T(8,128)(2,1)}, bf16[256,3072]{1,0:T(8,128)(2,1)}) custom-call(bf16[1024,1024]{1,0:T(8,128)(2,1)} %get-tuple-element.166.refs_0_, bf16[3,1024,512]{2,1,0:T(8,128)(2,1)} %get-tuple-element.155.refs_1_.do_ref, bf16[3,1024,512]{2,1,0:T(8,128)(2,1)} %get-tuple-element.147.refs_2_.dt_ref, ...), custom_call_target="tpu_custom_call" | custom-call | flops 4294967296 | bytes 65536 | tf_op jit(solution)/shard_map/group_kept/pallas_call | solution.py:849
  387.1 8.6 %collective-permute-done.28 = bf16[128,4096]{1,0:T(8,128)(2,1)} collective-permute-done((bf16[128,4096]{1,0:T(8,128)(2,1)}, bf16[128,4096]{1,0:T(8,128)(2,1)}, u32[]{:S(2)}, u32[]{:S(2)}) %collective-permute-start.28) | collective-permute-done | bytes 1048608 | tf_op jit(solution)/shard_map/ppermute | solution.py:27
  399.3 2.6 collective-permute-start.42
  402.0 19.0 %first_norm_backward.1 = (bf16[1024,1024]{1,0:T(8,128)(2,1)}, f32[2,1024]{1,0:T(2,128)}) custom-call(s32[2]{0:T(128)} %pad_add_fusion.where_ref, bf16[3,1024,512]{2,1,0:T(8,128)(2,1)} %get-tuple-element.155.refs_1_.do_ref, bf16[3,1024,512]{2,1,0:T(8,128)(2,1)} %get-tuple-element.147.refs_2_.dt_ref, bf16[3,1024,512]{2,1,0:T(8,128)(2,1)} %own_ref.9, ...), custom_call_target="tpu_custom_call" | custom-call | flops 4294967296 | bytes 65536 | tf_op jit(solution)/shard_map/first_norm_backward/pallas_call | solution.py:701
  425.4 4.5 maximum_select_fusion
  429.9 39.8 %collective-permute-done.32 = f32[21,1024]{1,0:T(8,128)S(1)} collective-permute-done((f32[21,1024]{1,0:T(8,128)S(1)}, f32[21,1024]{1,0:T(8,128)S(1)}, u32[]{:S(2)}, u32[]{:S(2)}) %collective-permute-start.32) | collective-permute-done | bytes 86048 | tf_op jit(solution)/shard_map/ppermute | solution.py:27
  471.7 4.3 collective-permute-done.34
  476.6 4.2 collective-permute-done.35
  481.8 5.4 %collective-permute-done.36 = f32[21,1024]{1,0:T(8,128)S(1)} collective-permute-done((f32[21,1024]{1,0:T(8,128)S(1)}, f32[21,1024]{1,0:T(8,128)S(1)}, u32[]{:S(2)}, u32[]{:S(2)}) %collective-permute-start.36) | collective-permute-done | bytes 86048 | tf_op jit(solution)/shard_map/ppermute | solution.py:27
  491.3 4.4 collective-permute-done.43
  495.8 12.0 %collective-permute-done.38 = bf16[128,3072]{1,0:T(8,128)(2,1)S(1)} collective-permute-done((bf16[128,3072]{1,0:T(8,128)(2,1)S(1)}, bf16[128,3072]{1,0:T(8,128)(2,1)S(1)}, u32[]{:S(2)}, u32[]{:S(2)}) %collective-permute-start.38) | collective-permute-done | bytes 786464 | tf_op jit(solution)/shard_map/ppermute | solution.py:27
  509.0 15.5 %collective-permute-done.39 = bf16[64,3072]{1,0:T(8,128)(2,1)S(1)} collective-permute-done((bf16[64,3072]{1,0:T(8,128)(2,1)S(1)}, bf16[64,3072]{1,0:T(8,128)(2,1)S(1)}, u32[]{:S(2)}, u32[]{:S(2)}) %collective-permute-start.39) | collective-permute-done | bytes 393248 | tf_op jit(solution)/shard_map/ppermute | solution.py:27
  525.1 3.8 fusion
  528.9 2.0 collective-permute-done.40
  (223 shorter events, 61.0 us)
Async XLA Ops:
  1.4 19.3 %collective-permute-start = (f32[17,512]{1,0:T(8,128)S(1)}, f32[17,512]{1,0:T(8,128)S(1)}, u32[]{:S(2)}, u32[]{:S(2)}) collective-permute-start(f32[17,512]{1,0:T(8,128)S(1)} %pad_maximum_fusion.2), channel_id=1, source_target_pairs={{0,1},{1,0},{2,3},{3,2},{4,5},{5,4},{6,7},{7,6},{8,9},{9,8},{10,11... | collective-permute-start | bytes 104456 | tf_op jit(solution)/shard_map/ppermute | solution.py:27
  6.4 20.6 %collective-permute-start.1 = (bf16[3,1024,128]{2,1,0:T(8,128)(2,1)}, bf16[3,1024,128]{2,1,0:T(8,128)(2,1)}, u32[]{:S(2)}, u32[]{:S(2)}) collective-permute-start(bf16[3,1024,128]{2,1,0:T(8,128)(2,1)} %constant_dynamic-slice_fusion.4), channel_id=1, source_target_pairs={{0,1},{1,0},{2,3},{3,2},{4,5},{5,4},{6,7},{7,6},{8,9},{9,8},{10,11... | collective-permute-start | bytes 2359304 | tf_op jit(solution)/shard_map/ppermute | solution.py:27
  7.0 7.2 %copy-start.6 = (bf16[3,1024,512]{2,1,0:T(8,128)(2,1)S(1)}, bf16[3,1024,512]{2,1,0:T(8,128)(2,1)}, u32[]{:S(2)}) copy-start(bf16[3,1024,512]{2,1,0:T(8,128)(2,1)} %own_ref.9) | copy-start | bytes 9437188
  14.3 6.4 %copy-start.30 = (f32[512]{0:T(512)S(1)}, f32[512]{0:T(512)}, u32[]{:S(2)}) copy-start(f32[512]{0:T(512)} %param.22) | copy-start | bytes 6148
  14.3 7.0 %copy-start.25 = (f32[16,512]{1,0:T(8,128)S(1)}, f32[16,512]{1,0:T(8,128)}, u32[]{:S(2)}) copy-start(f32[16,512]{1,0:T(8,128)} %param.21) | copy-start | bytes 98308
  27.1 19.4 %collective-permute-start.3 = (bf16[3,1024,128]{2,1,0:T(8,128)(2,1)}, bf16[3,1024,128]{2,1,0:T(8,128)(2,1)}, u32[]{:S(2)}, u32[]{:S(2)}) collective-permute-start(bf16[3,1024,128]{2,1,0:T(8,128)(2,1)} %collective-permute-done.1.p0), channel_id=1, source_target_pairs={{0,4},{2,6},{4,0},{6,2},{8,12},{10,14},{12,8},{14,10},{16,20},{18,... | collective-permute-start | bytes 2359304 | tf_op jit(solution)/shard_map/ppermute | solution.py:27
  29.2 29.2 %collective-permute-start.2 = (bf16[3,1024,128]{2,1,0:T(8,128)(2,1)}, bf16[3,1024,128]{2,1,0:T(8,128)(2,1)}, u32[]{:S(2)}, u32[]{:S(2)}) collective-permute-start(bf16[3,1024,128]{2,1,0:T(8,128)(2,1)} %collective-permute-done.1.p0), channel_id=1, source_target_pairs={{0,2},{2,0},{4,6},{6,4},{8,10},{10,8},{12,14},{14,12},{16,18},{18,... | collective-permute-start | bytes 2359304 | tf_op jit(solution)/shard_map/ppermute | solution.py:27
  46.5 11.9 %collective-permute-start.4 = (bf16[3,1024,128]{2,1,0:T(8,128)(2,1)}, bf16[3,1024,128]{2,1,0:T(8,128)(2,1)}, u32[]{:S(2)}, u32[]{:S(2)}) collective-permute-start(bf16[3,1024,128]{2,1,0:T(8,128)(2,1)} %collective-permute-done.3.p2), channel_id=1, source_target_pairs={{0,2},{2,0},{4,6},{6,4},{8,10},{10,8},{12,14},{14,12},{16,18},{18,... | collective-permute-start | bytes 2359304 | tf_op jit(solution)/shard_map/ppermute | solution.py:27
  47.5 9.2 %collective-permute-start.5 = (bf16[128,1024]{1,0:T(8,128)(2,1)S(1)}, bf16[128,1024]{1,0:T(8,128)(2,1)S(1)}, u32[]{:S(2)}, u32[]{:S(2)}) collective-permute-start(bf16[128,1024]{1,0:T(8,128)(2,1)S(1)} %constant_dynamic-slice_fusion.3), channel_id=1, source_target_pairs={{0,1},{1,0},{2,3},{3,2},{4,5},{5,4},{6,7},{7,6},{8,9},{9,8},{10,11... | collective-permute-start | bytes 786440 | tf_op jit(solution)/shard_map/ppermute | solution.py:27
  50.5 28.7 %collective-permute-start.6 = (bf16[1024,512]{1,0:T(8,128)(2,1)S(1)}, bf16[1024,512]{1,0:T(8,128)(2,1)}, u32[]{:S(2)}, u32[]{:S(2)}) collective-permute-start(bf16[1024,512]{1,0:T(8,128)(2,1)S(1)} %constant_dynamic-slice_fusion.2), channel_id=1, source_target_pairs={{0,1},{1,0},{2,3},{3,2},{4,5},{5,4},{6,7},{7,6},{8,9},{9,8},{10,11... | collective-permute-start | bytes 3145736 | tf_op jit(solution)/shard_map/ppermute | solution.py:27
  53.2 7.3 %copy-start.35 = (bf16[1024,1024]{1,0:T(8,128)(2,1)S(1)}, bf16[1024,1024]{1,0:T(8,128)(2,1)}, u32[]{:S(2)}) copy-start(bf16[1024,1024]{1,0:T(8,128)(2,1)} %get-tuple-element.97.v_ref) | copy-start | bytes 6291460
  53.2 51.5 %collective-permute-start.10 = (bf16[512,1024]{1,0:T(8,128)(2,1)}, bf16[512,1024]{1,0:T(8,128)(2,1)}, u32[]{:S(2)}, u32[]{:S(2)}) collective-permute-start(bf16[512,1024]{1,0:T(8,128)(2,1)} %constant_dynamic-slice_fusion.1), channel_id=1, source_target_pairs={{0,1},{1,0},{2,3},{3,2},{4,5},{5,4},{6,7},{7,6},{8,9},{9,8},{10,11... | collective-permute-start | bytes 3145736 | tf_op jit(solution)/shard_map/ppermute | solution.py:27
  56.6 22.6 %collective-permute-start.7 = (bf16[128,1024]{1,0:T(8,128)(2,1)S(1)}, bf16[128,1024]{1,0:T(8,128)(2,1)S(1)}, u32[]{:S(2)}, u32[]{:S(2)}) collective-permute-start(bf16[128,1024]{1,0:T(8,128)(2,1)S(1)} %collective-permute-done.5), channel_id=1, source_target_pairs={{0,4},{2,6},{4,0},{6,2},{8,12},{10,14},{12,8},{14,10},{16,20},{18,... | collective-permute-start | bytes 786440 | tf_op jit(solution)/shard_map/ppermute | solution.py:27
  58.4 32.8 %collective-permute-start.8 = (bf16[128,1024]{1,0:T(8,128)(2,1)S(1)}, bf16[128,1024]{1,0:T(8,128)(2,1)}, u32[]{:S(2)}, u32[]{:S(2)}) collective-permute-start(bf16[128,1024]{1,0:T(8,128)(2,1)S(1)} %collective-permute-done.5), channel_id=1, source_target_pairs={{0,2},{2,0},{4,6},{6,4},{8,10},{10,8},{12,14},{14,12},{16,18},{18,... | collective-permute-start | bytes 786440 | tf_op jit(solution)/shard_map/ppermute | solution.py:27
  60.5 21.2 %copy-start.34 = (bf16[128,1024]{1,0:T(8,128)(2,1)S(1)}, bf16[128,1024]{1,0:T(8,128)(2,1)}, u32[]{:S(2)}) copy-start(bf16[128,1024]{1,0:T(8,128)(2,1)} %get-tuple-element.110.c_ref) | copy-start | bytes 786436
  79.9 24.7 %collective-permute-start.12 = (bf16[1024,512]{1,0:T(8,128)(2,1)}, bf16[1024,512]{1,0:T(8,128)(2,1)}, u32[]{:S(2)}, u32[]{:S(2)}) collective-permute-start(bf16[1024,512]{1,0:T(8,128)(2,1)} %collective-permute-done.6.p0), channel_id=1, source_target_pairs={{0,4},{2,6},{4,0},{6,2},{8,12},{10,14},{12,8},{14,10},{16,20},{18,... | collective-permute-start | bytes 3145736 | tf_op jit(solution)/shard_map/ppermute | solution.py:27
  90.6 2.5 collective-permute-start.9
  90.6 14.0 %collective-permute-start.11 = (bf16[1024,512]{1,0:T(8,128)(2,1)}, bf16[1024,512]{1,0:T(8,128)(2,1)S(1)}, u32[]{:S(2)}, u32[]{:S(2)}) collective-permute-start(bf16[1024,512]{1,0:T(8,128)(2,1)} %collective-permute-done.6.p0), channel_id=1, source_target_pairs={{0,2},{2,0},{4,6},{6,4},{8,10},{10,8},{12,14},{14,12},{16,18},{18,... | collective-permute-start | bytes 3145736 | tf_op jit(solution)/shard_map/ppermute | solution.py:27
  104.6 2.9 collective-permute-start.13
  140.2 45.1 %collective-permute-start.17 = (bf16[512,4096]{1,0:T(8,128)(2,1)}, bf16[512,4096]{1,0:T(8,128)(2,1)}, u32[]{:S(2)}, u32[]{:S(2)}) collective-permute-start(bf16[512,4096]{1,0:T(8,128)(2,1)} %rows_sent.2), channel_id=1, source_target_pairs={{0,2},{2,0},{4,6},{6,4},{8,10},{10,8},{12,14},{14,12},{16,18},{18,... | collective-permute-start | bytes 12582920 | tf_op jit(solution)/shard_map/ppermute | solution.py:27
  140.3 25.7 %collective-permute-start.15 = (bf16[512,1024]{1,0:T(8,128)(2,1)}, bf16[512,1024]{1,0:T(8,128)(2,1)S(1)}, u32[]{:S(2)}, u32[]{:S(2)}) collective-permute-start(bf16[512,1024]{1,0:T(8,128)(2,1)} %collective-permute-done.10.p0), channel_id=1, source_target_pairs={{0,4},{2,6},{4,0},{6,2},{8,12},{10,14},{12,8},{14,10},{16,20},{18,... | collective-permute-start | bytes 3145736 | tf_op jit(solution)/shard_map/ppermute | solution.py:27
  142.1 23.9 %collective-permute-start.14 = (bf16[512,1024]{1,0:T(8,128)(2,1)}, bf16[512,1024]{1,0:T(8,128)(2,1)S(1)}, u32[]{:S(2)}, u32[]{:S(2)}) collective-permute-start(bf16[512,1024]{1,0:T(8,128)(2,1)} %collective-permute-done.10.p0), channel_id=1, source_target_pairs={{0,2},{2,0},{4,6},{6,4},{8,10},{10,8},{12,14},{14,12},{16,18},{18,... | collective-permute-start | bytes 3145736 | tf_op jit(solution)/shard_map/ppermute | solution.py:27
  166.0 2.7 collective-permute-start.16
  196.5 9.1 %copy-start.31 = (bf16[256,4096]{1,0:T(8,128)(2,1)S(1)}, bf16[256,4096]{1,0:T(8,128)(2,1)}, u32[]{:S(2)}) copy-start(bf16[256,4096]{1,0:T(8,128)(2,1)} %get-tuple-element.137) | copy-start | bytes 6291460
  205.4 23.7 %collective-permute-start.18 = (bf16[512,4096]{1,0:T(8,128)(2,1)}, bf16[512,4096]{1,0:T(8,128)(2,1)}, u32[]{:S(2)}, u32[]{:S(2)}) collective-permute-start(bf16[512,4096]{1,0:T(8,128)(2,1)} %rows_sent.3), channel_id=1, source_target_pairs={{0,2},{2,0},{4,6},{6,4},{8,10},{10,8},{12,14},{14,12},{16,18},{18,... | collective-permute-start | bytes 12582920 | tf_op jit(solution)/shard_map/ppermute | solution.py:27
  205.5 47.9 %collective-permute-start.19 = (bf16[256,4096]{1,0:T(8,128)(2,1)S(1)}, bf16[256,4096]{1,0:T(8,128)(2,1)S(1)}, u32[]{:S(2)}, u32[]{:S(2)}) collective-permute-start(bf16[256,4096]{1,0:T(8,128)(2,1)S(1)} %copy-done.31), channel_id=1, source_target_pairs={{0,4},{2,6},{4,0},{6,2},{8,12},{10,14},{12,8},{14,10},{16,20},{18,... | collective-permute-start | bytes 6291464 | tf_op jit(solution)/shard_map/ppermute | solution.py:27
  256.8 29.9 %collective-permute-start.21 = (bf16[128,4096]{1,0:T(8,128)(2,1)}, bf16[128,4096]{1,0:T(8,128)(2,1)}, u32[]{:S(2)}, u32[]{:S(2)}) collective-permute-start(bf16[128,4096]{1,0:T(8,128)(2,1)} %slice.584), channel_id=1, source_target_pairs={{0,8},{2,10},{4,12},{6,14},{8,0},{10,2},{12,4},{14,6},{16,24},{18,... | collective-permute-start | bytes 3145736 | tf_op jit(solution)/shard_map/ppermute | solution.py:27
  278.7 25.3 %collective-permute-start.22 = (bf16[512,1024]{1,0:T(8,128)(2,1)}, bf16[512,1024]{1,0:T(8,128)(2,1)}, u32[]{:S(2)}, u32[]{:S(2)}) collective-permute-start(bf16[512,1024]{1,0:T(8,128)(2,1)} %group_sent.2), channel_id=1, source_target_pairs={{0,2},{2,0},{4,6},{6,4},{8,10},{10,8},{12,14},{14,12},{16,18},{18,... | collective-permute-start | bytes 3145736 | tf_op jit(solution)/shard_map/ppermute | solution.py:27
  278.7 5.7 %copy-start.15 = (bf16[1024,1024]{1,0:T(8,128)(2,1)S(1)}, bf16[1024,1024]{1,0:T(8,128)(2,1)}, u32[]{:S(2)}) copy-start(bf16[1024,1024]{1,0:T(8,128)(2,1)} %get-tuple-element.143.dx_ref) | copy-start | bytes 6291460
  278.7 5.7 %copy-start.27 = (bf16[512,1024]{1,0:T(8,128)(2,1)S(1)}, bf16[512,1024]{1,0:T(8,128)(2,1)}, u32[]{:S(2)}) copy-start(bf16[512,1024]{1,0:T(8,128)(2,1)} %copy-done.26) | copy-start | bytes 3145732
  278.7 48.4 %collective-permute-start.23 = (bf16[256,4096]{1,0:T(8,128)(2,1)}, bf16[256,4096]{1,0:T(8,128)(2,1)}, u32[]{:S(2)}, u32[]{:S(2)}) collective-permute-start(bf16[256,4096]{1,0:T(8,128)(2,1)} %get-tuple-element.154), channel_id=1, source_target_pairs={{0,4},{2,6},{4,0},{6,2},{8,12},{10,14},{12,8},{14,10},{16,20},{18,... | collective-permute-start | bytes 6291464 | tf_op jit(solution)/shard_map/ppermute | solution.py:27
  290.3 29.0 %collective-permute-start.24 = (bf16[64,4096]{1,0:T(8,128)(2,1)}, bf16[64,4096]{1,0:T(8,128)(2,1)}, u32[]{:S(2)}, u32[]{:S(2)}) collective-permute-start(bf16[64,4096]{1,0:T(8,128)(2,1)} %slice.587), channel_id=1, source_target_pairs={{0,16},{2,18},{4,20},{6,22},{8,24},{10,26},{12,28},{14,30},{16,0},... | collective-permute-start | bytes 1572872 | tf_op jit(solution)/shard_map/ppermute | solution.py:27
  320.7 9.0 %copy-start.11 = (f32[64,4096]{1,0:T(8,128)}, f32[64,4096]{1,0:T(8,128)S(1)}, u32[]{:S(2)}) copy-start(f32[64,4096]{1,0:T(8,128)S(1)} %slice_add_fusion.4) | copy-start | bytes 3145732
  321.5 8.2 %copy-start.17 = (bf16[256,4096]{1,0:T(8,128)(2,1)S(1)}, bf16[256,4096]{1,0:T(8,128)(2,1)}, u32[]{:S(2)}) copy-start(bf16[256,4096]{1,0:T(8,128)(2,1)} %get-tuple-element.136) | copy-start | bytes 6291460
  342.7 34.5 %collective-permute-start.27 = (bf16[512,3072]{1,0:T(8,128)(2,1)}, bf16[512,3072]{1,0:T(8,128)(2,1)}, u32[]{:S(2)}, u32[]{:S(2)}) collective-permute-start(bf16[512,3072]{1,0:T(8,128)(2,1)} %group_sent.3), channel_id=1, source_target_pairs={{0,2},{2,0},{4,6},{6,4},{8,10},{10,8},{12,14},{14,12},{16,18},{18,... | collective-permute-start | bytes 9437192 | tf_op jit(solution)/shard_map/ppermute | solution.py:27
  342.7 14.7 %collective-permute-start.25 = (bf16[256,1024]{1,0:T(8,128)(2,1)}, bf16[256,1024]{1,0:T(8,128)(2,1)}, u32[]{:S(2)}, u32[]{:S(2)}) collective-permute-start(bf16[256,1024]{1,0:T(8,128)(2,1)} %get-tuple-element.160), channel_id=1, source_target_pairs={{0,4},{2,6},{4,0},{6,2},{8,12},{10,14},{12,8},{14,10},{16,20},{18,... | collective-permute-start | bytes 1572872 | tf_op jit(solution)/shard_map/ppermute | solution.py:27
  344.3 20.0 %copy-start.7 = (bf16[3,1024,512]{2,1,0:T(8,128)(2,1)S(1)}, bf16[3,1024,512]{2,1,0:T(8,128)(2,1)}, u32[]{:S(2)}) copy-start(bf16[3,1024,512]{2,1,0:T(8,128)(2,1)} %own_ref.9) | copy-start | bytes 9437188
  344.3 52.9 %collective-permute-start.20 = (bf16[1024,1024]{1,0:T(8,128)(2,1)}, bf16[1024,1024]{1,0:T(8,128)(2,1)}, u32[]{:S(2)}, u32[]{:S(2)}) collective-permute-start(bf16[1024,1024]{1,0:T(8,128)(2,1)} %hidden_out.1), channel_id=1, source_target_pairs={{0,1},{1,0},{2,3},{3,2},{4,5},{5,4},{6,7},{7,6},{8,9},{9,8},{10,11... | collective-permute-start | bytes 6291464 | tf_op jit(solution)/shard_map/ppermute | solution.py:27
  345.8 52.0 %collective-permute-start.30 = (bf16[64,2048]{1,0:T(8,128)(2,1)}, bf16[64,2048]{1,0:T(8,128)(2,1)S(1)}, u32[]{:S(2)}, u32[]{:S(2)}) collective-permute-start(bf16[64,2048]{1,0:T(8,128)(2,1)} %slice.591), channel_id=1, source_target_pairs={{0,1},{1,0},{2,3},{3,2},{4,5},{5,4},{6,7},{7,6},{8,9},{9,8},{10,11... | collective-permute-start | bytes 786440 | tf_op jit(solution)/shard_map/ppermute | solution.py:27
  362.2 11.2 %collective-permute-start.26 = (bf16[128,1024]{1,0:T(8,128)(2,1)}, bf16[128,1024]{1,0:T(8,128)(2,1)}, u32[]{:S(2)}, u32[]{:S(2)}) collective-permute-start(bf16[128,1024]{1,0:T(8,128)(2,1)} %slice.590), channel_id=1, source_target_pairs={{0,8},{2,10},{4,12},{6,14},{8,0},{10,2},{12,4},{14,6},{16,24},{18,... | collective-permute-start | bytes 786440 | tf_op jit(solution)/shard_map/ppermute | solution.py:27
  362.5 33.2 %collective-permute-start.28 = (bf16[128,4096]{1,0:T(8,128)(2,1)}, bf16[128,4096]{1,0:T(8,128)(2,1)}, u32[]{:S(2)}, u32[]{:S(2)}) collective-permute-start(bf16[128,4096]{1,0:T(8,128)(2,1)} %slice.583), channel_id=1, source_target_pairs={{0,8},{2,10},{4,12},{6,14},{8,0},{10,2},{12,4},{14,6},{16,24},{18,... | collective-permute-start | bytes 3145736 | tf_op jit(solution)/shard_map/ppermute | solution.py:27
  367.6 5.8 %copy-start.14 = (f32[256,1024]{1,0:T(8,128)S(1)}, f32[256,1024]{1,0:T(8,128)}, u32[]{:S(2)}) copy-start(f32[256,1024]{1,0:T(8,128)} %copy-done.13) | copy-start | bytes 3145732
  374.5 21.2 %copy-start.1 = (f32[256,4096]{1,0:T(8,128)S(1)}, f32[256,4096]{1,0:T(8,128)}, u32[]{:S(2)}) copy-start(f32[256,4096]{1,0:T(8,128)} %copy-done) | copy-start | bytes 12582916
  374.5 22.7 %collective-permute-start.29 = (bf16[64,1024]{1,0:T(8,128)(2,1)S(1)}, bf16[64,1024]{1,0:T(8,128)(2,1)S(1)}, u32[]{:S(2)}, u32[]{:S(2)}) collective-permute-start(bf16[64,1024]{1,0:T(8,128)(2,1)S(1)} %slice.593), channel_id=1, source_target_pairs={{0,16},{2,18},{4,20},{6,22},{8,24},{10,26},{12,28},{14,30},{16,0},... | collective-permute-start | bytes 393224 | tf_op jit(solution)/shard_map/ppermute | solution.py:27
  397.8 72.0 %collective-permute-start.41 = (bf16[64,512]{1,0:T(8,128)(2,1)S(1)}, bf16[64,512]{1,0:T(8,128)(2,1)S(1)}, u32[]{:S(2)}, u32[]{:S(2)}) collective-permute-start(bf16[64,512]{1,0:T(8,128)(2,1)S(1)} %slice.594), channel_id=1, source_target_pairs={{0,1},{1,0},{2,3},{3,2},{4,5},{5,4},{6,7},{7,6},{8,9},{9,8},{10,11... | collective-permute-start | bytes 196616 | tf_op jit(solution)/shard_map/ppermute | solution.py:27
  399.3 89.8 %collective-permute-start.42 = (bf16[64,4096]{1,0:T(8,128)(2,1)S(1)}, bf16[64,4096]{1,0:T(8,128)(2,1)S(1)}, u32[]{:S(2)}, u32[]{:S(2)}) collective-permute-start(bf16[64,4096]{1,0:T(8,128)(2,1)S(1)} %slice.586), channel_id=1, source_target_pairs={{0,16},{2,18},{4,20},{6,22},{8,24},{10,26},{12,28},{14,30},{16,0},... | collective-permute-start | bytes 1572872 | tf_op jit(solution)/shard_map/ppermute | solution.py:27
  401.9 19.7 %copy-start.22 = (f32[17,1024]{1,0:T(8,128)S(1)}, f32[17,1024]{1,0:T(8,128)}, u32[]{:S(2)}) copy-start(f32[17,1024]{1,0:T(8,128)} %get-tuple-element.175) | copy-start | bytes 208900
  401.9 19.7 %copy-start.28 = (f32[2,1024]{1,0:T(2,128)S(1)}, f32[2,1024]{1,0:T(2,128)}, u32[]{:S(2)}) copy-start(f32[2,1024]{1,0:T(2,128)} %get-tuple-element.176) | copy-start | bytes 24580
  401.9 22.0 %copy-start.32 = (bf16[256,3072]{1,0:T(8,128)(2,1)S(1)}, bf16[256,3072]{1,0:T(8,128)(2,1)}, u32[]{:S(2)}) copy-start(bf16[256,3072]{1,0:T(8,128)(2,1)} %get-tuple-element.178) | copy-start | bytes 4718596
  402.0 22.6 %copy-start.12 = (f32[64,4096]{1,0:T(8,128)S(1)}, f32[64,4096]{1,0:T(8,128)}, u32[]{:S(2)}) copy-start(f32[64,4096]{1,0:T(8,128)} %copy-done.11) | copy-start | bytes 3145732
  421.0 104.1 %collective-permute-start.31 = (bf16[1024,1024]{1,0:T(8,128)(2,1)}, bf16[1024,1024]{1,0:T(8,128)(2,1)S(1)}, u32[]{:S(2)}, u32[]{:S(2)}) collective-permute-start(bf16[1024,1024]{1,0:T(8,128)(2,1)} %get-tuple-element.174), channel_id=1, source_target_pairs={{0,1},{1,0},{2,3},{3,2},{4,5},{5,4},{6,7},{7,6},{8,9},{9,8},{10,11... | collective-permute-start | bytes 6291464 | tf_op jit(solution)/shard_map/ppermute | solution.py:27
  422.4 47.3 %collective-permute-start.32 = (f32[21,1024]{1,0:T(8,128)S(1)}, f32[21,1024]{1,0:T(8,128)S(1)}, u32[]{:S(2)}, u32[]{:S(2)}) collective-permute-start(f32[21,1024]{1,0:T(8,128)S(1)} %pad_maximum_fusion.1), channel_id=1, source_target_pairs={{0,1},{1,0},{2,3},{3,2},{4,5},{5,4},{6,7},{7,6},{8,9},{9,8},{10,11... | collective-permute-start | bytes 258056 | tf_op jit(solution)/shard_map/ppermute | solution.py:27
  423.9 66.0 %collective-permute-start.37 = (bf16[256,3072]{1,0:T(8,128)(2,1)S(1)}, bf16[256,3072]{1,0:T(8,128)(2,1)S(1)}, u32[]{:S(2)}, u32[]{:S(2)}) collective-permute-start(bf16[256,3072]{1,0:T(8,128)(2,1)S(1)} %copy-done.32), channel_id=1, source_target_pairs={{0,4},{2,6},{4,0},{6,2},{8,12},{10,14},{12,8},{14,10},{16,20},{18,... | collective-permute-start | bytes 4718600 | tf_op jit(solution)/shard_map/ppermute | solution.py:27
  425.4 44.3 %copy-start.29 = (f32[2,1024]{1,0:T(2,128)S(1)}, f32[2,1024]{1,0:T(2,128)}, u32[]{:S(2)}) copy-start(f32[2,1024]{1,0:T(2,128)} %get-tuple-element.177) | copy-start | bytes 24580
  429.9 59.3 %copy-start.4 = (f32[128,4096]{1,0:T(8,128)S(1)}, f32[128,4096]{1,0:T(8,128)}, u32[]{:S(2)}) copy-start(f32[128,4096]{1,0:T(8,128)} %copy-done.3) | copy-start | bytes 6291460
  469.7 1.4 collective-permute-start.33
  471.1 4.9 collective-permute-start.34
  476.1 4.7 collective-permute-start.35
  480.8 6.5 %collective-permute-start.36 = (f32[21,1024]{1,0:T(8,128)S(1)}, f32[21,1024]{1,0:T(8,128)S(1)}, u32[]{:S(2)}, u32[]{:S(2)}) collective-permute-start(f32[21,1024]{1,0:T(8,128)S(1)} %add.91), channel_id=1, source_target_pairs={{0,16},{2,18},{4,20},{6,22},{8,24},{10,26},{12,28},{14,30},{16,0},... | collective-permute-start | bytes 258056 | tf_op jit(solution)/shard_map/ppermute | solution.py:27
  489.3 6.4 %collective-permute-start.43 = (bf16[64,2048]{1,0:T(8,128)(2,1)S(1)}, bf16[64,2048]{1,0:T(8,128)(2,1)S(1)}, u32[]{:S(2)}, u32[]{:S(2)}) collective-permute-start(bf16[64,2048]{1,0:T(8,128)(2,1)S(1)} %slice.589), channel_id=1, source_target_pairs={{0,1},{1,0},{2,3},{3,2},{4,5},{5,4},{6,7},{7,6},{8,9},{9,8},{10,11... | collective-permute-start | bytes 786440 | tf_op jit(solution)/shard_map/ppermute | solution.py:27
  491.2 16.6 %collective-permute-start.38 = (bf16[128,3072]{1,0:T(8,128)(2,1)S(1)}, bf16[128,3072]{1,0:T(8,128)(2,1)S(1)}, u32[]{:S(2)}, u32[]{:S(2)}) collective-permute-start(bf16[128,3072]{1,0:T(8,128)(2,1)S(1)} %slice.585), channel_id=1, source_target_pairs={{0,8},{2,10},{4,12},{6,14},{8,0},{10,2},{12,4},{14,6},{16,24},{18,... | collective-permute-start | bytes 2359304 | tf_op jit(solution)/shard_map/ppermute | solution.py:27
  508.0 17.1 %copy-start.16 = (bf16[1024,1024]{1,0:T(8,128)(2,1)S(1)}, bf16[1024,1024]{1,0:T(8,128)(2,1)}, u32[]{:S(2)}) copy-start(bf16[1024,1024]{1,0:T(8,128)(2,1)} %get-tuple-element.174) | copy-start | bytes 6291460
  508.0 16.5 %collective-permute-start.39 = (bf16[64,3072]{1,0:T(8,128)(2,1)S(1)}, bf16[64,3072]{1,0:T(8,128)(2,1)S(1)}, u32[]{:S(2)}, u32[]{:S(2)}) collective-permute-start(bf16[64,3072]{1,0:T(8,128)(2,1)S(1)} %slice.588), channel_id=1, source_target_pairs={{0,16},{2,18},{4,20},{6,22},{8,24},{10,26},{12,28},{14,30},{16,0},... | collective-permute-start | bytes 1179656 | tf_op jit(solution)/shard_map/ppermute | solution.py:27
  524.7 6.3 %collective-permute-start.40 = (bf16[64,1536]{1,0:T(8,128)(2,1)S(1)}, bf16[64,1536]{1,0:T(8,128)(2,1)S(1)}, u32[]{:S(2)}, u32[]{:S(2)}) collective-permute-start(bf16[64,1536]{1,0:T(8,128)(2,1)S(1)} %slice.592), channel_id=1, source_target_pairs={{0,1},{1,0},{2,3},{3,2},{4,5},{5,4},{6,7},{7,6},{8,9},{9,8},{10,11... | collective-permute-start | bytes 589832 | tf_op jit(solution)/shard_map/ppermute | solution.py:27
  (16 other events, 36.8 us)

commit v3 on v2

--- a/solution.py
+++ b/solution.py
@@ -303,15 +303,13 @@
     return pltpu.CompilerParams(vmem_limit_bytes=56 << 20)
 
 
-def halving_order(count):
-    bits = count.bit_length() - 1
-    return [sum(((p >> (bits - 1 - b)) & 1) << b for b in range(bits)) for p in range(count)]
-
-
-def place_rows(where_ref, tall_ref, out_ref, count):
+def place_rows(where_ref, tall_ref, out_ref, count, depth):
     size = tall_ref.shape[0] // count
-    for p, code in enumerate(halving_order(count)):
-        start = pl.multiple_of((where_ref[1] ^ code) * size, size)
+    tail = count >> depth
+    low = where_ref[1] & ((1 << depth) - 1)
+    for p in range(count):
+        code = sum(((p // tail >> (depth - 1 - b)) & 1) << b for b in range(depth))
+        start = pl.multiple_of(((p % tail) * (1 << depth) + (low ^ code)) * size, size)
         out_ref[p * size : (p + 1) * size, :] = tall_ref[pl.ds(start, size), :]
 
 
@@ -339,9 +337,9 @@
         u = (hat * gain_ref[...] + bias_ref[...]).astype(BF16)
         u_ref[...] = u
         tall[...] = u.T
-        place_rows(where_ref, tall, ut_ref, count)
+        place_rows(where_ref, tall, ut_ref, count, 2)
         tall[...] = dy_ref[0, 0].T
-        place_rows(where_ref, tall, dyt_ref, count)
+        place_rows(where_ref, tall, dyt_ref, count, 1)
 
     mine = lambda i, w: (w[0], 0, i, 0)
     return pl.pallas_call(
@@ -375,7 +373,7 @@
 def context_rows(where, context, count):
     def kernel(where_ref, c_ref, out_ref, tall):
         tall[...] = c_ref[...].T
-        place_rows(where_ref, tall, out_ref, count)
+        place_rows(where_ref, tall, out_ref, count, 2)
 
     rows, width = context.shape
     return pl.pallas_call(
@@ -401,7 +399,7 @@
         u = (hat * gain_ref[...] + bias_ref[...]).astype(BF16)
         u_ref[...] = u
         tall[...] = u.T
-        place_rows(where_ref, tall, ut_ref, count)
+        place_rows(where_ref, tall, ut_ref, count, 2)
 
     row = lambda i, w: (i, 0)
     return pl.pallas_call(
@@ -439,26 +437,13 @@
 STEP = 1024
 
 
-def weight_copies(own_ref, piece_refs, held, sems, axis):
-    count = own_ref.shape[axis] // STEP
-    size = piece_refs[0].shape[axis]
-    per = STEP // size
-
-    def part(ref, start, extent):
-        return ref.at[pl.ds(start, extent), :] if axis == 0 else ref.at[:, pl.ds(start, extent)]
-
+def weight_copies(sides, held, sems, axis):
     copies = []
-    for j in range(count):
-        copies.append([pltpu.make_async_copy(part(own_ref, j * STEP, STEP), held.at[j], sems.at[j, 0])])
-    for j in range(len(piece_refs) // per):
-        copies.append(
-            [
-                pltpu.make_async_copy(
-                    piece_refs[j * per + k], part(held.at[count + j], k * size, size), sems.at[count + j, k]
-                )
-                for k in range(per)
-            ]
-        )
+    for ref in sides:
+        for j in range(ref.shape[axis] // STEP):
+            here = pl.ds(j * STEP, STEP)
+            source = ref.at[here, :] if axis == 0 else ref.at[:, here]
+            copies.append([pltpu.make_async_copy(source, held.at[len(copies)], sems.at[len(copies)])])
     return copies
 
 
@@ -491,13 +476,13 @@
     return (pre * half).astype(BF16), slope.astype(BF16)
 
 
-def hidden_forward(u2, up_own, up_pieces):
+def hidden_forward(u2, up_own, up_other):
     length, width = u2.shape
     steps = 2 * up_own.shape[1] // STEP
     chunk = 256
 
-    def kernel(u_ref, own_ref, p0, p1, p2, p3, hid_ref, slope_ref, held, sems):
-        stream_weights(weight_copies(own_ref, (p0, p1, p2, p3), held, sems, 1))
+    def kernel(u_ref, own_ref, other_ref, hid_ref, slope_ref, held, sems):
+        stream_weights(weight_copies((own_ref, other_ref), held, sems, 1))
         j = pl.program_id(0)
         for i in range(length // chunk):
             rows = slice(i * chunk, (i + 1) * chunk)
@@ -509,23 +494,23 @@
     return pl.pallas_call(
         kernel,
         grid=(steps,),
-        in_specs=[whole_block((length, width))] + [ANYWHERE] * 5,
+        in_specs=[whole_block((length, width))] + [ANYWHERE] * 2,
         out_specs=[tile, tile],
         out_shape=[jax.ShapeDtypeStruct((length, steps * STEP), BF16)] * 2,
-        scratch_shapes=[pltpu.VMEM((steps, width, STEP), BF16), pltpu.SemaphoreType.DMA((steps, 2))],
+        scratch_shapes=[pltpu.VMEM((steps, width, STEP), BF16), pltpu.SemaphoreType.DMA((steps,))],
         compiler_params=roomy(),
         cost_estimate=brief(),
         name="hidden_forward",
-    )(u2, up_own, *up_pieces)
-
-
-def hidden_backward(where, cotangent, down_own, down_pieces, slope):
+    )(u2, up_own, up_other)
+
+
+def hidden_backward(where, cotangent, down_own, down_other, slope):
     length, width = cotangent.shape[2:]
     steps = 2 * down_own.shape[0] // STEP
     chunk = 256
 
-    def kernel(where_ref, dy_ref, own_ref, p0, p1, p2, p3, slope_ref, out_ref, held, sems):
-        stream_weights(weight_copies(own_ref, (p0, p1, p2, p3), held, sems, 0))
+    def kernel(where_ref, dy_ref, own_ref, other_ref, slope_ref, out_ref, held, sems):
+        stream_weights(weight_copies((own_ref, other_ref), held, sems, 0))
         j = pl.program_id(0)
         for i in range(length // chunk):
             rows = slice(i * chunk, (i + 1) * chunk)
@@ -540,24 +525,24 @@
             in_specs=[
                 pl.BlockSpec((1, 1, length, width), lambda j, w: (w[0], 0, 0, 0), pipeline_mode=pl.Buffered(1))
             ]
-            + [ANYWHERE] * 5
+            + [ANYWHERE] * 2
             + [tile],
             out_specs=tile,
-            scratch_shapes=[pltpu.VMEM((steps, STEP, width), BF16), pltpu.SemaphoreType.DMA((steps, 2))],
+            scratch_shapes=[pltpu.VMEM((steps, STEP, width), BF16), pltpu.SemaphoreType.DMA((steps,))],
         ),
         out_shape=jax.ShapeDtypeStruct((length, steps * STEP), BF16),
         compiler_params=roomy(),
         cost_estimate=brief(),
         name="hidden_backward",
-    )(where, cotangent, down_own, *down_pieces, slope)
-
-
-def hidden_out(hid, down_own, down_pieces, x1):
+    )(where, cotangent, down_own, down_other, slope)
+
+
+def hidden_out(hid, down_own, down_other, x1):
     length, width = x1.shape
     steps = 2 * down_own.shape[0] // STEP
 
-    def kernel(hid_ref, own_ref, p0, p1, p2, p3, x1_ref, out_ref, held, total, sems):
-        stream_weights(weight_copies(own_ref, (p0, p1, p2, p3), held, sems, 0))
+    def kernel(hid_ref, own_ref, other_ref, x1_ref, out_ref, held, total, sems):
+        stream_weights(weight_copies((own_ref, other_ref), held, sems, 0))
         j = pl.program_id(0)
 
         @pl.when(j == 0)
@@ -573,27 +558,27 @@
     return pl.pallas_call(
         kernel,
         grid=(steps,),
-        in_specs=[pl.BlockSpec((length, STEP), lambda j: (0, j))] + [ANYWHERE] * 5 + [whole_block((length, width))],
+        in_specs=[pl.BlockSpec((length, STEP), lambda j: (0, j))] + [ANYWHERE] * 2 + [whole_block((length, width))],
         out_specs=whole_block((length, width)),
         out_shape=jax.ShapeDtypeStruct((length, width), BF16),
         scratch_shapes=[
             pltpu.VMEM((steps, STEP, width), BF16),
             pltpu.VMEM((length, width), F32),
-            pltpu.SemaphoreType.DMA((steps, 2)),
+            pltpu.SemaphoreType.DMA((steps,)),
         ],
         compiler_params=roomy(),
         cost_estimate=brief(),
         name="hidden_out",
-    )(hid, down_own, *down_pieces, x1)
-
-
-def second_norm_backward(where, dpre, up_own, up_pieces, x1, cotangent, gain, count):
+    )(hid, down_own, down_other, x1)
+
+
+def second_norm_backward(where, dpre, up_own, up_other, x1, cotangent, gain, count):
     length, width = x1.shape
     steps = 2 * up_own.shape[1] // STEP
     chunk = 128
 
-    def kernel(where_ref, dpre_ref, own_ref, p0, p1, p2, p3, x1_ref, dy_ref, gain_ref, out_ref, outt_ref, sums_ref, held, total, tall, sems):
-        stream_weights(weight_copies(own_ref, (p0, p1, p2, p3), held, sems, 1))
+    def kernel(where_ref, dpre_ref, own_ref, other_ref, x1_ref, dy_ref, gain_ref, out_ref, outt_ref, sums_ref, held, total, tall, sems):
+        stream_weights(weight_copies((own_ref, other_ref), held, sems, 1))
         j = pl.program_id(0)
 
         @pl.when(j == 0)
@@ -619,7 +604,7 @@
                 out_ref[rows, :] = out
                 tall[:, rows] = out.T
 
-            place_rows(where_ref, tall, outt_ref, count)
+            place_rows(where_ref, tall, outt_ref, count, 2)
 
     mine = pl.BlockSpec((1, 1, length, width), lambda j, w: (w[0], 0, 0, 0), pipeline_mode=pl.Buffered(1))
     return pl.pallas_call(
@@ -628,14 +613,14 @@
             num_scalar_prefetch=1,
             grid=(steps,),
             in_specs=[pl.BlockSpec((length, STEP), lambda j, w: (0, j))]
-            + [ANYWHERE] * 5
+            + [ANYWHERE] * 2
             + [whole_block((length, width)), mine, whole_block((1, width))],
             out_specs=[whole_block((length, width)), whole_block((width, length)), whole_block((2, width))],
             scratch_shapes=[
                 pltpu.VMEM((steps, width, STEP), BF16),
                 pltpu.VMEM((length, width), F32),
                 pltpu.VMEM((width, length), BF16),
-                pltpu.SemaphoreType.DMA((steps, 2)),
+                pltpu.SemaphoreType.DMA((steps,)),
             ],
         ),
         out_shape=[
@@ -646,34 +631,24 @@
         compiler_params=roomy(),
         cost_estimate=brief(),
         name="second_norm_backward",
-    )(where, dpre, up_own, *up_pieces, x1, cotangent, gain)
-
-
-def first_norm_backward(where, dsides, qkv_own, qkv_pieces, du_ssm, layer_in, dattn, gain):
+    )(where, dpre, up_own, up_other, x1, cotangent, gain)
+
+
+def first_norm_backward(where, dsides, qkv_own, qkv_other, du_ssm, layer_in, dattn, gain):
     length, width = layer_in.shape[2:]
     group = qkv_own.shape[2]
-    size = qkv_pieces[0].shape[2]
     chunk = 128
     steps = 6
 
-    def kernel(where_ref, do_ref, dt_ref, own_ref, p0, p1, p2, p3, ssm_ref, x_ref, dx_ref, gain_ref, out_ref, sums_ref, held, grads, total, sems):
-        copies = []
-        for s in range(3):
-            copies.append(
-                [
-                    pltpu.make_async_copy(do_ref.at[s], grads.at[s], sems.at[s, 0]),
-                    pltpu.make_async_copy(own_ref.at[s], held.at[s], sems.at[s, 1]),
-                ]
-            )
-        for s in range(3):
-            some = [pltpu.make_async_copy(dt_ref.at[s], grads.at[3 + s], sems.at[3 + s, 0])]
-            for k, piece in enumerate((p0, p1, p2, p3)):
-                some.append(
-                    pltpu.make_async_copy(
-                        piece.at[s], held.at[3 + s, :, pl.ds(k * size, size)], sems.at[3 + s, 1 + k]
-                    )
-                )
-            copies.append(some)
+    def kernel(where_ref, do_ref, dt_ref, own_ref, other_ref, ssm_ref, x_ref, dx_ref, gain_ref, out_ref, sums_ref, held, grads, total, sems):
+        copies = [
+            [
+                pltpu.make_async_copy(grad.at[s], grads.at[3 * k + s], sems.at[3 * k + s, 0]),
+                pltpu.make_async_copy(weight.at[s], held.at[3 * k + s], sems.at[3 * k + s, 1]),
+            ]
+            for k, (grad, weight) in enumerate(((do_ref, own_ref), (dt_ref, other_ref)))
+            for s in range(3)
+        ]
         stream_weights(copies)
         j = pl.program_id(0)
 
@@ -703,86 +678,120 @@
         grid_spec=pltpu.PrefetchScalarGridSpec(
             num_scalar_prefetch=1,
             grid=(steps,),
-            in_specs=[ANYWHERE] * 7
+            in_specs=[ANYWHERE] * 4
             + [whole_block(du_ssm.shape), mine, whole_block((length, width)), whole_block((1, width))],
             out_specs=[whole_block((length, width)), whole_block((2, width))],
             scratch_shapes=[
                 pltpu.VMEM((steps, width, group), BF16),
                 pltpu.VMEM((steps, length, group), BF16),
                 pltpu.VMEM((length, width), F32),
-                pltpu.SemaphoreType.DMA((steps, 5)),
+                pltpu.SemaphoreType.DMA((steps, 2)),
             ],
         ),
         out_shape=[jax.ShapeDtypeStruct((length, width), BF16), jax.ShapeDtypeStruct((2, width), F32)],
         compiler_params=roomy(),
         cost_estimate=brief(),
         name="first_norm_backward",
-    )(where, dsides[0], dsides[1], qkv_own, *qkv_pieces, du_ssm, layer_in, dattn, gain)
-
-
-def rows_sent(left, right):
+    )(where, dsides[0], dsides[1], qkv_own, qkv_other, du_ssm, layer_in, dattn, gain)
+
+
+def down_rows(left, right, got):
     width, length = left.shape
     half = width // 2
     columns = right.shape[1]
 
-    def kernel(left_ref, right_ref, out_ref):
-        out_ref[...] = mm(left_ref[...], right_ref[...]).astype(BF16)
-
+    def kernel(left_ref, right_ref, *rest):
+        total = mm(left_ref[...], right_ref[...])
+        if got is not None:
+            total += rest[0][...].astype(F32)
+        rest[-1][...] = total.astype(BF16)
+
+    tile = pl.BlockSpec((half, STEP), lambda j: (0, j))
+    pick = 1 if got is None else 0
     return pl.pallas_call(
         kernel,
         grid=(columns // STEP,),
         in_specs=[
-            pl.BlockSpec((half, length), lambda j: (1, 0), pipeline_mode=pl.Buffered(1)),
+            pl.BlockSpec((half, length), lambda j: (pick, 0), pipeline_mode=pl.Buffered(1)),
             pl.BlockSpec((length, STEP), lambda j: (0, j)),
-        ],
-        out_specs=pl.BlockSpec((half, STEP), lambda j: (0, j)),
+        ]
+        + ([] if got is None else [tile]),
+        out_specs=tile,
         out_shape=jax.ShapeDtypeStruct((half, columns), BF16),
         compiler_params=roomy(),
         cost_estimate=brief(),
-        name="rows_sent",
-    )(left, right)
-
-
-def rows_kept(left, right, got):
+        name="down_sent" if got is None else "down_kept",
+    )(left, right, *([] if got is None else [got]))
+
+
+def up_rows(left, right, out_left, heads_own, heads_other, got):
     width, length = left.shape
     half = width // 2
     quart = width // 4
     columns = right.shape[1]
-    piece = columns // 8
-    steps = columns // STEP
-
-    def kernel(left_ref, right_ref, got_ref, keep_ref, send_ref):
+    group = heads_own.shape[1]
+    tile = group
+    ups = columns // 2 // tile
+    steps = 2 * (ups + 1)
+    keeping = got is not None
+
+    def kernel(left_ref, right_ref, out_left_ref, own_ref, other_ref, *rest):
         j = pl.program_id(0)
-        for part, out_ref in enumerate((keep_ref, send_ref)):
-            rows = slice(part * quart, (part + 1) * quart)
-            total = mm(left_ref[rows, :], right_ref[...])
-
-            @pl.when(j < steps // 2)
-            def _(total=total, out_ref=out_ref, rows=rows):
-                out_ref[...] = (total + got_ref[rows, :].astype(F32)).astype(BF16)
-
-            @pl.when(j >= steps // 2)
-            def _(total=total, out_ref=out_ref, rows=rows):
-                for k in range(STEP // piece):
-                    here = slice(k * piece, (k + 1) * piece)
-                    there = slice((k ^ 1) * piece, ((k ^ 1) + 1) * piece)
-                    out_ref[:, here] = (total[:, here] + got_ref[rows, there].astype(F32)).astype(BF16)
-
-    tile = pl.BlockSpec((quart, STEP), lambda j: (0, j))
+
+        def emit(lref, rref, swap):
+            for part in range(2 if keeping else 1):
+                rows = slice(part * quart, (part + 1) * quart) if keeping else slice(0, half)
+                total = mm(lref[rows, :], rref[...])
+                if not keeping:
+                    rest[0][...] = total.astype(BF16)
+                    continue
+                come = rest[0][rows, :].astype(F32)
+                if swap:
+                    come = jnp.concatenate([come[:, tile // 2 :], come[:, : tile // 2]], axis=1)
+                rest[1 + part][...] = (total + come).astype(BF16)
+
+        @pl.when(lax.rem(j, ups + 1) < ups)
+        def _():
+            emit(left_ref, right_ref, False)
+
+        @pl.when(j == ups)
+        def _():
+            emit(out_left_ref, own_ref, False)
+
+        @pl.when(j == 2 * ups + 1)
+        def _():
+            emit(out_left_ref, other_ref, True)
+
+    pick = 0 if keeping else 1
+    side = pl.BlockSpec((half, length), lambda j: (pick, 0), pipeline_mode=pl.Buffered(1))
+    up_tile = lambda j: jnp.where(j <= ups, jnp.minimum(j, ups - 1), jnp.minimum(j - 1, 2 * ups - 1))
+    in_specs = [
+        side,
+        pl.BlockSpec((length, tile), lambda j: (0, up_tile(j))),
+        side,
+        whole_block((length, group)),
+        whole_block((length, group)),
+    ]
+    operands = [left, right, out_left, heads_own, heads_other]
+    total_columns = steps * tile
+    if keeping:
+        in_specs.append(pl.BlockSpec((half, tile), lambda j: (0, j)))
+        operands.append(got)
+        out_specs = [pl.BlockSpec((quart, tile), lambda j: (0, j))] * 2
+        out_shape = [jax.ShapeDtypeStruct((quart, total_columns), BF16)] * 2
+    else:
+        out_specs = pl.BlockSpec((half, tile), lambda j: (0, j))
+        out_shape = jax.ShapeDtypeStruct((half, total_columns), BF16)
     return pl.pallas_call(
         kernel,
         grid=(steps,),
-        in_specs=[
-            pl.BlockSpec((half, length), lambda j: (0, 0), pipeline_mode=pl.Buffered(1)),
-            pl.BlockSpec((length, STEP), lambda j: (0, j)),
-            pl.BlockSpec((half, STEP), lambda j: (0, j)),
-        ],
-        out_specs=[tile, tile],
-        out_shape=[jax.ShapeDtypeStruct((quart, columns), BF16)] * 2,
+        in_specs=in_specs,
+        out_specs=out_specs,
+        out_shape=out_shape,
         compiler_params=roomy(),
         cost_estimate=brief(),
-        name="rows_kept",
-    )(left, right, got)
+        name="up_kept" if keeping else "up_sent",
+    )(*operands)
 
 
 def group_rows(left, own, other, extra, got):
@@ -790,7 +799,7 @@
     half = width // 2
     quart = width // 4
     count, _, group = own.shape
-    piece = group // 4
+    piece = group // 2
     keeping = got is not None
 
     def kernel(*refs):
@@ -813,7 +822,7 @@
                     if not keeping:
                         refs[0][...] = total.astype(BF16)
                         continue
-                    for k in range(4):
+                    for k in range(2):
                         here = slice(k * piece, (k + 1) * piece)
                         come = k ^ side
                         there = slice(come * piece, (come + 1) * piece)
@@ -858,10 +867,10 @@
     )(*operands)
 
 
-def reorder(values, count, mask):
-    piece = values.shape[1] // (4 * count)
-    order = [4 * c + (k ^ mask) for c in range(count) for k in range(4)]
-    return jnp.concatenate([values[:, i * piece : (i + 1) * piece] for i in order], axis=1)
+def swap_halves(values, width):
+    half = width // 2
+    order = [start + half * k for start in range(0, values.shape[1], width) for k in (1, 0)]
+    return jnp.concatenate([values[:, i : i + half] for i in order], axis=1)
 
 
 def shards(
@@ -884,24 +893,26 @@
     mine = lax.axis_index("tensor")
     place = lax.axis_index("dp")
     where = jnp.stack([mine, place]).astype(jnp.int32)
-    bits = dp_count.bit_length() - 1
     rows_each = width // dp_count
     gain1, bias1, gain2, bias2 = ln1_gain[None], ln1_bias[None], ln2_gain[None], ln2_bias[None]
 
     over_x = lambda v: swap(v, "tensor", 1, 2)
     over = lambda v, bit: swap(v, "dp", 1 << bit, dp_count)
-
-    quarter = place & 3
-
-    def quarter_of(weight, axis):
-        size = weight.shape[axis] // 4
-        return lax.dynamic_slice_in_dim(weight, quarter * size, size, axis)
-
-    def pieces(first, beside):
-        return [first, over(first, 0), beside, over(beside, 0)]
+    core = place & 1
+
+    def scatter(values, depth):
+        groups = [[(k << depth) | low for k in range(dp_count >> depth)] for low in range(1 << depth)]
+        return lax.psum_scatter(values, "dp", scatter_dimension=0, axis_index_groups=groups, tiled=True)
+
+    def part_of(weight, axis, index, count):
+        size = weight.shape[axis] // count
+        return lax.dynamic_slice_in_dim(weight, index * size, size, axis)
 
     small = over_x(jnp.concatenate([ssm_coef, ssm_skip[None]], axis=0))
-    qkv_first = over_x(quarter_of(qkv_weight, 2))
+    up_part = over_x(part_of(up_weight, 0, place, dp_count))
+    qkv_first = over_x(part_of(qkv_weight, 2, core, 2))
+    down_part = over_x(part_of(down_weight, 0, place, dp_count))
+    out_first = over_x(part_of(out_weight, 0, core, 2))
 
     def in_order(own, other, axis):
         return jnp.where(
@@ -911,140 +922,101 @@
     coef = in_order(ssm_coef, small[:NS], 1)
     skip = in_order(ssm_skip[None], small[NS:], 1)
 
-    class Halvings:
-        def __init__(self, keep, send, count):
-            self.columns, self.count, self.bit, self.crossed = keep.shape[1] // 2, count, 2, False
-            self.total, self.message = keep.astype(F32), send
-            self.got = over(send, 1)
-
-        def step(self, *deps):
-            got = tie(self.got, *deps)
-            if self.bit == 2:
-                other = reorder(got[:, self.columns :], self.count, 2)
-                got = jnp.concatenate([got[:, : self.columns], other], axis=1)
-            self.total = self.total + got
-            if self.bit < bits:
-                rows = self.total.shape[0] // 2
-                self.message = self.total[rows:].astype(BF16)
-                self.total = self.total[:rows]
-                self.got = over(self.message, self.bit)
-                self.bit += 1
-            else:
-                self.message = self.total[:, self.columns :].astype(BF16)
-                self.got = over_x(self.message)
-                self.crossed = True
-            return self.message
-
-        def last(self):
-            while not self.crossed:
-                self.step()
-            got = self.got
-            for bit in range(2):
-                got = jnp.where((place >> bit) & 1 == 1, reorder(got, self.count, 1 << bit), got)
-            return self.total[:, : self.columns] + got
-
     u1, u1_rows, dy_rows = first_norm(where, layer_in, cotangent, gain1, bias1, dp_count)
 
     def project(rows, weight):
         return jnp.einsum("td,sde->ste", rows, weight, preferred_element_type=F32).astype(BF16)
 
-    out_first = over_x(tie(quarter_of(out_weight, 0), u1))
-    up_first = over_x(tie(quarter_of(up_weight, 1), u1))
-    qkv_own = project(u1, qkv_weight)
-    down_first = over_x(tie(quarter_of(down_weight, 0), qkv_own))
-    context, state = ssm_forward(tie(u1, qkv_own), coef, skip)
-    qkv_first = tie(qkv_first, context)
-    qkv_beside = over(qkv_first, 1)
-    context_turned = context_rows(tie(where, context, qkv_first), context, dp_count)
+    up_other = lax.all_gather(up_part, "dp", axis=0, tiled=True)
+    qkv_own = project(tie(u1, up_part), qkv_weight)
+    down_other = lax.all_gather(tie(down_part, qkv_own), "dp", axis=0, tiled=True)
+    context, state = ssm_forward(tie(u1, qkv_own, down_part), coef, skip)
+    context_turned = context_rows(tie(where, context), context, dp_count)
     ckv_own = project(tie(context, context_turned), qkv_weight[1:])
     heads_own, lse_own = attend_forward(qkv_own, ckv_own)
-    out_first = tie(out_first, heads_own)
-    out_beside = over(out_first, 1)
-    qkv_pieces = pieces(qkv_first, tie(qkv_beside, heads_own))
-    qkv_other_weight = tie(jnp.concatenate(qkv_pieces, axis=2), heads_own, out_first)
-    qkv_other = project(u1, qkv_other_weight)
-    up_first = tie(up_first, qkv_other)
-    up_beside = over(up_first, 1)
-    out_beside = tie(out_beside, qkv_other)
-    out_pieces = pieces(out_first, out_beside)
-    ckv_other = project(tie(context, up_first, out_beside), qkv_other_weight[1:])
-    heads_other, lse_other = attend_forward(qkv_other, ckv_other)
-    out_other = jnp.concatenate([tie(piece, heads_other) for piece in out_pieces], axis=0)
+    qkv_first = tie(qkv_first, heads_own)
+    qkv_other_weight = jnp.concatenate([qkv_first, over(qkv_first, 0)], axis=2)
+    qkv_other = project(tie(u1, heads_own), qkv_other_weight)
+    ckv_other = project(context, qkv_other_weight[1:])
+    out_first = tie(out_first, qkv_other)
+    out_second = over(out_first, 0)
+    heads_other, lse_other = attend_forward(qkv_other, tie(ckv_other, out_first))
+    out_other = jnp.concatenate([out_first, tie(out_second, heads_other)], axis=0)
     x1, u2, u2_rows = attention_out(
         where, layer_in, heads_own, heads_other, out_weight, out_other, gain2, bias2, dp_count
     )
-    up_pieces = pieces(up_first, tie(up_beside, u2))
-    down_first = tie(down_first, u2)
-    down_beside = over(down_first, 1)
-    hid, slope = hidden_forward(tie(u2, down_first), up_weight, up_pieces)
-
-    down_part = rows_sent(dy_rows, hid)
-    down_got = over(down_part, 0)
-    down_pieces = pieces(down_first, tie(down_beside, down_part))
-    dpre = hidden_backward(tie(where, down_part), cotangent, down_weight, down_pieces, slope)
-    down_keep, down_send = rows_kept(tie(dy_rows, dpre), hid, tie(down_got, dpre))
-    down = Halvings(down_keep, down_send, 1)
-    up_part = rows_sent(tie(u2_rows, down_keep), dpre)
-    up_got = over(up_part, 0)
+    hid, slope = hidden_forward(u2, up_weight, up_other)
+
+    down_mine = down_rows(dy_rows, hid, None)
+    down_got = over(down_mine, 0)
+    dpre = hidden_backward(tie(where, down_mine), cotangent, down_weight, down_other, slope)
+    down_kept = down_rows(tie(dy_rows, dpre), hid, tie(down_got, dpre))
+    down_sum = scatter(down_kept, 1)
     dattn, dattn_rows, sums2 = second_norm_backward(
-        tie(where, up_part), dpre, up_weight, up_pieces, x1, cotangent, gain2, dp_count
+        tie(where, down_kept), dpre, up_weight, up_other, x1, cotangent, gain2, dp_count
     )
-    up_keep, up_send = rows_kept(tie(u2_rows, dattn), dpre, tie(up_got, dattn))
-    up = Halvings(up_keep, up_send, 1)
-    message = down.step(up_keep)
-    layer_out = hidden_out(hid, down_weight, down_pieces, tie(x1, up_keep, message))
+    up_mine = up_rows(u2_rows, dpre, dattn_rows, heads_own, heads_other, None)
+    up_got = over(up_mine, 0)
+    layer_out = hidden_out(hid, down_weight, down_other, tie(x1, up_mine))
     layer_out_other = over_x(layer_out)
-
-    out_part = group_rows(tie(dattn_rows, layer_out), heads_own[None], heads_other[None], None, None)
-    out_got = over(out_part, 0)
-    dattn_then = tie(dattn, out_part)
+    up_keep, up_send = up_rows(tie(u2_rows, layer_out), dpre, dattn_rows, heads_own, heads_other, tie(up_got, layer_out))
+    up_got = over(up_send, 1)
+    dattn_then = tie(dattn, up_keep)
     dheads_other = mm_nt(dattn_then, out_other).astype(BF16)
     dheads_own = mm_nt(dattn_then, out_weight).astype(BF16)
-    message = down.step(dheads_own, dheads_other)
-    dqkv_other, dckv_other = attend_backward(
-        qkv_other, ckv_other, tie(dheads_other, dheads_own, message), lse_other
-    )
-    out_keep, out_send = group_rows(
-        tie(dattn_rows, dqkv_other), heads_own[None], heads_other[None], None, tie(out_got, dqkv_other)
-    )
-    out = Halvings(out_keep, out_send, 1)
-    dqkv_own, dckv_own = attend_backward(qkv_own, ckv_own, tie(dheads_own, out_keep), lse_own)
+    dqkv_other, dckv_other = attend_backward(qkv_other, ckv_other, tie(dheads_other, dheads_own), lse_other)
+    dqkv_own, dckv_own = attend_backward(qkv_own, ckv_own, tie(dheads_own, dqkv_other), lse_own)
 
     extra = (context_turned, dckv_own, dckv_other)
-    message_up, message_down = up.step(dqkv_own), down.step(dqkv_own)
-    qkv_part = group_rows(tie(u1_rows, message_up, message_down), dqkv_own, dqkv_other, extra, None)
-    qkv_got = over(qkv_part, 0)
-    message = out.step(qkv_part)
-    dckv_then = tie(dckv_own, qkv_part, message)
+    layer_out_other, down_sum = tie(layer_out_other, dqkv_own), tie(down_sum, dqkv_own)
+    down_cross = down_sum[:, down_sum.shape[1] // 2 :]
+    qkv_mine = group_rows(tie(u1_rows, layer_out_other, down_cross), dqkv_own, dqkv_other, extra, None)
+    qkv_got = over(qkv_mine, 0)
+    dckv_then = tie(dckv_own, qkv_mine)
     dcontext = jnp.einsum("sce,sde->cd", dckv_then, qkv_weight[1:], preferred_element_type=F32)
     dcontext += jnp.einsum("sce,sde->cd", dckv_other, qkv_other_weight[1:], preferred_element_type=F32)
     du_ssm, small_ssm = ssm_backward(u1, dcontext, coef, skip, state)
-    message = out.step(du_ssm)
+    up_sum = (up_keep.astype(F32) + tie(up_got, du_ssm)).astype(BF16)
     qkv_keep, qkv_send = group_rows(
-        tie(u1_rows, du_ssm, message), dqkv_own, dqkv_other, extra, tie(qkv_got, du_ssm)
+        tie(u1_rows, du_ssm, up_sum), dqkv_own, dqkv_other, extra, tie(qkv_got, du_ssm)
     )
-    qkv = Halvings(qkv_keep, qkv_send, 3)
-    message_up, message_out = up.step(qkv_keep), out.step(qkv_keep)
-    layer_out_other, down.got = tie(layer_out_other, qkv_keep), tie(down.got, qkv_keep)
+    up_sum = scatter(up_sum, 2)
+    qkv_got = over(qkv_send, 1)
     grad_in, sums1 = first_norm_backward(
-        tie(where, qkv_keep, message_up, message_out, layer_out_other, down.got),
+        tie(where, qkv_keep),
         (dqkv_own, dqkv_other),
         qkv_weight,
-        qkv_pieces,
+        qkv_other_weight,
         du_ssm,
         layer_in,
         dattn,
         gain1,
     )
     grad_in_other = over_x(grad_in)
-    up.step(grad_in)
+    qkv_sum = (qkv_keep.astype(F32) + tie(qkv_got, grad_in)).astype(BF16)
 
     small_all = jnp.concatenate([small_ssm, sums2, sums1], axis=0)
-    small_all = small_all + over_x(small_all)
-    for bit in range(bits):
+    small_all = small_all + tie(over_x(small_all), qkv_sum)
+    qkv_sum = scatter(qkv_sum, 2)
+    for bit in range(dp_count.bit_length() - 1):
         small_all = small_all + over(small_all, bit)
     here = lax.dynamic_slice_in_dim(small_all[: NS + 1], mine * group, group, 1)
-    grad_down, grad_up, grad_out, grad_qkv = down.last(), up.last(), out.last(), qkv.last()
+
+    def cross(values):
+        half = values.shape[1] // 2
+        return values[:, :half].astype(F32), over_x(values[:, half:]).astype(F32)
+
+    def ordered(values):
+        return jnp.where(core == 1, swap_halves(values, group), values)
+
+    down_own, down_come = cross(down_sum)
+    up_own, up_come = cross(up_sum)
+    qkv_mine, qkv_come = cross(qkv_sum)
+    hidden = up_weight.shape[1]
+    grad_down = down_own + down_come
+    grad_up = up_own[:, :hidden] + up_come[:, :hidden]
+    grad_out = up_own[:, hidden:] + ordered(up_come[:, hidden:])
+    grad_qkv = qkv_mine + ordered(qkv_come)
 
     def both_parts(own, other):
         return jnp.where(mine == 0, jnp.stack([own, other]), jnp.stack([other, own]))[:, None]

time: 542 us -> 430 us (0.79)
  waiting for transfers between devices: 181 us -> 96 us
  starting transfers between devices: 40.5 us -> 23.6 us
  local copies, waits for them, and re-layouts: 31.5 us -> 17.4 us
  between operations: 1.99 us -> 14.4 us
    ppermute x44 -> x22, waiting for transfers between devices: 181 us -> 95.9 us  [swap(): return lax.ppermute(value, axis, [(i, i ^ mask) for i in range(count)])]
    ppermute x44 -> x22, starting transfers between devices: 40.5 us -> 23 us  [swap(): return lax.ppermute(value, axis, [(i, i ^ mask) for i in range(count)])]
    pallas_call x4 -> x2, Pallas kernels: 27.6 us -> 19.4 us  [group_rows(): pl.pallas_call(kernel, grid=(2 * count,), in_specs=in_specs, out_specs=ou...]
    add x15 -> x3, other arithmetic: 9.77 us -> 1.86 us  [the longest x1 0.99 us: shards(): grad_qkv = qkv_mine + ordered(qkv_come)]
    unnamed x98 -> x52, local copies, waits for them, and re-layouts: 13.1 us -> 5.26 us
    slice x24 -> x3, local copies, waits for them, and re-layouts: 9.67 us -> 1.92 us  [the longest x1 0.97 us: shards(): down_cross = down_sum[:, down_sum.shape[1] // 2:]]
    convert_element_type x0 -> x5, other arithmetic: none -> 7.22 us  [the longest x1 4.28 us: shards(): up_sum = (up_keep.astype(F32) + tie(up_got, du_ssm)).astype(BF16)]
    pallas_call x4, Pallas kernels: 39.9 us -> 46.6 us  [the longest x2 27.6 us: up_rows(): pl.pallas_call(kernel, grid=(steps,), in_specs=in_specs, out_specs=out_sp...]
  transfers between devices with their start and end apart: 44 -> 27, of which waited for: 21 -> 12; matrix products, arithmetic and copies ran while one was open for 12% -> 14% of each run, Pallas kernels for 32% -> 51%
where the time goes in v3:
time: 430 us; the launch traced here: 424 us
  Pallas kernels  227 us (53%)
  waiting for transfers between devices  96 us (22%)
  other arithmetic  24.6 us (6%)
  starting transfers between devices  23.6 us (5%)
  matrix products  20.6 us (5%)
  local copies, waits for them, and re-layouts  17.4 us (4%)
  between operations  14.4 us (3%)
    ppermute x22, waiting for transfers between devices, swap(): return lax.ppermute(value, axis, [(i, i ^ mask) for i in range(count)])  95.9 us
    pallas_call x2, Pallas kernels, up_rows(): pl.pallas_call(kernel, grid=(steps,), in_specs=in_specs, out_specs=out_sp...  27.6 us
    ppermute x22, starting transfers between devices, swap(): return lax.ppermute(value, axis, [(i, i ^ mask) for i in range(count)])  23 us
    pallas_call x1, Pallas kernels, hidden_forward(): pl.pallas_call(kernel, grid=(steps,), in_specs=[whole_block((length, widt...  22.3 us
    pallas_call x2, Pallas kernels, attend_backward(): pl.pallas_call(attend_backward_kernel, grid=(heads,), in_specs=[pick(0),...  22.2 us
    pallas_call x1, Pallas kernels, second_norm_backward(): pl.pallas_call(kernel, grid_spec=pltpu.PrefetchScalarGridSpec(num_scalar_...  21.7 us
    pallas_call x2, Pallas kernels, group_rows(): pl.pallas_call(kernel, grid=(2 * count,), in_specs=in_specs, out_specs=ou...  19.4 us
    pallas_call x2, Pallas kernels, down_rows(): pl.pallas_call(kernel, grid=(columns // STEP,), in_specs=[pl.BlockSpec((h...  18.9 us
  transfers between devices with their start and end apart: 27, of which 12 were waited for; matrix products, arithmetic and copies ran while one was open for 14% of the time, Pallas kernels for 51%

profile of v3, /device:TPU:0, one launch (start us, length us, event | category | flops | bytes accessed | tf_op | source)
XLA Modules:
  0.0 423.7 jit_solution(7450114318141626868)
XLA Ops:
  7.2 1.0 constant_dynamic-slice_fusion.4
  8.2 3.0 collective-permute-start
  11.2 6.3 %collective-permute-done = bf16[64,2048]{1,0:T(8,128)(2,1)S(1)} collective-permute-done((bf16[64,2048]{1,0:T(8,128)(2,1)S(1)}, bf16[64,2048]{1,0:T(8,128)(2,1)S(1)}, u32[]{:S(2)}, u32[]{:S(2)}) %collective-permute-start) | collective-permute-done | bytes 262176 | tf_op jit(solution)/shard_map/ppermute | solution.py:27
  18.3 1.0 constant_dynamic-slice_fusion.3
  19.3 1.8 collective-permute-start.1
  22.1 2.7 constant_dynamic-slice_fusion.2
  24.8 1.7 collective-permute-start.3
  27.1 7.5 %first_norm.1 = (bf16[1024,1024]{1,0:T(8,128)(2,1)}, bf16[1024,1024]{1,0:T(8,128)(2,1)}, bf16[1024,1024]{1,0:T(8,128)(2,1)}) custom-call(s32[2]{0:T(128)} %pad_add_fusion.where_ref, bf16[2,1,1024,1024]{3,2,1,0:T(8,128)(2,1)} %x_ref.5, bf16[2,1,1024,1024]{3,2,1,0:T(8,128)(2,1)} %dy_ref.5, f32[1,1024]{1,0:T(1,128)} %bitcast.65, f32[1,1024]{1,0:T(1,128)} %bitcast.72), custom_call_target="tpu_custom_call" | custom-call | flops 4294967296 | bytes 65536 | tf_op jit(solution)/shard_map/first_norm/pallas_call | solution.py:345
  35.9 6.4 %convert_bitcast_fusion.1.q_ref.k_ref.v_ref = bf16[3,1024,512]{2,1,0:T(8,128)(2,1)} fusion(bf16[3,1024,512]{2,1,0:T(8,128)(2,1)S(1)} %copy-done.2, bf16[1024,1024]{1,0:T(8,128)(2,1)} %get-tuple-element.79.v_ref), kind=kOutput, calls=%fused_computation.6 | convolution fusion | flops 3222798336 | bytes 8388608 | tf_op jit(solution)/shard_map/td,sde->ste/dot_general | solution.py:928
  42.3 5.1 %ssm_forward.1 = (bf16[128,1024]{1,0:T(8,128)(2,1)}, f32[16,1024]{1,0:T(8,128)}) custom-call(bf16[1024,1024]{1,0:T(8,128)(2,1)} %get-tuple-element.79.v_ref, f32[16,1]{1,0:T(8,128)} %constant.28.clone.rates_ref, f32[16,1]{1,0:T(8,128)} %constant.29.clone.norms_ref, f32[16,1024]{1,0:T(8,128)} %maximum_select_fusion.2.coef_ref, ...), custom_call_target="tpu_custom_call" | custom-call | flops 4294967296 | bytes 65536 | tf_op jit(solution)/shard_map/ssm_forward/pallas_call | solution.py:100
  47.4 1.9 context_rows.1.refs_3_
  49.3 1.2 fusion.29.ck_ref.cv_ref
  50.5 7.9 %attend_forward.2 = (bf16[1024,512]{1,0:T(8,128)(2,1)}, f32[4,1,1024]{2,1,0:T(1,128)}) custom-call(bf16[3,1024,512]{2,1,0:T(8,128)(2,1)} %convert_bitcast_fusion.1.q_ref.k_ref.v_ref, bf16[3,1024,512]{2,1,0:T(8,128)(2,1)} %convert_bitcast_fusion.1.q_ref.k_ref.v_ref, bf16[3,1024,512]{2,1,0:T(8,128)(2,1)} %convert_bitcast_fusion.1.q_ref.k_ref.v_ref, ...), custom_call_target="tpu_custom_call" | custom-call | flops 4294967296 | bytes 65536 | tf_op jit(solution)/shard_map/attend_forward/pallas_call | solution.py:215
  58.4 3.3 collective-permute-done.3
  62.0 1.5 collective-permute-start.5
  63.5 1.5 constant_dynamic-update-slice_fusion.1
  65.4 1.5 constant_dynamic-update-slice_fusion.other_ref
  67.0 4.9 %convert_bitcast_fusion.q_ref.k_ref.v_ref = bf16[3,1024,512]{2,1,0:T(8,128)(2,1)} fusion(bf16[3,1024,512]{2,1,0:T(8,128)(2,1)S(1)} %constant_dynamic-update-slice_fusion.other_ref, bf16[1024,1024]{1,0:T(8,128)(2,1)S(1)} %copy-done.21), kind=kOutput, calls=%fused_computation.5 | convolution fusion | flops 3222798336 | bytes 8388608 | tf_op jit(solution)/shard_map/td,sde->ste/dot_general | solution.py:928
  71.9 4.6 %collective-permute-done.5 = bf16[256,1024]{1,0:T(8,128)(2,1)} collective-permute-done((bf16[256,1024]{1,0:T(8,128)(2,1)S(1)}, bf16[256,1024]{1,0:T(8,128)(2,1)}, u32[]{:S(2)}, u32[]{:S(2)}) %collective-permute-start.5) | collective-permute-done | bytes 524320 | tf_op jit(solution)/shard_map/ppermute | solution.py:27
  76.5 1.2 fusion.26.ck_ref.cv_ref
  77.7 1.9 constant_dynamic-update-slice_fusion.3
  79.6 7.8 %attend_forward.3 = (bf16[1024,512]{1,0:T(8,128)(2,1)}, f32[4,1,1024]{2,1,0:T(1,128)}) custom-call(bf16[3,1024,512]{2,1,0:T(8,128)(2,1)} %convert_bitcast_fusion.q_ref.k_ref.v_ref, bf16[3,1024,512]{2,1,0:T(8,128)(2,1)} %convert_bitcast_fusion.q_ref.k_ref.v_ref, bf16[3,1024,512]{2,1,0:T(8,128)(2,1)} %convert_bitcast_fusion.q_ref.k_ref.v_ref, ...), custom_call_target="tpu_custom_call" | custom-call | flops 4294967296 | bytes 65536 | tf_op jit(solution)/shard_map/attend_forward/pallas_call | solution.py:215
  87.4 1.9 constant_dynamic-update-slice_fusion.2.wt_ref
  89.3 8.9 %attention_out.1 = (f32[1024,1024]{1,0:T(8,128)}, bf16[1024,1024]{1,0:T(8,128)(2,1)}, bf16[1024,1024]{1,0:T(8,128)(2,1)}) custom-call(s32[2]{0:T(128)} %pad_add_fusion.where_ref, bf16[2,1,1024,1024]{3,2,1,0:T(8,128)(2,1)} %x_ref.5, bf16[1024,512]{1,0:T(8,128)(2,1)} %get-tuple-element.77.ho_ref.own_ref, bf16[1024,512]{1,0:T(8,128)(2,1)} %get-tuple-element.82.ht_ref.other_ref, ...), custom_call_target="tpu_custom_call" | custom-call | flops 4294967296 | bytes 65536 | tf_op jit(solution)/shard_map/attention_out/pallas_call | solution.py:405
  98.2 22.3 %hidden_forward.1 = (bf16[1024,4096]{1,0:T(8,128)(2,1)}, bf16[1024,4096]{1,0:T(8,128)(2,1)}) custom-call(bf16[1024,1024]{1,0:T(8,128)(2,1)} %get-tuple-element.84.u_ref, bf16[1024,2048]{1,0:T(8,128)(2,1)} %own_ref.7, bf16[1024,2048]{1,0:T(8,128)(2,1)} %all-gather.3.cloned.1.call-done.other_ref), custom_call_target="tpu_custom_call" | custom-call | flops 4294967296 | bytes 65536 | tf_op jit(solution)/shard_map/hidden_forward/pallas_call | solution.py:494
  120.5 8.8 %down_sent.1 = bf16[512,4096]{1,0:T(8,128)(2,1)} custom-call(bf16[1024,1024]{1,0:T(8,128)(2,1)} %get-tuple-element.92.left_ref, bf16[1024,4096]{1,0:T(8,128)(2,1)} %get-tuple-element.85.right_ref.hid_ref), custom_call_target="tpu_custom_call" | custom-call | flops 4294967296 | bytes 65536 | tf_op jit(solution)/shard_map/down_sent/pallas_call | solution.py:711
  129.8 15.7 %hidden_backward.1.dpre_ref.right_ref = bf16[1024,4096]{1,0:T(8,128)(2,1)} custom-call(s32[2]{0:T(128)} %pad_add_fusion.where_ref, bf16[2,1,1024,1024]{3,2,1,0:T(8,128)(2,1)} %dy_ref.5, bf16[2048,1024]{1,0:T(8,128)(2,1)} %own_ref.8, bf16[2048,1024]{1,0:T(8,128)(2,1)} %all-gather.5.cloned.1.call-done.other_ref, bf16[1024,4096]{1,0:T(8,128)(2,1)} %get-tuple-element.91.slope_ref), custom_call_target="tpu_custom_call" | custom-call | flops 4294967296 | bytes 65536 | tf_op jit(solution)/shard_map/hidden_backward/pallas_call | solution.py:520
  145.5 10.1 %down_kept.1 = bf16[512,4096]{1,0:T(8,128)(2,1)} custom-call(bf16[1024,1024]{1,0:T(8,128)(2,1)} %get-tuple-element.92.left_ref, bf16[1024,4096]{1,0:T(8,128)(2,1)} %get-tuple-element.85.right_ref.hid_ref, bf16[512,4096]{1,0:T(8,128)(2,1)} %collective-permute-done.7.rest_0_), custom_call_target="tpu_custom_call" | custom-call | flops 4294967296 | bytes 65536 | tf_op jit(solution)/shard_map/down_kept/pallas_call | solution.py:711
  155.9 21.7 %second_norm_backward.1 = (bf16[1024,1024]{1,0:T(8,128)(2,1)}, bf16[1024,1024]{1,0:T(8,128)(2,1)}, f32[2,1024]{1,0:T(2,128)}) custom-call(s32[2]{0:T(128)} %pad_add_fusion.where_ref, bf16[1024,4096]{1,0:T(8,128)(2,1)} %hidden_backward.1.dpre_ref.right_ref, bf16[1024,2048]{1,0:T(8,128)(2,1)} %own_ref.7, ...), custom_call_target="tpu_custom_call" | custom-call | flops 4294967296 | bytes 65536 | tf_op jit(solution)/shard_map/second_norm_backward/pallas_call | solution.py:610
  177.5 13.3 %up_sent.1 = bf16[512,5120]{1,0:T(8,128)(2,1)} custom-call(bf16[1024,1024]{1,0:T(8,128)(2,1)} %get-tuple-element.98.left_ref, bf16[1024,4096]{1,0:T(8,128)(2,1)} %hidden_backward.1.dpre_ref.right_ref, bf16[1024,1024]{1,0:T(8,128)(2,1)} %get-tuple-element.95.out_left_ref, bf16[1024,512]{1,0:T(8,128)(2,1)} %get-tuple-element.77.ho_ref.own_ref, ...), custom_call_target="tpu_custom_call" | custom-call | flops 4294967296 | bytes 65536 | tf_op jit(solution)/shard_map/up_sent/pallas_call | solution.py:785
  190.8 15.9 %hidden_out.1 = bf16[1024,1024]{1,0:T(8,128)(2,1)} custom-call(bf16[1024,4096]{1,0:T(8,128)(2,1)} %get-tuple-element.85.right_ref.hid_ref, bf16[2048,1024]{1,0:T(8,128)(2,1)} %own_ref.8, bf16[2048,1024]{1,0:T(8,128)(2,1)} %all-gather.5.cloned.1.call-done.other_ref, f32[1024,1024]{1,0:T(8,128)} %get-tuple-element.96.x1_ref), custom_call_target="tpu_custom_call" | custom-call | flops 4294967296 | bytes 65536 | tf_op jit(solution)/shard_map/hidden_out/pallas_call | solution.py:558
  206.8 1.5 collective-permute-start.8
  208.3 14.4 %up_kept.1 = (bf16[256,5120]{1,0:T(8,128)(2,1)}, bf16[256,5120]{1,0:T(8,128)(2,1)}) custom-call(bf16[1024,1024]{1,0:T(8,128)(2,1)} %get-tuple-element.98.left_ref, bf16[1024,4096]{1,0:T(8,128)(2,1)} %hidden_backward.1.dpre_ref.right_ref, bf16[1024,1024]{1,0:T(8,128)(2,1)} %get-tuple-element.95.out_left_ref, ...), custom_call_target="tpu_custom_call" | custom-call | flops 4294967296 | bytes 65536 | tf_op jit(solution)/shard_map/up_kept/pallas_call | solution.py:785
  222.7 1.5 collective-permute-start.10
  224.2 2.3 convolution_convert_fusion.1.dout_ref
  226.5 2.3 convolution_convert_fusion.dout_ref
  228.8 11.3 %attend_backward.2 = (bf16[3,1024,512]{2,1,0:T(8,128)(2,1)}, bf16[2,128,512]{2,1,0:T(8,128)(2,1)}) custom-call(bf16[3,1024,512]{2,1,0:T(8,128)(2,1)} %convert_bitcast_fusion.q_ref.k_ref.v_ref, bf16[3,1024,512]{2,1,0:T(8,128)(2,1)} %convert_bitcast_fusion.q_ref.k_ref.v_ref, bf16[3,1024,512]{2,1,0:T(8,128)(2,1)} %convert_bitcast_fusion.q_ref.k_ref.v_ref, ...), custom_call_target="tpu_custom_call" | custom-call | flops 4294967296 | bytes 65536 | tf_op jit(solution)/shard_map/attend_backward/pallas_call | solution.py:273
  240.0 10.9 %attend_backward.3 = (bf16[3,1024,512]{2,1,0:T(8,128)(2,1)}, bf16[2,128,512]{2,1,0:T(8,128)(2,1)}) custom-call(bf16[3,1024,512]{2,1,0:T(8,128)(2,1)} %convert_bitcast_fusion.1.q_ref.k_ref.v_ref, bf16[3,1024,512]{2,1,0:T(8,128)(2,1)} %convert_bitcast_fusion.1.q_ref.k_ref.v_ref, bf16[3,1024,512]{2,1,0:T(8,128)(2,1)} %convert_bitcast_fusion.1.q_ref.k_ref.v_ref, ...), custom_call_target="tpu_custom_call" | custom-call | flops 4294967296 | bytes 65536 | tf_op jit(solution)/shard_map/attend_backward/pallas_call | solution.py:273
  250.9 4.2 collective-permute-done.8
  255.2 1.0 slice.96
  256.2 9.3 %group_sent.1 = bf16[512,3072]{1,0:T(8,128)(2,1)} custom-call(bf16[1024,1024]{1,0:T(8,128)(2,1)} %get-tuple-element.119.refs_0_, bf16[3,1024,512]{2,1,0:T(8,128)(2,1)} %get-tuple-element.107.refs_1_.do_ref, bf16[3,1024,512]{2,1,0:T(8,128)(2,1)} %get-tuple-element.104.refs_2_.dt_ref, bf16[1024,128]{1,0:T(8,128)(2,1)} %context_rows.1.refs_3_, ...), custom_call_target="tpu_custom_call" | custom-call | flops 4294967296 | bytes 65536 | tf_op jit(solution)/shard_map/group_sent/pallas_call | solution.py:858
  266.4 1.6 fusion.17.grad_ref
  268.0 5.9 %ssm_backward.1 = (f32[512,1024]{1,0:T(8,128)}, f32[17,1024]{1,0:T(8,128)}) custom-call(bf16[1024,1024]{1,0:T(8,128)(2,1)} %get-tuple-element.79.v_ref, f32[128,1024]{1,0:T(8,128)} %fusion.17.grad_ref, f32[16,1]{1,0:T(8,128)} %constant.28.clone.rates_ref, f32[16,1]{1,0:T(8,128)} %constant.29.clone.norms_ref, f32[16,1024]{1,0:T(8,128)} %maximum_select_fusion.2.coef_ref, ...), custom_call_target="tpu_custom_call" | custom-call | flops 4294967296 | bytes 65536 | tf_op jit(solution)/shard_map/ssm_backward/pallas_call | solution.py:152
  273.9 13.7 %collective-permute-done.10 = bf16[256,5120]{1,0:T(8,128)(2,1)} collective-permute-done((bf16[256,5120]{1,0:T(8,128)(2,1)}, bf16[256,5120]{1,0:T(8,128)(2,1)}, u32[]{:S(2)}, u32[]{:S(2)}) %collective-permute-start.10) | collective-permute-done | bytes 2621472 | tf_op jit(solution)/shard_map/ppermute | solution.py:27
  287.6 4.3 %add_convert_fusion = bf16[256,5120]{1,0:T(8,128)(2,1)} fusion(bf16[256,5120]{1,0:T(8,128)(2,1)} %collective-permute-done.10, bf16[256,5120]{1,0:T(8,128)(2,1)S(1)} %copy-done.4), kind=kLoop, calls=%fused_computation | loop fusion | flops 5242880 | bytes 7864320 | tf_op jit(solution)/shard_map/convert_element_type | solution.py:979
  292.0 10.1 %group_kept.1 = (bf16[256,3072]{1,0:T(8,128)(2,1)}, bf16[256,3072]{1,0:T(8,128)(2,1)}) custom-call(bf16[1024,1024]{1,0:T(8,128)(2,1)} %get-tuple-element.119.refs_0_, bf16[3,1024,512]{2,1,0:T(8,128)(2,1)} %get-tuple-element.107.refs_1_.do_ref, bf16[3,1024,512]{2,1,0:T(8,128)(2,1)} %get-tuple-element.104.refs_2_.dt_ref, ...), custom_call_target="tpu_custom_call" | custom-call | flops 4294967296 | bytes 65536 | tf_op jit(solution)/shard_map/group_kept/pallas_call | solution.py:858
  302.1 1.3 collective-permute-start.14
  303.4 18.5 %first_norm_backward.1 = (bf16[1024,1024]{1,0:T(8,128)(2,1)}, f32[2,1024]{1,0:T(2,128)}) custom-call(s32[2]{0:T(128)} %pad_add_fusion.where_ref, bf16[3,1024,512]{2,1,0:T(8,128)(2,1)} %get-tuple-element.107.refs_1_.do_ref, bf16[3,1024,512]{2,1,0:T(8,128)(2,1)} %get-tuple-element.104.refs_2_.dt_ref, bf16[3,1024,512]{2,1,0:T(8,128)(2,1)} %own_ref.9, ...), custom_call_target="tpu_custom_call" | custom-call | flops 4294967296 | bytes 65536 | tf_op jit(solution)/shard_map/first_norm_backward/pallas_call | solution.py:676
  322.8 1.2 collective-permute-start.13
  324.0 14.3 %collective-permute-done.14 = bf16[256,3072]{1,0:T(8,128)(2,1)S(1)} collective-permute-done((bf16[256,3072]{1,0:T(8,128)(2,1)}, bf16[256,3072]{1,0:T(8,128)(2,1)S(1)}, u32[]{:S(2)}, u32[]{:S(2)}) %collective-permute-start.14) | collective-permute-done | bytes 1572896 | tf_op jit(solution)/shard_map/ppermute | solution.py:27
  338.2 1.7 add_convert_fusion.1
  341.4 1.8 collective-permute-start.16
  343.2 0.9 collective-permute-start.21
  344.1 2.2 collective-permute-done.16
  346.3 1.5 collective-permute-start.17
  347.8 4.5 %maximum_select_fusion = bf16[2,1,1024,1024]{3,2,1,0:T(8,128)(2,1)} fusion(bf16[1,1,1024,1024]{3,2,1,0:T(8,128)(2,1)} %bitcast.16, bf16[1,1,1024,1024]{3,2,1,0:T(8,128)(2,1)S(1)} %bitcast.56, pred[]{:T(512)S(6)} %eq.4), kind=kLoop, calls=%fused_computation.1 | loop fusion | flops 6291456 | bytes 8388609 | tf_op jit(solution)/shard_map/jit(_where)/select_n | solution.py:1022
  352.4 2.7 collective-permute-start.18
  355.1 38.9 %collective-permute-done.21 = bf16[64,2048]{1,0:T(8,128)(2,1)S(1)} collective-permute-done((bf16[64,2048]{1,0:T(8,128)(2,1)S(1)}, bf16[64,2048]{1,0:T(8,128)(2,1)S(1)}, u32[]{:S(2)}, u32[]{:S(2)}) %collective-permute-start.21) | collective-permute-done | bytes 262176 | tf_op jit(solution)/shard_map/ppermute | solution.py:27
  396.6 1.1 slice_convert_fusion
  398.3 6.1 %fusion = f32[2,1,1024,1024]{3,2,1,0:T(8,128)} fusion(bf16[1,1,1024,1024]{3,2,1,0:T(8,128)(2,1)} %bitcast.20, bf16[1,1,1024,1024]{3,2,1,0:T(8,128)(2,1)S(1)} %bitcast.57, pred[]{:T(512)S(6)} %eq.4), kind=kLoop, calls=%fused_computation.3 | loop fusion | flops 8388608 | bytes 12582913 | tf_op jit(solution)/shard_map/convert_element_type | solution.py:1026
  404.4 2.7 collective-permute-done.20
  408.1 0.9 slice.127
  410.2 4.5 %collective-permute-done.19 = bf16[64,1536]{1,0:T(8,128)(2,1)S(1)} collective-permute-done((bf16[64,1536]{1,0:T(8,128)(2,1)S(1)}, bf16[64,1536]{1,0:T(8,128)(2,1)S(1)}, u32[]{:S(2)}, u32[]{:S(2)}) %collective-permute-start.19) | collective-permute-done | bytes 196640 | tf_op jit(solution)/shard_map/ppermute | solution.py:27
  414.8 1.0 select_add_fusion
  (112 shorter events, 15.0 us)
Async XLA Ops:
  7.2 91.0 %all-gather.3.cloned.1.call-start = ((), (), s32[]{:S(2)}) async-start(), calls=%async_computation.3 | async-start | bytes 4456448 | tf_op jit(solution)/shard_map/all_gather | solution.py:930
  8.2 9.3 %collective-permute-start = (bf16[64,2048]{1,0:T(8,128)(2,1)S(1)}, bf16[64,2048]{1,0:T(8,128)(2,1)S(1)}, u32[]{:S(2)}, u32[]{:S(2)}) collective-permute-start(bf16[64,2048]{1,0:T(8,128)(2,1)S(1)} %constant_dynamic-slice_fusion.4), channel_id=1, source_target_pairs={{0,1},{1,0},{2,3},{3,2},{4,5},{5,4},{6,7},{7,6},{8,9},{9,8},{10,11... | collective-permute-start | bytes 786440 | tf_op jit(solution)/shard_map/ppermute | solution.py:27
  17.5 0.7 copy-start.11
  18.2 111.5 %all-gather.5.cloned.1.call-start = ((), (), s32[]{:S(2)}) async-start(), calls=%async_computation.4 | async-start | bytes 4456448 | tf_op jit(solution)/shard_map/all_gather | solution.py:932
  19.3 23.0 %collective-permute-start.1 = (bf16[128,1024]{1,0:T(8,128)(2,1)S(1)}, bf16[128,1024]{1,0:T(8,128)(2,1)}, u32[]{:S(2)}, u32[]{:S(2)}) collective-permute-start(bf16[128,1024]{1,0:T(8,128)(2,1)S(1)} %constant_dynamic-slice_fusion.3), channel_id=1, source_target_pairs={{0,1},{1,0},{2,3},{3,2},{4,5},{5,4},{6,7},{7,6},{8,9},{9,8},{10,11... | collective-permute-start | bytes 786440 | tf_op jit(solution)/shard_map/ppermute | solution.py:27
  21.9 12.7 %collective-permute-start.2 = (f32[17,512]{1,0:T(8,128)S(1)}, f32[17,512]{1,0:T(8,128)S(1)}, u32[]{:S(2)}, u32[]{:S(2)}) collective-permute-start(f32[17,512]{1,0:T(8,128)S(1)} %pad_maximum_fusion.1), channel_id=1, source_target_pairs={{0,1},{1,0},{2,3},{3,2},{4,5},{5,4},{6,7},{7,6},{8,9},{9,8},{10,11... | collective-permute-start | bytes 104456 | tf_op jit(solution)/shard_map/ppermute | solution.py:27
  24.8 36.9 %collective-permute-start.3 = (bf16[3,1024,256]{2,1,0:T(8,128)(2,1)}, bf16[3,1024,256]{2,1,0:T(8,128)(2,1)}, u32[]{:S(2)}, u32[]{:S(2)}) collective-permute-start(bf16[3,1024,256]{2,1,0:T(8,128)(2,1)} %constant_dynamic-slice_fusion.2), channel_id=1, source_target_pairs={{0,1},{1,0},{2,3},{3,2},{4,5},{5,4},{6,7},{7,6},{8,9},{9,8},{10,11... | collective-permute-start | bytes 4718600 | tf_op jit(solution)/shard_map/ppermute | solution.py:27
  27.1 7.5 %copy-start.18 = (f32[512]{0:T(512)S(1)}, f32[512]{0:T(512)}, u32[]{:S(2)}) copy-start(f32[512]{0:T(512)} %param.22) | copy-start | bytes 6148
  27.1 8.1 %copy-start.15 = (f32[16,512]{1,0:T(8,128)S(1)}, f32[16,512]{1,0:T(8,128)}, u32[]{:S(2)}) copy-start(f32[16,512]{1,0:T(8,128)} %param.21) | copy-start | bytes 98308
  27.1 8.7 %copy-start.2 = (bf16[3,1024,512]{2,1,0:T(8,128)(2,1)S(1)}, bf16[3,1024,512]{2,1,0:T(8,128)(2,1)}, u32[]{:S(2)}) copy-start(bf16[3,1024,512]{2,1,0:T(8,128)(2,1)} %own_ref.9) | copy-start | bytes 9437188
  47.4 1.9 copy-start.20
  50.5 11.5 %copy-start.12 = (bf16[512,1024]{1,0:T(8,128)(2,1)S(1)}, bf16[512,1024]{1,0:T(8,128)(2,1)}, u32[]{:S(2)}) copy-start(bf16[512,1024]{1,0:T(8,128)(2,1)} %wo_ref.1) | copy-start | bytes 3145732
  61.7 3.8 collective-permute-start.4
  61.7 193.5 %reduce-scatter.4.cloned.1.call-start = ((), (), s32[]{:S(2)}) async-start(), calls=%async_computation.5 | async-start | bytes 4718592 | tf_op jit(solution)/shard_map/reduce_scatter | solution.py:905
  62.0 5.0 %copy-start.21 = (bf16[1024,1024]{1,0:T(8,128)(2,1)S(1)}, bf16[1024,1024]{1,0:T(8,128)(2,1)}, u32[]{:S(2)}) copy-start(bf16[1024,1024]{1,0:T(8,128)(2,1)} %get-tuple-element.79.v_ref) | copy-start | bytes 6291460
  62.0 14.5 %collective-permute-start.5 = (bf16[256,1024]{1,0:T(8,128)(2,1)S(1)}, bf16[256,1024]{1,0:T(8,128)(2,1)}, u32[]{:S(2)}, u32[]{:S(2)}) collective-permute-start(bf16[256,1024]{1,0:T(8,128)(2,1)S(1)} %constant_dynamic-slice_fusion.1), channel_id=1, source_target_pairs={{0,1},{1,0},{2,3},{3,2},{4,5},{5,4},{6,7},{7,6},{8,9},{9,8},{10,11... | collective-permute-start | bytes 1572872 | tf_op jit(solution)/shard_map/ppermute | solution.py:27
  67.0 199.3 %copy-start = (bf16[3,1024,512]{2,1,0:T(8,128)(2,1)}, bf16[3,1024,512]{2,1,0:T(8,128)(2,1)S(1)}, u32[]{:S(2)}) copy-start(bf16[3,1024,512]{2,1,0:T(8,128)(2,1)S(1)} %constant_dynamic-update-slice_fusion.other_ref) | copy-start | bytes 9437188
  76.5 10.9 %collective-permute-start.6 = (bf16[256,1024]{1,0:T(8,128)(2,1)}, bf16[256,1024]{1,0:T(8,128)(2,1)}, u32[]{:S(2)}, u32[]{:S(2)}) collective-permute-start(bf16[256,1024]{1,0:T(8,128)(2,1)} %collective-permute-done.5), channel_id=1, source_target_pairs={{0,2},{2,0},{4,6},{6,4},{8,10},{10,8},{12,14},{14,12},{16,18},{18,... | collective-permute-start | bytes 1572872 | tf_op jit(solution)/shard_map/ppermute | solution.py:27
  129.3 16.2 %collective-permute-start.7 = (bf16[512,4096]{1,0:T(8,128)(2,1)}, bf16[512,4096]{1,0:T(8,128)(2,1)}, u32[]{:S(2)}, u32[]{:S(2)}) collective-permute-start(bf16[512,4096]{1,0:T(8,128)(2,1)} %down_sent.1), channel_id=1, source_target_pairs={{0,2},{2,0},{4,6},{6,4},{8,10},{10,8},{12,14},{14,12},{16,18},{18,... | collective-permute-start | bytes 12582920 | tf_op jit(solution)/shard_map/ppermute | solution.py:27
  155.6 241.1 %reduce-scatter.8.cloned.1.call-start = ((), (), s32[]{:S(2)}) async-start(), calls=%async_computation.7 | async-start | bytes 3276800 | tf_op jit(solution)/shard_map/reduce_scatter | solution.py:905
  190.8 17.5 %collective-permute-start.9 = (bf16[512,5120]{1,0:T(8,128)(2,1)}, bf16[512,5120]{1,0:T(8,128)(2,1)}, u32[]{:S(2)}, u32[]{:S(2)}) collective-permute-start(bf16[512,5120]{1,0:T(8,128)(2,1)} %up_sent.1), channel_id=1, source_target_pairs={{0,2},{2,0},{4,6},{6,4},{8,10},{10,8},{12,14},{14,12},{16,18},{18,... | collective-permute-start | bytes 15728648 | tf_op jit(solution)/shard_map/ppermute | solution.py:27
  206.7 17.4 %copy-start.6 = (bf16[1024,1024]{1,0:T(8,128)(2,1)S(1)}, bf16[1024,1024]{1,0:T(8,128)(2,1)}, u32[]{:S(2)}) copy-start(bf16[1024,1024]{1,0:T(8,128)(2,1)} %get-tuple-element.101.dx_ref) | copy-start | bytes 6291460
  206.8 17.4 %copy-start.13 = (bf16[512,1024]{1,0:T(8,128)(2,1)S(1)}, bf16[512,1024]{1,0:T(8,128)(2,1)}, u32[]{:S(2)}) copy-start(bf16[512,1024]{1,0:T(8,128)(2,1)} %wo_ref.1) | copy-start | bytes 3145732
  206.8 48.4 %collective-permute-start.8 = (bf16[1024,1024]{1,0:T(8,128)(2,1)}, bf16[1024,1024]{1,0:T(8,128)(2,1)}, u32[]{:S(2)}, u32[]{:S(2)}) collective-permute-start(bf16[1024,1024]{1,0:T(8,128)(2,1)} %hidden_out.1), channel_id=1, source_target_pairs={{0,1},{1,0},{2,3},{3,2},{4,5},{5,4},{6,7},{7,6},{8,9},{9,8},{10,11... | collective-permute-start | bytes 6291464 | tf_op jit(solution)/shard_map/ppermute | solution.py:27
  222.7 3.8 copy-start.10
  222.7 64.9 %collective-permute-start.10 = (bf16[256,5120]{1,0:T(8,128)(2,1)}, bf16[256,5120]{1,0:T(8,128)(2,1)}, u32[]{:S(2)}, u32[]{:S(2)}) collective-permute-start(bf16[256,5120]{1,0:T(8,128)(2,1)} %get-tuple-element.117), channel_id=1, source_target_pairs={{0,4},{2,6},{4,0},{6,2},{8,12},{10,14},{12,8},{14,10},{16,20},{18,... | collective-permute-start | bytes 7864328 | tf_op jit(solution)/shard_map/ppermute | solution.py:27
  256.1 9.4 %copy-start.3 = (bf16[3,1024,512]{2,1,0:T(8,128)(2,1)S(1)}, bf16[3,1024,512]{2,1,0:T(8,128)(2,1)}, u32[]{:S(2)}) copy-start(bf16[3,1024,512]{2,1,0:T(8,128)(2,1)} %own_ref.9) | copy-start | bytes 9437188
  256.2 9.3 %copy-start.19 = (bf16[2,128,512]{2,1,0:T(8,128)(2,1)S(1)}, bf16[2,128,512]{2,1,0:T(8,128)(2,1)}, u32[]{:S(2)}) copy-start(bf16[2,128,512]{2,1,0:T(8,128)(2,1)} %get-tuple-element.114.refs_4_) | copy-start | bytes 786436
  265.5 0.9 copy-start.14
  265.5 26.5 %collective-permute-start.11 = (bf16[512,3072]{1,0:T(8,128)(2,1)}, bf16[512,3072]{1,0:T(8,128)(2,1)}, u32[]{:S(2)}, u32[]{:S(2)}) collective-permute-start(bf16[512,3072]{1,0:T(8,128)(2,1)} %group_sent.1), channel_id=1, source_target_pairs={{0,2},{2,0},{4,6},{6,4},{8,10},{10,8},{12,14},{14,12},{16,18},{18,... | collective-permute-start | bytes 9437192 | tf_op jit(solution)/shard_map/ppermute | solution.py:27
  268.0 19.5 %copy-start.4 = (bf16[256,5120]{1,0:T(8,128)(2,1)S(1)}, bf16[256,5120]{1,0:T(8,128)(2,1)}, u32[]{:S(2)}) copy-start(bf16[256,5120]{1,0:T(8,128)(2,1)} %get-tuple-element.100) | copy-start | bytes 7864324
  291.9 116.2 %reduce-scatter.6.cloned.1.call-start = ((), (), s32[]{:S(2)}) async-start(), calls=%async_computation.6 | async-start | bytes 1966080 | tf_op jit(solution)/shard_map/reduce_scatter | solution.py:905
  302.1 36.1 %collective-permute-start.14 = (bf16[256,3072]{1,0:T(8,128)(2,1)}, bf16[256,3072]{1,0:T(8,128)(2,1)S(1)}, u32[]{:S(2)}, u32[]{:S(2)}) collective-permute-start(bf16[256,3072]{1,0:T(8,128)(2,1)} %get-tuple-element.127), channel_id=1, source_target_pairs={{0,4},{2,6},{4,0},{6,2},{8,12},{10,14},{12,8},{14,10},{16,20},{18,... | collective-permute-start | bytes 4718600 | tf_op jit(solution)/shard_map/ppermute | solution.py:27
  303.4 18.6 %copy-start.9 = (f32[17,1024]{1,0:T(8,128)S(1)}, f32[17,1024]{1,0:T(8,128)}, u32[]{:S(2)}) copy-start(f32[17,1024]{1,0:T(8,128)} %get-tuple-element.124) | copy-start | bytes 208900
  303.4 18.6 %copy-start.16 = (f32[2,1024]{1,0:T(2,128)S(1)}, f32[2,1024]{1,0:T(2,128)}, u32[]{:S(2)}) copy-start(f32[2,1024]{1,0:T(2,128)} %get-tuple-element.125) | copy-start | bytes 24580
  303.4 34.8 %copy-start.7 = (bf16[256,3072]{1,0:T(8,128)(2,1)S(1)}, bf16[256,3072]{1,0:T(8,128)(2,1)}, u32[]{:S(2)}) copy-start(bf16[256,3072]{1,0:T(8,128)(2,1)} %get-tuple-element.121) | copy-start | bytes 4718596
  322.0 18.0 %copy-start.17 = (f32[2,1024]{1,0:T(2,128)S(1)}, f32[2,1024]{1,0:T(2,128)}, u32[]{:S(2)}) copy-start(f32[2,1024]{1,0:T(2,128)} %get-tuple-element.126) | copy-start | bytes 24580
  322.8 17.2 %collective-permute-start.13 = (f32[21,1024]{1,0:T(8,128)S(1)}, f32[21,1024]{1,0:T(8,128)S(1)}, u32[]{:S(2)}, u32[]{:S(2)}) collective-permute-start(f32[21,1024]{1,0:T(8,128)S(1)} %pad_maximum_fusion), channel_id=1, source_target_pairs={{0,1},{1,0},{2,3},{3,2},{4,5},{5,4},{6,7},{7,6},{8,9},{9,8},{10,11... | collective-permute-start | bytes 258056 | tf_op jit(solution)/shard_map/ppermute | solution.py:27
  338.2 9.6 %copy-start.1 = (bf16[1024,1024]{1,0:T(8,128)(2,1)S(1)}, bf16[1024,1024]{1,0:T(8,128)(2,1)}, u32[]{:S(2)}) copy-start(bf16[1024,1024]{1,0:T(8,128)(2,1)} %hidden_out.1) | copy-start | bytes 6291460
  340.0 1.4 collective-permute-start.15
  340.1 58.3 %collective-permute-start.12 = (bf16[1024,1024]{1,0:T(8,128)(2,1)}, bf16[1024,1024]{1,0:T(8,128)(2,1)}, u32[]{:S(2)}, u32[]{:S(2)}) collective-permute-start(bf16[1024,1024]{1,0:T(8,128)(2,1)} %get-tuple-element.123), channel_id=1, source_target_pairs={{0,1},{1,0},{2,3},{3,2},{4,5},{5,4},{6,7},{7,6},{8,9},{9,8},{10,11... | collective-permute-start | bytes 6291464 | tf_op jit(solution)/shard_map/ppermute | solution.py:27
  341.4 4.9 %collective-permute-start.16 = (f32[21,1024]{1,0:T(8,128)S(1)}, f32[21,1024]{1,0:T(8,128)S(1)}, u32[]{:S(2)}, u32[]{:S(2)}) collective-permute-start(f32[21,1024]{1,0:T(8,128)S(1)} %add.62), channel_id=1, source_target_pairs={{0,4},{2,6},{4,0},{6,2},{8,12},{10,14},{12,8},{14,10},{16,20},{18,... | collective-permute-start | bytes 258056 | tf_op jit(solution)/shard_map/ppermute | solution.py:27
  343.2 50.7 %collective-permute-start.21 = (bf16[64,2048]{1,0:T(8,128)(2,1)S(1)}, bf16[64,2048]{1,0:T(8,128)(2,1)S(1)}, u32[]{:S(2)}, u32[]{:S(2)}) collective-permute-start(bf16[64,2048]{1,0:T(8,128)(2,1)S(1)} %slice.96), channel_id=1, source_target_pairs={{0,1},{1,0},{2,3},{3,2},{4,5},{5,4},{6,7},{7,6},{8,9},{9,8},{10,11... | collective-permute-start | bytes 786440 | tf_op jit(solution)/shard_map/ppermute | solution.py:27
  346.3 6.1 %collective-permute-start.17 = (f32[21,1024]{1,0:T(8,128)S(1)}, f32[21,1024]{1,0:T(8,128)S(1)}, u32[]{:S(2)}, u32[]{:S(2)}) collective-permute-start(f32[21,1024]{1,0:T(8,128)S(1)} %add.63), channel_id=1, source_target_pairs={{0,8},{2,10},{4,12},{6,14},{8,0},{10,2},{12,4},{14,6},{16,24},{18,... | collective-permute-start | bytes 258056 | tf_op jit(solution)/shard_map/ppermute | solution.py:27
  347.8 46.1 %copy-start.8 = (bf16[64,4096]{1,0:T(8,128)(2,1)S(1)}, bf16[64,4096]{1,0:T(8,128)(2,1)}, u32[]{:S(2)}) copy-start(bf16[64,4096]{1,0:T(8,128)(2,1)} %reduce-scatter.4.cloned.1.call-done) | copy-start | bytes 1572868
  352.4 46.0 %copy-start.5 = (bf16[1024,1024]{1,0:T(8,128)(2,1)S(1)}, bf16[1024,1024]{1,0:T(8,128)(2,1)}, u32[]{:S(2)}) copy-start(bf16[1024,1024]{1,0:T(8,128)(2,1)} %get-tuple-element.123) | copy-start | bytes 6291460
  352.4 42.4 %collective-permute-start.18 = (f32[21,1024]{1,0:T(8,128)S(1)}, f32[21,1024]{1,0:T(8,128)S(1)}, u32[]{:S(2)}, u32[]{:S(2)}) collective-permute-start(f32[21,1024]{1,0:T(8,128)S(1)} %add.64), channel_id=1, source_target_pairs={{0,16},{2,18},{4,20},{6,22},{8,24},{10,26},{12,28},{14,30},{16,0},... | collective-permute-start | bytes 258056 | tf_op jit(solution)/shard_map/ppermute | solution.py:27
  397.8 9.3 %collective-permute-start.20 = (bf16[64,2560]{1,0:T(8,128)(2,1)S(1)}, bf16[64,2560]{1,0:T(8,128)(2,1)S(1)}, u32[]{:S(2)}, u32[]{:S(2)}) collective-permute-start(bf16[64,2560]{1,0:T(8,128)(2,1)S(1)} %get-tuple-element.143), channel_id=1, source_target_pairs={{0,1},{1,0},{2,3},{3,2},{4,5},{5,4},{6,7},{7,6},{8,9},{9,8},{10,11... | collective-permute-start | bytes 983048 | tf_op jit(solution)/shard_map/ppermute | solution.py:27
  409.0 5.7 %collective-permute-start.19 = (bf16[64,1536]{1,0:T(8,128)(2,1)S(1)}, bf16[64,1536]{1,0:T(8,128)(2,1)S(1)}, u32[]{:S(2)}, u32[]{:S(2)}) collective-permute-start(bf16[64,1536]{1,0:T(8,128)(2,1)S(1)} %slice.127), channel_id=1, source_target_pairs={{0,1},{1,0},{2,3},{3,2},{4,5},{5,4},{6,7},{7,6},{8,9},{9,8},{10,11... | collective-permute-start | bytes 589832 | tf_op jit(solution)/shard_map/ppermute | solution.py:27
Sparse Core Ops, SparseCore 0:
  18.4 52.0 all-gather.2
  72.6 49.0 all-gather.4
  155.7 93.7 reduce-scatter.3
  292.0 52.5 reduce-scatter.7
  346.8 36.3 reduce-scatter.5
